TPU v7x, 32 devices: a whole 2x2x4 slice. The times are simulated.
32 devices in a mesh: scene: 4 (over y, core), frame: 8 (over z, x).
Axes of the slice: x: 2, y: 2, z: 4, core: 2. Of those that a mesh axis runs over, the one named last changes fastest.
Arguments:
- occupancy: bfloat16 [4, 32, 64, 2048], P('scene', 'frame'), may hold values from -6 to 6
- scene_lengths: int32 [4], P('scene'), may hold values from 8 to 32, as said below
- conv1_weight: bfloat16 [128, 1728], replicated, may hold values from -0.15625 to 0.15625
- conv2_weight: bfloat16 [256, 3456], replicated, may hold values from -0.109375 to 0.109375
- temporal_weight: bfloat16 [3, 256, 256], replicated, may hold values from -0.21875 to 0.21875
- query_weight: bfloat16 [256, 256], replicated
- key_weight: bfloat16 [256, 256], replicated
- value_weight: bfloat16 [256, 256], replicated, may hold values from -0.375 to 0.375
- out_weight: bfloat16 [256, 256], replicated, may hold values from -0.375 to 0.375
Outputs:
- encoded: bfloat16 [4, 32, 256, 512], P('scene', 'frame')
- kl_loss: float32 [], replicated
Inputs may be any that keep to these rules, and one draw needn't show every extreme that they name: `scene_lengths`: non-decreasing along the scenes; the first scene has exactly 8 frames with data and the last exactly 32.
All inputs are finite; a program needn't handle non-finite values.
Results may differ from a plain program's by a relative error of at most 0.011.
Values may be sent and summed in bfloat16 or wider, within the bound.
No kernel may reach another device: no remote copies, remote signals or barrier semaphores. Data moves between devices by JAX's collectives and lax.ppermute only.
A program may use at most 192 MiB of HBM per device.

v0:
```python
import functools

import jax
import jax.numpy as jnp
from jax import lax
from jax.experimental import pallas as pl
from jax.experimental.pallas import tpu as pltpu
from jax.sharding import PartitionSpec as P


CIN = 64
C1 = 128
C2 = 256
HEADS = 4
HD = 64
HI = 16
ZD = 8
CELLS = 512
ROWS = 8
ROW = 64
HALVES = 2
NORM_EPS = 1e-06
NEG = -1e30
TAIL = 16
VMEM_LIMIT = 24 << 20


def silu(v):
    half = 0.5 * v
    return half + half * jnp.tanh(half)


def shift_z(v, step):
    if step == 0:
        return v
    z = lax.broadcasted_iota(jnp.int32, v.shape, v.ndim - 2)
    moved = pltpu.roll(v, (-step) % ZD, v.ndim - 2)
    keep = (z + step >= 0) & (z + step < ZD)
    return jnp.where(keep, moved, 0.0)


def shift_w(v, step):
    if step == 0:
        return v
    zero = jnp.zeros_like(v[:1])
    if step < 0:
        return jnp.concatenate([zero, v[:-1]], axis=0)
    return jnp.concatenate([v[1:], zero], axis=0)


def store_cols(cols, f, h, v):
    for kz in range(3):
        moved = shift_z(v, kz - 1)
        for kw in range(3):
            lanes = slice((kw * 3 + kz) * C1, (kw * 3 + kz + 1) * C1)
            cols[f, (h + 1) * ROW : (h + 2) * ROW, lanes] = (
                shift_w(moved, kw - 1).reshape(ROW, C1).astype(jnp.bfloat16)
            )


def second_conv(n, far, meta, cols2, w2s, y2, outs):
    frames = cols2.shape[0]
    me = lax.axis_index("frame")
    half = CELLS // 2
    count = CELLS // n
    side = me // (n // 2)
    first = (1 - side if far else side) * half
    acc = jnp.zeros((frames * half, C2), jnp.float32)
    for kh in range(3):
        start = pl.multiple_of(first + kh * ROW, ROW)
        lhs = cols2[:, pl.ds(start, half), :].reshape(frames * half, 9 * C1)
        acc = acc + jnp.dot(lhs, w2s[kh], preferred_element_type=jnp.float32)
    y2[...] = acc
    for f in range(frames):
        valid = jnp.where(me * frames + f < meta[0], 1.0, 0.0)
        for r in range(0, half, ROW):
            rows = slice(f * half + r, f * half + r + ROW)
            y2[rows, :] = silu(y2[rows, :]) * valid
        for k in range(n // 2):
            at = (me ^ (k + n // 2 if far else k)) % (n // 2)
            start = pl.multiple_of(f * half + at * count, count)
            outs[k][f] = y2[pl.ds(start, count), :].astype(jnp.bfloat16)


def conv_kernel(n, meta, occ_hbm, w1_hbm, w2_hbm, *rest):
    outs = rest[: n // 2]
    cols2, w2s = rest[n // 2 : n // 2 + 2]
    occ, w1, w2, t1, t2, w1s, cols1, y1, y2, sems = rest[n // 2 + 2 :]
    frames = occ.shape[0]
    bf16 = jnp.bfloat16

    copies = [pltpu.make_async_copy(w1_hbm, w1, sems.at[0])]
    for f in range(frames):
        copies.append(pltpu.make_async_copy(occ_hbm.at[0, f], occ.at[f], sems.at[1 + f]))
    for half in range(2):
        rows = slice(half * 128, half * 128 + 128)
        copies.append(
            pltpu.make_async_copy(w2_hbm.at[rows, :], w2.at[rows, :], sems.at[1 + frames + half])
        )
    for copy in copies:
        copy.start()
    cols1[:, 0:ROW, :] = jnp.zeros((frames, ROW, cols1.shape[2]), bf16)
    edge = jnp.zeros((frames, ROW, cols2.shape[2]), bf16)
    cols2[:, 0:ROW, :] = edge
    cols2[:, (ROWS + 1) * ROW :, :] = edge
    zero = jnp.zeros((CIN, C1), bf16)

    copies[0].wait()
    t1[...] = w1[...].astype(jnp.float32)
    for kz in range(3):

        def tap1(kh, kw):
            return t1[pl.ds(kh * 9 + kw * 3 + kz, CIN, stride=27), :].astype(bf16)

        for place, (kw, hp) in enumerate([(1, 0), (1, 1), (2, 0), (2, 1), (0, 0), (0, 1)]):
            rows = slice(kz * 384 + place * CIN, kz * 384 + place * CIN + CIN)
            w1s[rows, 0:C1] = tap1(hp + 1, kw)
            w1s[rows, C1 : 2 * C1] = tap1(0, kw) if hp == 1 else zero

    for f in range(frames):
        copies[1 + f].wait()
        for h in range(ROWS):
            upper = occ[f, :, h * 256 : h * 256 + 128]
            lower = occ[f, :, h * 256 + 128 : h * 256 + 256]
            tile = jnp.concatenate([upper, lower], axis=0).astype(jnp.float32).T
            tile = tile.reshape(8, 2, ZD, 128)
            even, odd = tile[:, 0], tile[:, 1]
            for kz in range(3):
                e, o = shift_z(even, kz - 1), shift_z(odd, kz - 1)
                parts = (e, o, shift_w(o, -1))
                for i, part in enumerate(parts):
                    lanes = slice(kz * 384 + i * 128, kz * 384 + i * 128 + 128)
                    cols1[f, (h + 1) * ROW : (h + 2) * ROW, lanes] = part.reshape(ROW, 128).astype(bf16)
        y1[f] = jnp.dot(cols1[f], w1s[...], preferred_element_type=jnp.float32)
        if f == 0:
            copies[1 + frames].wait()
            copies[2 + frames].wait()
        pieces = w2.shape[1] // 128
        for j in range(f * pieces // frames, (f + 1) * pieces // frames):
            for half in range(2):
                t2[half, j * 128 : j * 128 + 128, :] = (
                    w2[half * 128 : half * 128 + 128, j * 128 : j * 128 + 128].astype(jnp.float32).T
                )
        for h in range(ROWS):
            v = (
                y1[f, (h + 1) * ROW : (h + 2) * ROW, 0:C1]
                + y1[f, h * ROW : (h + 1) * ROW, C1 : 2 * C1]
            )
            store_cols(cols2, f, h, silu(v).reshape(8, ZD, C1))
    for kh in range(3):
        for kw in range(3):
            for kz in range(3):
                rows = slice((kw * 3 + kz) * C1, (kw * 3 + kz + 1) * C1)
                for half in range(2):
                    w2s[kh, rows, half * 128 : half * 128 + 128] = t2[
                        half, pl.ds(kh * 9 + kw * 3 + kz, C1, stride=27), :
                    ].astype(bf16)
    second_conv(n, True, meta, cols2, w2s, y2, outs)


def near_kernel(n, meta, cols2, w2s, *rest):
    second_conv(n, False, meta, cols2, w2s, rest[n // 2], rest[: n // 2])


def conv_far(n, meta, occ, w1, w2):
    frames = occ.shape[1]
    count = CELLS // n
    vmem = pl.BlockSpec(memory_space=pltpu.VMEM)
    hbm = pl.BlockSpec(memory_space=pltpu.HBM)
    f32, bf16 = jnp.float32, jnp.bfloat16
    res = pl.pallas_call(
        functools.partial(conv_kernel, n),
        out_shape=[jax.ShapeDtypeStruct((frames, count, C2), bf16)] * (n // 2)
        + [
            jax.ShapeDtypeStruct((frames, (ROWS + 2) * ROW, 9 * C1), bf16),
            jax.ShapeDtypeStruct((3, 9 * C1, C2), bf16),
        ],
        in_specs=[pl.BlockSpec(memory_space=pltpu.SMEM), hbm, hbm, hbm],
        out_specs=[vmem] * (n // 2 + 2),
        scratch_shapes=[
            pltpu.VMEM((frames, CIN, HI * HI * ZD), bf16),
            pltpu.VMEM((CIN * 27, C1), bf16),
            pltpu.VMEM((C2, C1 * 27), bf16),
            pltpu.VMEM((CIN * 27, C1), f32),
            pltpu.VMEM((2, C1 * 27, 128), f32),
            pltpu.VMEM((1152, 2 * C1), bf16),
            pltpu.VMEM((frames, (ROWS + 1) * ROW, 1152), bf16),
            pltpu.VMEM((frames, (ROWS + 1) * ROW, 2 * C1), f32),
            pltpu.VMEM((frames * CELLS // 2, C2), f32),
            pltpu.SemaphoreType.DMA((3 + frames,)),
        ],
        compiler_params=pltpu.CompilerParams(vmem_limit_bytes=40 << 20),
        cost_estimate=pl.CostEstimate(
            flops=2 * frames * CELLS * (C1 * CIN * 27 + C2 * C1 * 27 // 2),
            bytes_accessed=4_000_000,
            transcendentals=frames * CELLS * (C1 + C2),
        ),
    )(meta, *[pltpu.with_memory_space_constraint(x, pltpu.HBM) for x in (occ, w1, w2)])
    return res[: n // 2], res[n // 2], res[n // 2 + 1]


def conv_near(n, meta, cols2, w2s):
    frames = cols2.shape[0]
    count = CELLS // n
    vmem = pl.BlockSpec(memory_space=pltpu.VMEM)
    return pl.pallas_call(
        functools.partial(near_kernel, n),
        out_shape=[jax.ShapeDtypeStruct((frames, count, C2), jnp.bfloat16)] * (n // 2),
        in_specs=[pl.BlockSpec(memory_space=pltpu.SMEM), vmem, vmem],
        out_specs=[vmem] * (n // 2),
        scratch_shapes=[pltpu.VMEM((frames * CELLS // 2, C2), jnp.float32)],
        compiler_params=pltpu.CompilerParams(vmem_limit_bytes=VMEM_LIMIT),
        cost_estimate=pl.CostEstimate(
            flops=2 * frames * CELLS * C2 * C1 * 27 // 2,
            bytes_accessed=4_000_000,
            transcendentals=frames * CELLS * C2 // 2,
        ),
    )(meta, cols2, w2s)


def nt_dot(a, b):
    return lax.dot_general(a, b, (((1,), (1,)), ((), ())), preferred_element_type=jnp.float32)


def attend_kernel(n, half, meta, *rest):
    blocks = rest[:n]
    tw, wq, wk, wv, wo, before = rest[n : n + 6]
    rest = rest[n + 6 :]
    kept, rest = rest[: n // 2 * half], rest[n // 2 * half :]
    outs, squares = rest[:n], rest[n]
    seen, resid, att, bias, ones, p_s, vb = rest[n + 1 :]
    me, length = lax.axis_index("frame"), meta[0]
    frames, count = blocks[0].shape[0], blocks[0].shape[1] // HALVES
    groups = count // 8
    total = n * frames
    rows = total * 8
    bf16 = jnp.bfloat16
    head_of = lax.broadcasted_iota(jnp.int32, (rows, C2), 1) // HD

    edge = jnp.zeros((groups, 1, 8, C2), jnp.float32)
    seen[:, 0:1] = edge
    seen[:, total + 1 : total + 2] = edge
    for k in range(n):
        first = (me ^ k) * frames + 1
        for f in range(frames):
            tile = blocks[k][f, half * count : (half + 1) * count, :].astype(jnp.float32).reshape(groups, 8, C2)
            for g in range(groups):
                seen[g, first + f] = tile[g]

    at = lax.broadcasted_iota(jnp.int32, (rows, rows), 0)
    to = lax.broadcasted_iota(jnp.int32, (rows, rows), 1)
    bias[...] = jnp.where((at % 8 == to % 8) & (to // 8 < length), 0.0, NEG)
    for h in range(HEADS):
        ones[h * rows : (h + 1) * rows, :] = jnp.where(head_of == h, 1.0, 0.0).astype(bf16)
    squares[...] = before[...]

    def group(g, carry):
        slot = g % 2
        mix = jnp.concatenate(
            [seen[g, j : j + total].reshape(rows, C2).astype(bf16) for j in range(3)], axis=1
        )
        summed = jnp.zeros((rows, C2), jnp.float32)
        for j in range(3):
            summed = summed + nt_dot(mix[:, j * C2 : (j + 1) * C2], tw[j])
        here = seen[g, 1 : total + 1].reshape(rows, C2)
        res = (here + silu(summed)).astype(bf16).astype(jnp.float32)
        resid[slot] = res
        mean = jnp.sum(res * res, axis=1, keepdims=True) * (1.0 / C2)
        normed = (res * lax.rsqrt(mean + NORM_EPS)).astype(bf16)
        q = (nt_dot(normed, wq[...]).astype(bf16) * HD ** (-0.5)).astype(bf16)
        keys = nt_dot(normed, wk[...]).astype(bf16)
        values = nt_dot(normed, wv[...]).astype(bf16)
        none = jnp.zeros((rows, C2), bf16)
        for h in range(HEADS):
            mine = head_of == h
            s = nt_dot(q, jnp.where(mine, keys, none)) + bias[...]
            top = jnp.max(s, axis=1, keepdims=True)
            p_s[slot, :, h * rows : (h + 1) * rows] = jnp.exp(s - top).astype(bf16)
            vb[slot, h * rows : (h + 1) * rows, :] = jnp.where(mine, values, none)
        weighted = jnp.dot(p_s[slot], vb[slot], preferred_element_type=jnp.float32)
        sums = jnp.dot(p_s[slot], ones[...], preferred_element_type=jnp.float32)
        attended = (weighted / sums).astype(bf16)
        full = resid[slot] + nt_dot(attended, wo[...])
        t = lax.broadcasted_iota(jnp.int32, (rows, C2), 0) // 8
        full = jnp.where(t < length, full, 0.0).astype(bf16).astype(jnp.float32)
        att[g] = full.reshape(total, 8, C2)
        sq = full * full
        squares[...] = squares[...] + jnp.sum(sq.reshape(total, 8, C2), axis=0)
        return carry

    for g in range(groups):
        group(g, 0)
    for k in range(n):
        first = (me ^ k) * frames
        at = 0
        if half == 1 and k < n // 2:
            outs[k][0 : frames * count, :] = kept[k][...]
            at = frames * count
        for f in range(frames):
            tile = jnp.concatenate([att[g, first + f] for g in range(groups)], axis=0)
            outs[k][at + f * count : at + (f + 1) * count, :] = tile.astype(bf16)
    if half == 1:
        sum_of = jnp.broadcast_to(jnp.sum(squares[...], keepdims=True), (TAIL, C2))
        row = lax.broadcasted_iota(jnp.int32, (TAIL, C2), 0)
        high = sum_of.astype(bf16).astype(jnp.float32)
        middle = (sum_of - high).astype(bf16).astype(jnp.float32)
        low = sum_of - high - middle
        tail = jnp.where(row == 0, high, jnp.where(row == 1, middle, jnp.where(row == 2, low, 0.0)))
        for k in range(n):
            outs[k][outs[k].shape[0] - TAIL :, :] = tail.astype(bf16)


def attend(n, half, meta, blocks, weights, before, kept):
    frames, both, _ = blocks[0].shape
    count = both // HALVES
    total = n * frames
    rows = total * 8
    groups = count // 8
    vmem = pl.BlockSpec(memory_space=pltpu.VMEM)
    sizes = [frames * count] * n
    if half == 1:
        sizes = [frames * (both if k < n // 2 else count) + TAIL for k in range(n)]
    res = pl.pallas_call(
        functools.partial(attend_kernel, n, half),
        out_shape=[jax.ShapeDtypeStruct((size, C2), jnp.bfloat16) for size in sizes]
        + [jax.ShapeDtypeStruct((8, C2), jnp.float32)],
        in_specs=[pl.BlockSpec(memory_space=pltpu.SMEM)] + [vmem] * (n + 6 + len(kept)),
        out_specs=[vmem] * (n + 1),
        scratch_shapes=[
            pltpu.VMEM((groups, total + 2, 8, C2), jnp.float32),
            pltpu.VMEM((2, rows, C2), jnp.float32),
            pltpu.VMEM((groups, total, 8, C2), jnp.float32),
            pltpu.VMEM((rows, rows), jnp.float32),
            pltpu.VMEM((HEADS * rows, C2), jnp.bfloat16),
            pltpu.VMEM((2, rows, HEADS * rows), jnp.bfloat16),
            pltpu.VMEM((2, HEADS * rows, C2), jnp.bfloat16),
        ],
        compiler_params=pltpu.CompilerParams(vmem_limit_bytes=VMEM_LIMIT),
        cost_estimate=pl.CostEstimate(
            flops=2 * groups * rows * C2 * (7 * C2 + 12 * rows),
            bytes_accessed=4_000_000,
            transcendentals=groups * rows * HEADS * rows,
        ),
    )(meta, *blocks, *weights, before, *kept)
    return res[:n], res[n]


def gather_kernel(n, *rest):
    early, late, out, whole = rest[: n // 2], rest[n // 2 : n // 2 + n], rest[-2], rest[-1]
    me = lax.axis_index("frame")
    frames = out.shape[0]
    count = CELLS // n
    part = count // HALVES
    for k in range(n):
        start = pl.multiple_of((me ^ k) * count, count)
        for half in range(HALVES):
            block, first = late[k], 0
            if k >= n // 2 and half == 0:
                block = early[k - n // 2]
            elif k < n // 2:
                first = half * frames * part
            for f in range(frames):
                rows = slice(first + f * part, first + (f + 1) * part)
                whole[f, pl.ds(start + half * part, part), :] = block[rows, :]
    for f in range(frames):
        out[f] = whole[f].astype(jnp.float32).T.astype(jnp.bfloat16)


def gather(n, frames, early, late):
    vmem = pl.BlockSpec(memory_space=pltpu.VMEM)
    return pl.pallas_call(
        functools.partial(gather_kernel, n),
        out_shape=jax.ShapeDtypeStruct((frames, C2, CELLS), jnp.bfloat16),
        in_specs=[vmem] * (len(early) + len(late)),
        out_specs=vmem,
        scratch_shapes=[pltpu.VMEM((frames, CELLS, C2), jnp.bfloat16)],
        compiler_params=pltpu.CompilerParams(vmem_limit_bytes=VMEM_LIMIT),
        cost_estimate=pl.CostEstimate(flops=0, bytes_accessed=4_000_000, transcendentals=0),
    )(*early, *late)


def tally_kernel(n, *rest):
    total = jnp.zeros((TAIL, C2), jnp.float32)
    for k in range(n):
        total = total + rest[k][...].astype(jnp.float32)
    rest[n][...] = jnp.broadcast_to(jnp.sum(total, axis=0, keepdims=True)[:, :128], (8, 128))


def last_tile(rows):
    return pl.BlockSpec((TAIL, C2), lambda i: (rows // TAIL - 1, 0))


def tally(n, blocks):
    return pl.pallas_call(
        functools.partial(tally_kernel, n),
        grid=(1,),
        out_shape=jax.ShapeDtypeStruct((8, 128), jnp.float32),
        in_specs=[last_tile(block.shape[0]) for block in blocks],
        out_specs=pl.BlockSpec((8, 128), lambda i: (0, 0)),
        compiler_params=pltpu.CompilerParams(vmem_limit_bytes=VMEM_LIMIT // 16),
        cost_estimate=pl.CostEstimate(flops=0, bytes_accessed=100_000, transcendentals=0),
    )(*blocks)


def far_of(n):
    return sorted(range(n // 2, n), key=lambda k: (-(k // 2), k))


def near_of(n):
    return sorted(range(1, n // 2), key=lambda k: (-(k // 2), k))


def send(n, k, block):
    return lax.ppermute(block, "frame", [(i, i ^ k) for i in range(n)])


def shards(occ, lengths, w1, w2, tw, wq, wk, wv, wo):
    n = lax.axis_size("frame")
    scenes = lax.axis_size("scene")
    frames = occ.shape[1]
    weights = (tw, wq, wk, wv, wo)
    far, cols2, w2s = conv_far(n, lengths, occ, w1.T, w2)
    moved = [None] * n
    for k in far_of(n):
        moved[k] = send(n, k, far[k - n // 2])
    near = conv_near(n, lengths, cols2, w2s)
    moved[0] = near[0]
    for k in near_of(n):
        moved[k] = send(n, k, near[k])
    squares = jnp.zeros((8, C2), jnp.float32)
    first, squares = attend(n, 0, lengths, moved, weights, squares, [])
    early = {k: send(n, k, first[k]) for k in far_of(n)}
    second, _ = attend(n, 1, lengths, moved, weights, squares, list(first[: n // 2]))
    late = [second[0]] + [None] * (n - 1)
    for k in far_of(n) + near_of(n):
        late[k] = send(n, k, second[k])
    mine = tally(n, late)
    total = mine
    for step in range(1, scenes):
        total = total + lax.ppermute(mine, "scene", [(i, i ^ step) for i in range(scenes)])
    encoded = gather(n, frames, [early[k] for k in range(n // 2, n)], late)
    slot_count = float(scenes * n * frames * CELLS * C2)
    return (encoded[None], 0.5 * total[0, 0] / slot_count)


def solution(mesh):
    placed = (P("scene", "frame", None, None), P("scene"), P(), P(), P(), P(), P(), P(), P())
    return jax.shard_map(
        shards,
        mesh=mesh,
        in_specs=placed,
        out_specs=(P("scene", "frame", None, None), P()),
        check_vma=False,
    )
```

profile of v0, /device:TPU:0, one launch (start us, length us, event | category | flops | bytes accessed | tf_op | source)
XLA Modules:
  0.0 85.2 jit_solution(11394294793877839969)
XLA Ops:
  1.3 8.1 %shard_map.104 = (bf16[4,64,256]{2,1,0:T(8,128)(2,1)S(1)}, bf16[4,64,256]{2,1,0:T(8,128)(2,1)S(1)}, bf16[4,64,256]{2,1,0:T(8,128)(2,1)S(1)}, bf16[4,64,256]{2,1,...) custom-call(s32[1]{0:T(128)S(6)} %copy.11.meta, ...), custom_call_target="tpu_custom_call" | custom-call | flops 2717908992 | bytes 4000000 | tf_op jit(solution)/shard_map/pallas_call | solution.py:171
  9.4 2.3 %shard_map.105 = (bf16[4,64,256]{2,1,0:T(8,128)(2,1)S(1)}, bf16[4,64,256]{2,1,0:T(8,128)(2,1)S(1)}, bf16[4,64,256]{2,1,0:T(8,128)(2,1)S(1)}, bf16[4,64,256]{2,1,0:T(8,128)(2,1)S(1)}) custom-call(s32[1]{0:T(128)S(6)} %copy.11.meta, bf16[4,640,1152]{2,1,0:T(8,128)(2,1)S(1)} %get-tuple-element.29.cols2, bf16[3,1152,256]{2,1,0:T(8,128)(2,1)S(1)} %get-tuple-element.30.w2s), custom_call_target="tpu_custom_call" | custom-call | flops 1811939328 | bytes 4000000 | tf_op jit(solution)/shard_map/pallas_call | solution.py:206
  11.7 3.0 %collective-permute-start = (bf16[4,64,256]{2,1,0:T(8,128)(2,1)S(1)}, bf16[4,64,256]{2,1,0:T(8,128)(2,1)S(1)}, u32[]{:S(2)}, u32[]{:S(2)}) collective-permute-start(bf16[4,64,256]{2,1,0:T(8,128)(2,1)S(1)} %get-tuple-element.32), channel_id=1, source_target_pairs={{0,1},{1,0},{2,3},{3,2},{4,5},{5,4},{6,7},{7,6},{8,9},{9,8},{10,11... | collective-permute-start | bytes 393224 | tf_op jit(solution)/shard_map/ppermute | solution.py:414
  14.7 1.6 %collective-permute-start.1 = (bf16[4,64,256]{2,1,0:T(8,128)(2,1)S(1)}, bf16[4,64,256]{2,1,0:T(8,128)(2,1)S(1)}, u32[]{:S(2)}, u32[]{:S(2)}) collective-permute-start(bf16[4,64,256]{2,1,0:T(8,128)(2,1)S(1)} %get-tuple-element.33), channel_id=1, source_target_pairs={{0,2},{1,3},{2,0},{3,1},{4,6},{5,7},{6,4},{7,5},{8,10},{9,11},{10,... | collective-permute-start | bytes 393224 | tf_op jit(solution)/shard_map/ppermute | solution.py:414
  16.3 3.0 %collective-permute-start.3 = (bf16[4,64,256]{2,1,0:T(8,128)(2,1)S(1)}, bf16[4,64,256]{2,1,0:T(8,128)(2,1)S(1)}, u32[]{:S(2)}, u32[]{:S(2)}) collective-permute-start(bf16[4,64,256]{2,1,0:T(8,128)(2,1)S(1)} %get-tuple-element.35), channel_id=1, source_target_pairs={{0,4},{1,5},{2,6},{3,7},{4,0},{5,1},{6,2},{7,3},{8,12},{9,13},{10,... | collective-permute-start | bytes 393224 | tf_op jit(solution)/shard_map/ppermute | solution.py:414
  19.3 1.3 %collective-permute-start.4 = (bf16[4,64,256]{2,1,0:T(8,128)(2,1)S(1)}, bf16[4,64,256]{2,1,0:T(8,128)(2,1)S(1)}, u32[]{:S(2)}, u32[]{:S(2)}) collective-permute-start(bf16[4,64,256]{2,1,0:T(8,128)(2,1)S(1)} %get-tuple-element.36), channel_id=1, source_target_pairs={{0,5},{1,4},{2,7},{3,6},{4,1},{5,0},{6,3},{7,2},{8,13},{9,12},{10,... | collective-permute-start | bytes 393224 | tf_op jit(solution)/shard_map/ppermute | solution.py:414
  20.6 3.6 %collective-permute-start.5 = (bf16[4,64,256]{2,1,0:T(8,128)(2,1)S(1)}, bf16[4,64,256]{2,1,0:T(8,128)(2,1)S(1)}, u32[]{:S(2)}, u32[]{:S(2)}) collective-permute-start(bf16[4,64,256]{2,1,0:T(8,128)(2,1)S(1)} %get-tuple-element.37), channel_id=1, source_target_pairs={{0,6},{1,7},{2,4},{3,5},{4,2},{5,3},{6,0},{7,1},{8,14},{9,15},{10,... | collective-permute-start | bytes 393224 | tf_op jit(solution)/shard_map/ppermute | solution.py:414
  24.2 1.3 %collective-permute-done.1.rest_2_ = bf16[4,64,256]{2,1,0:T(8,128)(2,1)S(1)} collective-permute-done((bf16[4,64,256]{2,1,0:T(8,128)(2,1)S(1)}, bf16[4,64,256]{2,1,0:T(8,128)(2,1)S(1)}, u32[]{:S(2)}, u32[]{:S(2)}) %collective-permute-start.1) | collective-permute-done | bytes 131104 | tf_op jit(solution)/shard_map/ppermute | solution.py:414
  26.3 12.4 %collective-permute-done.4.rest_5_ = bf16[4,64,256]{2,1,0:T(8,128)(2,1)S(1)} collective-permute-done((bf16[4,64,256]{2,1,0:T(8,128)(2,1)S(1)}, bf16[4,64,256]{2,1,0:T(8,128)(2,1)S(1)}, u32[]{:S(2)}, u32[]{:S(2)}) %collective-permute-start.4) | collective-permute-done | bytes 131104 | tf_op jit(solution)/shard_map/ppermute | solution.py:414
  38.8 5.0 %shard_map.106 = (bf16[128,256]{1,0:T(8,128)(2,1)S(1)}, bf16[128,256]{1,0:T(8,128)(2,1)S(1)}, bf16[128,256]{1,0:T(8,128)(2,1)S(1)}, bf16[128,256]{1,0:T(8,128)(2...) custom-call(s32[1]{0:T(128)S(6)} %copy.11.meta, ...), custom_call_target="tpu_custom_call" | custom-call | flops 2550136832 | bytes 4000000 | tf_op jit(solution)/shard_map/pallas_call | solution.py:323
  43.8 5.8 %shard_map.107 = (bf16[272,256]{1,0:T(8,128)(2,1)S(1)}, bf16[272,256]{1,0:T(8,128)(2,1)S(1)}, bf16[272,256]{1,0:T(8,128)(2,1)S(1)}, bf16[272,256]{1,0:T(8,128)(2...) custom-call(s32[1]{0:T(128)S(6)} %copy.11.meta, ...), custom_call_target="tpu_custom_call" | custom-call | flops 2550136832 | bytes 4000000 | tf_op jit(solution)/shard_map/pallas_call | solution.py:323
  49.7 6.6 %collective-permute-start.14 = (bf16[144,256]{1,0:T(8,128)(2,1)S(1)}, bf16[144,256]{1,0:T(8,128)(2,1)S(1)}, u32[]{:S(2)}, u32[]{:S(2)}) collective-permute-start(bf16[144,256]{1,0:T(8,128)(2,1)S(1)} %get-tuple-element.52), channel_id=1, source_target_pairs={{0,4},{1,5},{2,6},{3,7},{4,0},{5,1},{6,2},{7,3},{8,12},{9,13},{10,... | collective-permute-start | bytes 221192 | tf_op jit(solution)/shard_map/ppermute | solution.py:414
  56.3 1.4 %collective-permute-start.11 = (bf16[272,256]{1,0:T(8,128)(2,1)S(1)}, bf16[272,256]{1,0:T(8,128)(2,1)S(1)}, u32[]{:S(2)}, u32[]{:S(2)}) collective-permute-start(bf16[272,256]{1,0:T(8,128)(2,1)S(1)} %get-tuple-element.49), channel_id=1, source_target_pairs={{0,1},{1,0},{2,3},{3,2},{4,5},{5,4},{6,7},{7,6},{8,9},{9,8},{10,11... | collective-permute-start | bytes 417800 | tf_op jit(solution)/shard_map/ppermute | solution.py:414
  57.7 1.4 %collective-permute-start.12 = (bf16[272,256]{1,0:T(8,128)(2,1)S(1)}, bf16[272,256]{1,0:T(8,128)(2,1)S(1)}, u32[]{:S(2)}, u32[]{:S(2)}) collective-permute-start(bf16[272,256]{1,0:T(8,128)(2,1)S(1)} %get-tuple-element.50), channel_id=1, source_target_pairs={{0,2},{1,3},{2,0},{3,1},{4,6},{5,7},{6,4},{7,5},{8,10},{9,11},{10,... | collective-permute-start | bytes 417800 | tf_op jit(solution)/shard_map/ppermute | solution.py:414
  59.8 1.8 %collective-permute-done.14.rest_8_.rest_4_ = bf16[144,256]{1,0:T(8,128)(2,1)S(1)} collective-permute-done((bf16[144,256]{1,0:T(8,128)(2,1)S(1)}, bf16[144,256]{1,0:T(8,128)(2,1)S(1)}, u32[]{:S(2)}, u32[]{:S(2)}) %collective-permute-start.14) | collective-permute-done | bytes 73760 | tf_op jit(solution)/shard_map/ppermute | solution.py:414
  63.0 2.4 %collective-permute-start.17 = (bf16[144,256]{1,0:T(8,128)(2,1)S(1)}, bf16[144,256]{1,0:T(8,128)(2,1)S(1)}, u32[]{:S(2)}, u32[]{:S(2)}) collective-permute-start(bf16[144,256]{1,0:T(8,128)(2,1)S(1)} %get-tuple-element.55), channel_id=1, source_target_pairs={{0,7},{1,6},{2,5},{3,4},{4,3},{5,2},{6,1},{7,0},{8,15},{9,14},{10,... | collective-permute-start | bytes 221192 | tf_op jit(solution)/shard_map/ppermute | solution.py:414
  65.3 3.9 %collective-permute-done.16.rest_10_.rest_6_ = bf16[144,256]{1,0:T(8,128)(2,1)S(1)} collective-permute-done((bf16[144,256]{1,0:T(8,128)(2,1)S(1)}, bf16[144,256]{1,0:T(8,128)(2,1)S(1)}, u32[]{:S(2)}, u32[]{:S(2)}) %collective-permute-start.16) | collective-permute-done | bytes 73760 | tf_op jit(solution)/shard_map/ppermute | solution.py:414
  69.3 2.2 %collective-permute-start.10 = (bf16[128,256]{1,0:T(8,128)(2,1)S(1)}, bf16[128,256]{1,0:T(8,128)(2,1)S(1)}, u32[]{:S(2)}, u32[]{:S(2)}) collective-permute-start(bf16[128,256]{1,0:T(8,128)(2,1)S(1)} %get-tuple-element.42), channel_id=1, source_target_pairs={{0,7},{1,6},{2,5},{3,4},{4,3},{5,2},{6,1},{7,0},{8,15},{9,14},{10,... | collective-permute-start | bytes 196616 | tf_op jit(solution)/shard_map/ppermute | solution.py:414
  72.1 3.3 %collective-permute-start.8 = (bf16[128,256]{1,0:T(8,128)(2,1)S(1)}, bf16[128,256]{1,0:T(8,128)(2,1)S(1)}, u32[]{:S(2)}, u32[]{:S(2)}) collective-permute-start(bf16[128,256]{1,0:T(8,128)(2,1)S(1)} %get-tuple-element.40), channel_id=1, source_target_pairs={{0,5},{1,4},{2,7},{3,6},{4,1},{5,0},{6,3},{7,2},{8,13},{9,12},{10,... | collective-permute-start | bytes 196616 | tf_op jit(solution)/shard_map/ppermute | solution.py:414
  75.5 1.4 %collective-permute-start.9 = (bf16[128,256]{1,0:T(8,128)(2,1)S(1)}, bf16[128,256]{1,0:T(8,128)(2,1)S(1)}, u32[]{:S(2)}, u32[]{:S(2)}) collective-permute-start(bf16[128,256]{1,0:T(8,128)(2,1)S(1)} %get-tuple-element.41), channel_id=1, source_target_pairs={{0,6},{1,7},{2,4},{3,5},{4,2},{5,3},{6,0},{7,1},{8,14},{9,15},{10,... | collective-permute-start | bytes 196616 | tf_op jit(solution)/shard_map/ppermute | solution.py:414
  77.0 1.6 %collective-permute-start.19 = (f32[8,128]{1,0:T(8,128)S(1)}, f32[8,128]{1,0:T(8,128)S(1)}, u32[]{:S(2)}, u32[]{:S(2)}) collective-permute-start(f32[8,128]{1,0:T(8,128)S(1)} %shard_map.109), channel_id=1, source_target_pairs={{0,16},{8,24},{16,0},{24,8},{1,17},{9,25},{17,1},{25,9},{2,18},{10... | collective-permute-start | bytes 12296 | tf_op jit(solution)/shard_map/ppermute | solution.py:440
  78.9 1.3 %collective-permute-done.8.rest_1_ = bf16[128,256]{1,0:T(8,128)(2,1)S(1)} collective-permute-done((bf16[128,256]{1,0:T(8,128)(2,1)S(1)}, bf16[128,256]{1,0:T(8,128)(2,1)S(1)}, u32[]{:S(2)}, u32[]{:S(2)}) %collective-permute-start.8) | collective-permute-done | bytes 65568 | tf_op jit(solution)/shard_map/ppermute | solution.py:414
  80.2 1.3 %collective-permute-done.9.rest_2_ = bf16[128,256]{1,0:T(8,128)(2,1)S(1)} collective-permute-done((bf16[128,256]{1,0:T(8,128)(2,1)S(1)}, bf16[128,256]{1,0:T(8,128)(2,1)S(1)}, u32[]{:S(2)}, u32[]{:S(2)}) %collective-permute-start.9) | collective-permute-done | bytes 65568 | tf_op jit(solution)/shard_map/ppermute | solution.py:414
  81.5 1.4 %shard_map.108 = bf16[4,256,512]{2,1,0:T(8,128)(2,1)} custom-call(bf16[128,256]{1,0:T(8,128)(2,1)S(1)} %collective-permute-done.7.rest_0_, bf16[128,256]{1,0:T(8,128)(2,1)S(1)} %collective-permute-done.8.rest_1_, bf16[128,256]{1,0:T(8,128)(2,1)S(1)} %collective-permute-done.9.rest_2_, bf16[128,256]{1,0:T(8,128)(2,1)S(1)} %collective-permute-done.10.rest_3_, ...), custom_call_target="tpu_custom_call" | custom-call | bytes 4000000 | tf_op jit(solution)/shard_map/pallas_call | solution.py:371
  (37 shorter events, 4.5 us)
Async XLA Ops:
  9.3 29.4 %copy-start = (bf16[3,256,256]{2,1,0:T(8,128)(2,1)S(1)}, bf16[3,256,256]{2,1,0:T(8,128)(2,1)}, u32[]{:S(2)}) copy-start(bf16[3,256,256]{2,1,0:T(8,128)(2,1)} %rest_8_.3) | copy-start | bytes 1179652
  9.4 29.4 %copy-start.1 = (bf16[256,256]{1,0:T(8,128)(2,1)S(1)}, bf16[256,256]{1,0:T(8,128)(2,1)}, u32[]{:S(2)}) copy-start(bf16[256,256]{1,0:T(8,128)(2,1)} %rest_9_.3) | copy-start | bytes 393220
  9.4 29.4 %copy-start.2 = (bf16[256,256]{1,0:T(8,128)(2,1)S(1)}, bf16[256,256]{1,0:T(8,128)(2,1)}, u32[]{:S(2)}) copy-start(bf16[256,256]{1,0:T(8,128)(2,1)} %rest_10_.3) | copy-start | bytes 393220
  11.7 8.9 %collective-permute-start = (bf16[4,64,256]{2,1,0:T(8,128)(2,1)S(1)}, bf16[4,64,256]{2,1,0:T(8,128)(2,1)S(1)}, u32[]{:S(2)}, u32[]{:S(2)}) collective-permute-start(bf16[4,64,256]{2,1,0:T(8,128)(2,1)S(1)} %get-tuple-element.32), channel_id=1, source_target_pairs={{0,1},{1,0},{2,3},{3,2},{4,5},{5,4},{6,7},{7,6},{8,9},{9,8},{10,11... | collective-permute-start | bytes 393224 | tf_op jit(solution)/shard_map/ppermute | solution.py:414
  14.7 10.8 %collective-permute-start.1 = (bf16[4,64,256]{2,1,0:T(8,128)(2,1)S(1)}, bf16[4,64,256]{2,1,0:T(8,128)(2,1)S(1)}, u32[]{:S(2)}, u32[]{:S(2)}) collective-permute-start(bf16[4,64,256]{2,1,0:T(8,128)(2,1)S(1)} %get-tuple-element.33), channel_id=1, source_target_pairs={{0,2},{1,3},{2,0},{3,1},{4,6},{5,7},{6,4},{7,5},{8,10},{9,11},{10,... | collective-permute-start | bytes 393224 | tf_op jit(solution)/shard_map/ppermute | solution.py:414
  16.3 9.9 %collective-permute-start.2 = (bf16[4,64,256]{2,1,0:T(8,128)(2,1)S(1)}, bf16[4,64,256]{2,1,0:T(8,128)(2,1)S(1)}, u32[]{:S(2)}, u32[]{:S(2)}) collective-permute-start(bf16[4,64,256]{2,1,0:T(8,128)(2,1)S(1)} %get-tuple-element.34), channel_id=1, source_target_pairs={{0,3},{1,2},{2,1},{3,0},{4,7},{5,6},{6,5},{7,4},{8,11},{9,10},{10,... | collective-permute-start | bytes 393224 | tf_op jit(solution)/shard_map/ppermute | solution.py:414
  16.3 9.9 %collective-permute-start.3 = (bf16[4,64,256]{2,1,0:T(8,128)(2,1)S(1)}, bf16[4,64,256]{2,1,0:T(8,128)(2,1)S(1)}, u32[]{:S(2)}, u32[]{:S(2)}) collective-permute-start(bf16[4,64,256]{2,1,0:T(8,128)(2,1)S(1)} %get-tuple-element.35), channel_id=1, source_target_pairs={{0,4},{1,5},{2,6},{3,7},{4,0},{5,1},{6,2},{7,3},{8,12},{9,13},{10,... | collective-permute-start | bytes 393224 | tf_op jit(solution)/shard_map/ppermute | solution.py:414
  19.3 19.4 %collective-permute-start.4 = (bf16[4,64,256]{2,1,0:T(8,128)(2,1)S(1)}, bf16[4,64,256]{2,1,0:T(8,128)(2,1)S(1)}, u32[]{:S(2)}, u32[]{:S(2)}) collective-permute-start(bf16[4,64,256]{2,1,0:T(8,128)(2,1)S(1)} %get-tuple-element.36), channel_id=1, source_target_pairs={{0,5},{1,4},{2,7},{3,6},{4,1},{5,0},{6,3},{7,2},{8,13},{9,12},{10,... | collective-permute-start | bytes 393224 | tf_op jit(solution)/shard_map/ppermute | solution.py:414
  20.6 18.1 %collective-permute-start.5 = (bf16[4,64,256]{2,1,0:T(8,128)(2,1)S(1)}, bf16[4,64,256]{2,1,0:T(8,128)(2,1)S(1)}, u32[]{:S(2)}, u32[]{:S(2)}) collective-permute-start(bf16[4,64,256]{2,1,0:T(8,128)(2,1)S(1)} %get-tuple-element.37), channel_id=1, source_target_pairs={{0,6},{1,7},{2,4},{3,5},{4,2},{5,3},{6,0},{7,1},{8,14},{9,15},{10,... | collective-permute-start | bytes 393224 | tf_op jit(solution)/shard_map/ppermute | solution.py:414
  25.5 13.2 %collective-permute-start.6 = (bf16[4,64,256]{2,1,0:T(8,128)(2,1)S(1)}, bf16[4,64,256]{2,1,0:T(8,128)(2,1)S(1)}, u32[]{:S(2)}, u32[]{:S(2)}) collective-permute-start(bf16[4,64,256]{2,1,0:T(8,128)(2,1)S(1)} %get-tuple-element.38), channel_id=1, source_target_pairs={{0,7},{1,6},{2,5},{3,4},{4,3},{5,2},{6,1},{7,0},{8,15},{9,14},{10,... | collective-permute-start | bytes 393224 | tf_op jit(solution)/shard_map/ppermute | solution.py:414
  49.7 11.9 %collective-permute-start.14 = (bf16[144,256]{1,0:T(8,128)(2,1)S(1)}, bf16[144,256]{1,0:T(8,128)(2,1)S(1)}, u32[]{:S(2)}, u32[]{:S(2)}) collective-permute-start(bf16[144,256]{1,0:T(8,128)(2,1)S(1)} %get-tuple-element.52), channel_id=1, source_target_pairs={{0,4},{1,5},{2,6},{3,7},{4,0},{5,1},{6,2},{7,3},{8,12},{9,13},{10,... | collective-permute-start | bytes 221192 | tf_op jit(solution)/shard_map/ppermute | solution.py:414
  56.2 6.7 %collective-permute-start.15 = (bf16[144,256]{1,0:T(8,128)(2,1)S(1)}, bf16[144,256]{1,0:T(8,128)(2,1)S(1)}, u32[]{:S(2)}, u32[]{:S(2)}) collective-permute-start(bf16[144,256]{1,0:T(8,128)(2,1)S(1)} %get-tuple-element.53), channel_id=1, source_target_pairs={{0,5},{1,4},{2,7},{3,6},{4,1},{5,0},{6,3},{7,2},{8,13},{9,12},{10,... | collective-permute-start | bytes 221192 | tf_op jit(solution)/shard_map/ppermute | solution.py:414
  56.3 15.8 %collective-permute-start.11 = (bf16[272,256]{1,0:T(8,128)(2,1)S(1)}, bf16[272,256]{1,0:T(8,128)(2,1)S(1)}, u32[]{:S(2)}, u32[]{:S(2)}) collective-permute-start(bf16[272,256]{1,0:T(8,128)(2,1)S(1)} %get-tuple-element.49), channel_id=1, source_target_pairs={{0,1},{1,0},{2,3},{3,2},{4,5},{5,4},{6,7},{7,6},{8,9},{9,8},{10,11... | collective-permute-start | bytes 417800 | tf_op jit(solution)/shard_map/ppermute | solution.py:414
  57.7 17.8 %collective-permute-start.12 = (bf16[272,256]{1,0:T(8,128)(2,1)S(1)}, bf16[272,256]{1,0:T(8,128)(2,1)S(1)}, u32[]{:S(2)}, u32[]{:S(2)}) collective-permute-start(bf16[272,256]{1,0:T(8,128)(2,1)S(1)} %get-tuple-element.50), channel_id=1, source_target_pairs={{0,2},{1,3},{2,0},{3,1},{4,6},{5,7},{6,4},{7,5},{8,10},{9,11},{10,... | collective-permute-start | bytes 417800 | tf_op jit(solution)/shard_map/ppermute | solution.py:414
  59.1 17.8 %collective-permute-start.13 = (bf16[272,256]{1,0:T(8,128)(2,1)S(1)}, bf16[272,256]{1,0:T(8,128)(2,1)S(1)}, u32[]{:S(2)}, u32[]{:S(2)}) collective-permute-start(bf16[272,256]{1,0:T(8,128)(2,1)S(1)} %get-tuple-element.51), channel_id=1, source_target_pairs={{0,3},{1,2},{2,1},{3,0},{4,7},{5,6},{6,5},{7,4},{8,11},{9,10},{10,... | collective-permute-start | bytes 417800 | tf_op jit(solution)/shard_map/ppermute | solution.py:414
  61.5 7.7 %collective-permute-start.16 = (bf16[144,256]{1,0:T(8,128)(2,1)S(1)}, bf16[144,256]{1,0:T(8,128)(2,1)S(1)}, u32[]{:S(2)}, u32[]{:S(2)}) collective-permute-start(bf16[144,256]{1,0:T(8,128)(2,1)S(1)} %get-tuple-element.54), channel_id=1, source_target_pairs={{0,6},{1,7},{2,4},{3,5},{4,2},{5,3},{6,0},{7,1},{8,14},{9,15},{10,... | collective-permute-start | bytes 221192 | tf_op jit(solution)/shard_map/ppermute | solution.py:414
  63.0 8.4 %collective-permute-start.17 = (bf16[144,256]{1,0:T(8,128)(2,1)S(1)}, bf16[144,256]{1,0:T(8,128)(2,1)S(1)}, u32[]{:S(2)}, u32[]{:S(2)}) collective-permute-start(bf16[144,256]{1,0:T(8,128)(2,1)S(1)} %get-tuple-element.55), channel_id=1, source_target_pairs={{0,7},{1,6},{2,5},{3,4},{4,3},{5,2},{6,1},{7,0},{8,15},{9,14},{10,... | collective-permute-start | bytes 221192 | tf_op jit(solution)/shard_map/ppermute | solution.py:414
  69.3 7.8 %collective-permute-start.10 = (bf16[128,256]{1,0:T(8,128)(2,1)S(1)}, bf16[128,256]{1,0:T(8,128)(2,1)S(1)}, u32[]{:S(2)}, u32[]{:S(2)}) collective-permute-start(bf16[128,256]{1,0:T(8,128)(2,1)S(1)} %get-tuple-element.42), channel_id=1, source_target_pairs={{0,7},{1,6},{2,5},{3,4},{4,3},{5,2},{6,1},{7,0},{8,15},{9,14},{10,... | collective-permute-start | bytes 196616 | tf_op jit(solution)/shard_map/ppermute | solution.py:414
  71.4 7.2 %collective-permute-start.7 = (bf16[128,256]{1,0:T(8,128)(2,1)S(1)}, bf16[128,256]{1,0:T(8,128)(2,1)S(1)}, u32[]{:S(2)}, u32[]{:S(2)}) collective-permute-start(bf16[128,256]{1,0:T(8,128)(2,1)S(1)} %get-tuple-element.39), channel_id=1, source_target_pairs={{0,4},{1,5},{2,6},{3,7},{4,0},{5,1},{6,2},{7,3},{8,12},{9,13},{10,... | collective-permute-start | bytes 196616 | tf_op jit(solution)/shard_map/ppermute | solution.py:414
  72.1 8.1 %collective-permute-start.8 = (bf16[128,256]{1,0:T(8,128)(2,1)S(1)}, bf16[128,256]{1,0:T(8,128)(2,1)S(1)}, u32[]{:S(2)}, u32[]{:S(2)}) collective-permute-start(bf16[128,256]{1,0:T(8,128)(2,1)S(1)} %get-tuple-element.40), channel_id=1, source_target_pairs={{0,5},{1,4},{2,7},{3,6},{4,1},{5,0},{6,3},{7,2},{8,13},{9,12},{10,... | collective-permute-start | bytes 196616 | tf_op jit(solution)/shard_map/ppermute | solution.py:414
  75.5 6.1 %collective-permute-start.9 = (bf16[128,256]{1,0:T(8,128)(2,1)S(1)}, bf16[128,256]{1,0:T(8,128)(2,1)S(1)}, u32[]{:S(2)}, u32[]{:S(2)}) collective-permute-start(bf16[128,256]{1,0:T(8,128)(2,1)S(1)} %get-tuple-element.41), channel_id=1, source_target_pairs={{0,6},{1,7},{2,4},{3,5},{4,2},{5,3},{6,0},{7,1},{8,14},{9,15},{10,... | collective-permute-start | bytes 196616 | tf_op jit(solution)/shard_map/ppermute | solution.py:414
  76.9 6.0 %collective-permute-start.18 = (f32[8,128]{1,0:T(8,128)S(1)}, f32[8,128]{1,0:T(8,128)S(1)}, u32[]{:S(2)}, u32[]{:S(2)}) collective-permute-start(f32[8,128]{1,0:T(8,128)S(1)} %shard_map.109), channel_id=1, source_target_pairs={{0,8},{8,0},{16,24},{24,16},{1,9},{9,1},{17,25},{25,17},{2,10},{10... | collective-permute-start | bytes 12296 | tf_op jit(solution)/shard_map/ppermute | solution.py:440
  77.0 5.9 %collective-permute-start.19 = (f32[8,128]{1,0:T(8,128)S(1)}, f32[8,128]{1,0:T(8,128)S(1)}, u32[]{:S(2)}, u32[]{:S(2)}) collective-permute-start(f32[8,128]{1,0:T(8,128)S(1)} %shard_map.109), channel_id=1, source_target_pairs={{0,16},{8,24},{16,0},{24,8},{1,17},{9,25},{17,1},{25,9},{2,18},{10... | collective-permute-start | bytes 12296 | tf_op jit(solution)/shard_map/ppermute | solution.py:440
  78.6 4.3 %collective-permute-start.20 = (f32[8,128]{1,0:T(8,128)S(1)}, f32[8,128]{1,0:T(8,128)S(1)}, u32[]{:S(2)}, u32[]{:S(2)}) collective-permute-start(f32[8,128]{1,0:T(8,128)S(1)} %shard_map.109), channel_id=1, source_target_pairs={{0,24},{8,16},{16,8},{24,0},{1,25},{9,17},{17,9},{25,1},{2,26},{10... | collective-permute-start | bytes 12296 | tf_op jit(solution)/shard_map/ppermute | solution.py:440
  (2 other events, 58.8 us)
where the time goes:
time: 85.4 us; the launch traced here: 85.2 us
  starting transfers between devices  35.9 us (42%)
  waiting for transfers between devices  23 us (27%)
  Pallas kernels  22.7 us (27%)
  between operations  3.21 us (4%)
    ppermute x18, starting transfers between devices, send(): return lax.ppermute(block, 'frame', [(i, i ^ k) for i in range(n)])  33.9 us
    ppermute x18, waiting for transfers between devices, send(): return lax.ppermute(block, 'frame', [(i, i ^ k) for i in range(n)])  23 us
    pallas_call x2, Pallas kernels, attend(): pl.pallas_call(functools.partial(attend_kernel, n, half), out_shape=[jax....  10.9 us
    pallas_call x1, Pallas kernels, conv_far(): pl.pallas_call(functools.partial(conv_kernel, n), out_shape=[jax.ShapeDty...  8.06 us
    pallas_call x1, Pallas kernels, conv_near(): pl.pallas_call(functools.partial(near_kernel, n), out_shape=[jax.ShapeDty...  2.3 us
    ppermute x3, starting transfers between devices, shards(): lax.ppermute(mine, 'scene', [(i, i ^ step) for i in range(scenes)])  1.91 us
  transfers between devices with their start and end apart: 21, of which 7 were waited for; matrix products, arithmetic and copies ran while one was open for 0% of the time, Pallas kernels for 2%

commit v1 on v0

--- a/solution.py
+++ b/solution.py
@@ -79,13 +79,18 @@
         for k in range(n // 2):
             at = (me ^ (k + n // 2 if far else k)) % (n // 2)
             start = pl.multiple_of(f * half + at * count, count)
-            outs[k][f] = y2[pl.ds(start, count), :].astype(jnp.bfloat16)
+            block = y2[pl.ds(start, count), :].astype(jnp.bfloat16)
+            if far:
+                outs[k][f] = block[: count // 2]
+                outs[k + n // 2][f] = block[count // 2 :]
+            else:
+                outs[k][f] = block
 
 
 def conv_kernel(n, meta, occ_hbm, w1_hbm, w2_hbm, *rest):
-    outs = rest[: n // 2]
-    cols2, w2s = rest[n // 2 : n // 2 + 2]
-    occ, w1, w2, t1, t2, w1s, cols1, y1, y2, sems = rest[n // 2 + 2 :]
+    outs = rest[:n]
+    cols2, w2s = rest[n : n + 2]
+    occ, w1, w2, t1, t2, w1s, cols1, y1, y2, sems = rest[n + 2 :]
     frames = occ.shape[0]
     bf16 = jnp.bfloat16
 
@@ -170,13 +175,13 @@
     f32, bf16 = jnp.float32, jnp.bfloat16
     res = pl.pallas_call(
         functools.partial(conv_kernel, n),
-        out_shape=[jax.ShapeDtypeStruct((frames, count, C2), bf16)] * (n // 2)
+        out_shape=[jax.ShapeDtypeStruct((frames, count // 2, C2), bf16)] * n
         + [
             jax.ShapeDtypeStruct((frames, (ROWS + 2) * ROW, 9 * C1), bf16),
             jax.ShapeDtypeStruct((3, 9 * C1, C2), bf16),
         ],
         in_specs=[pl.BlockSpec(memory_space=pltpu.SMEM), hbm, hbm, hbm],
-        out_specs=[vmem] * (n // 2 + 2),
+        out_specs=[vmem] * (n + 2),
         scratch_shapes=[
             pltpu.VMEM((frames, CIN, HI * HI * ZD), bf16),
             pltpu.VMEM((CIN * 27, C1), bf16),
@@ -196,7 +201,7 @@
             transcendentals=frames * CELLS * (C1 + C2),
         ),
     )(meta, *[pltpu.with_memory_space_constraint(x, pltpu.HBM) for x in (occ, w1, w2)])
-    return res[: n // 2], res[n // 2], res[n // 2 + 1]
+    return res[: n // 2], res[n // 2 : n], res[n], res[n + 1]
 
 
 def conv_near(n, meta, cols2, w2s):
@@ -222,74 +227,92 @@
     return lax.dot_general(a, b, (((1,), (1,)), ((), ())), preferred_element_type=jnp.float32)
 
 
+def swap_cells(even, odd):
+    upper = lax.broadcasted_iota(jnp.int32, even.shape, even.ndim - 2) < 4
+    low = jnp.where(upper, even, pltpu.roll(odd, 4, odd.ndim - 2))
+    high = jnp.where(upper, pltpu.roll(even, 4, even.ndim - 2), odd)
+    return low, high
+
+
 def attend_kernel(n, half, meta, *rest):
     blocks = rest[:n]
     tw, wq, wk, wv, wo, before = rest[n : n + 6]
     rest = rest[n + 6 :]
     kept, rest = rest[: n // 2 * half], rest[n // 2 * half :]
     outs, squares = rest[:n], rest[n]
-    seen, resid, att, bias, ones, p_s, vb = rest[n + 1 :]
+    seen, resid, q_s, k_s, v_s, a_s, kb, vb, p_s, bias, ones = rest[n + 1 :]
     me, length = lax.axis_index("frame"), meta[0]
     frames, count = blocks[0].shape[0], blocks[0].shape[1] // HALVES
+    first_cell = [half * count if k < n // 2 else 0 for k in range(n)]
     groups = count // 8
     total = n * frames
-    rows = total * 8
-    bf16 = jnp.bfloat16
+    rows = total * 4
+    everything = 2 * groups * rows
+    f32, bf16 = jnp.float32, jnp.bfloat16
     head_of = lax.broadcasted_iota(jnp.int32, (rows, C2), 1) // HD
 
-    edge = jnp.zeros((groups, 1, 8, C2), jnp.float32)
+    edge = jnp.zeros((groups, 1, 8, C2), f32)
     seen[:, 0:1] = edge
     seen[:, total + 1 : total + 2] = edge
     for k in range(n):
         first = (me ^ k) * frames + 1
         for f in range(frames):
-            tile = blocks[k][f, half * count : (half + 1) * count, :].astype(jnp.float32).reshape(groups, 8, C2)
+            tile = blocks[k][f, first_cell[k] : first_cell[k] + count, :]
+            tile = tile.astype(f32).reshape(groups, 8, C2)
             for g in range(groups):
                 seen[g, first + f] = tile[g]
 
     at = lax.broadcasted_iota(jnp.int32, (rows, rows), 0)
     to = lax.broadcasted_iota(jnp.int32, (rows, rows), 1)
-    bias[...] = jnp.where((at % 8 == to % 8) & (to // 8 < length), 0.0, NEG)
+    bias[...] = jnp.where((at % 4 == to % 4) & (to // 4 < length), 0.0, NEG)
     for h in range(HEADS):
         ones[h * rows : (h + 1) * rows, :] = jnp.where(head_of == h, 1.0, 0.0).astype(bf16)
-    squares[...] = before[...]
-
-    def group(g, carry):
-        slot = g % 2
-        mix = jnp.concatenate(
-            [seen[g, j : j + total].reshape(rows, C2).astype(bf16) for j in range(3)], axis=1
-        )
-        summed = jnp.zeros((rows, C2), jnp.float32)
+
+    for g in range(groups):
+        summed = jnp.zeros((total * 8, C2), f32)
         for j in range(3):
-            summed = summed + nt_dot(mix[:, j * C2 : (j + 1) * C2], tw[j])
-        here = seen[g, 1 : total + 1].reshape(rows, C2)
-        res = (here + silu(summed)).astype(bf16).astype(jnp.float32)
-        resid[slot] = res
-        mean = jnp.sum(res * res, axis=1, keepdims=True) * (1.0 / C2)
-        normed = (res * lax.rsqrt(mean + NORM_EPS)).astype(bf16)
-        q = (nt_dot(normed, wq[...]).astype(bf16) * HD ** (-0.5)).astype(bf16)
-        keys = nt_dot(normed, wk[...]).astype(bf16)
-        values = nt_dot(normed, wv[...]).astype(bf16)
-        none = jnp.zeros((rows, C2), bf16)
+            mix = seen[g, j : j + total].reshape(total * 8, C2).astype(bf16)
+            summed = summed + nt_dot(mix, tw[j])
+        res = (seen[g, 1 : total + 1].reshape(total * 8, C2) + silu(summed)).astype(bf16)
+        res = res.astype(f32).reshape(total // 2, 2, 8, C2)
+        low, high = swap_cells(res[:, 0], res[:, 1])
+        for part, value in ((0, low), (1, high)):
+            value = value.reshape(rows, C2)
+            start = (2 * g + part) * rows
+            resid[start : start + rows, :] = value
+            mean = jnp.sum(value * value, axis=1, keepdims=True) * (1.0 / C2)
+            a_s[start : start + rows, :] = (value * lax.rsqrt(mean + NORM_EPS)).astype(bf16)
+    normed = a_s[...]
+    q_s[...] = (nt_dot(normed, wq[...]).astype(bf16) * HD ** (-0.5)).astype(bf16)
+    k_s[...] = nt_dot(normed, wk[...]).astype(bf16)
+    v_s[...] = nt_dot(normed, wv[...]).astype(bf16)
+
+    none = jnp.zeros((rows, C2), bf16)
+    for b in range(2 * groups):
+        slot = b % 2
+        here = slice(b * rows, (b + 1) * rows)
+        keys, values = k_s[here, :], v_s[here, :]
         for h in range(HEADS):
-            mine = head_of == h
-            s = nt_dot(q, jnp.where(mine, keys, none)) + bias[...]
-            top = jnp.max(s, axis=1, keepdims=True)
-            p_s[slot, :, h * rows : (h + 1) * rows] = jnp.exp(s - top).astype(bf16)
-            vb[slot, h * rows : (h + 1) * rows, :] = jnp.where(mine, values, none)
-        weighted = jnp.dot(p_s[slot], vb[slot], preferred_element_type=jnp.float32)
-        sums = jnp.dot(p_s[slot], ones[...], preferred_element_type=jnp.float32)
-        attended = (weighted / sums).astype(bf16)
-        full = resid[slot] + nt_dot(attended, wo[...])
-        t = lax.broadcasted_iota(jnp.int32, (rows, C2), 0) // 8
-        full = jnp.where(t < length, full, 0.0).astype(bf16).astype(jnp.float32)
-        att[g] = full.reshape(total, 8, C2)
-        sq = full * full
-        squares[...] = squares[...] + jnp.sum(sq.reshape(total, 8, C2), axis=0)
-        return carry
-
+            kb[slot, h * rows : (h + 1) * rows, :] = jnp.where(head_of == h, keys, none)
+            vb[slot, h * rows : (h + 1) * rows, :] = jnp.where(head_of == h, values, none)
+        s = nt_dot(q_s[here, :], kb[slot])
+        for h in range(HEADS):
+            mine = s[:, h * rows : (h + 1) * rows] + bias[...]
+            top = jnp.max(mine, axis=1, keepdims=True)
+            p_s[slot, :, h * rows : (h + 1) * rows] = jnp.exp(mine - top).astype(bf16)
+        weighted = jnp.dot(p_s[slot], vb[slot], preferred_element_type=f32)
+        sums = jnp.dot(p_s[slot], ones[...], preferred_element_type=f32)
+        a_s[here, :] = (weighted / sums).astype(bf16)
+
+    full = resid[...] + nt_dot(a_s[...], wo[...])
+    t = lax.broadcasted_iota(jnp.int32, (everything, C2), 0) % rows // 4
+    full = jnp.where(t < length, full, 0.0).astype(bf16).astype(f32)
+    squares[...] = before[...] + jnp.sum((full * full).reshape(everything // 8, 8, C2), axis=0)
+    full = full.reshape(groups, 2, total // 2, 8, C2)
     for g in range(groups):
-        group(g, 0)
+        even, odd = swap_cells(full[g, 0], full[g, 1])
+        seen[g, 0:total] = jnp.stack([even, odd], axis=1).reshape(total, 8, C2)
+
     for k in range(n):
         first = (me ^ k) * frames
         at = 0
@@ -297,13 +320,13 @@
             outs[k][0 : frames * count, :] = kept[k][...]
             at = frames * count
         for f in range(frames):
-            tile = jnp.concatenate([att[g, first + f] for g in range(groups)], axis=0)
+            tile = jnp.concatenate([seen[g, first + f] for g in range(groups)], axis=0)
             outs[k][at + f * count : at + (f + 1) * count, :] = tile.astype(bf16)
     if half == 1:
         sum_of = jnp.broadcast_to(jnp.sum(squares[...], keepdims=True), (TAIL, C2))
         row = lax.broadcasted_iota(jnp.int32, (TAIL, C2), 0)
-        high = sum_of.astype(bf16).astype(jnp.float32)
-        middle = (sum_of - high).astype(bf16).astype(jnp.float32)
+        high = sum_of.astype(bf16).astype(f32)
+        middle = (sum_of - high).astype(bf16).astype(f32)
         low = sum_of - high - middle
         tail = jnp.where(row == 0, high, jnp.where(row == 1, middle, jnp.where(row == 2, low, 0.0)))
         for k in range(n):
@@ -314,32 +337,38 @@
     frames, both, _ = blocks[0].shape
     count = both // HALVES
     total = n * frames
-    rows = total * 8
+    rows = total * 4
     groups = count // 8
+    everything = 2 * groups * rows
     vmem = pl.BlockSpec(memory_space=pltpu.VMEM)
+    f32, bf16 = jnp.float32, jnp.bfloat16
     sizes = [frames * count] * n
     if half == 1:
         sizes = [frames * (both if k < n // 2 else count) + TAIL for k in range(n)]
     res = pl.pallas_call(
         functools.partial(attend_kernel, n, half),
-        out_shape=[jax.ShapeDtypeStruct((size, C2), jnp.bfloat16) for size in sizes]
-        + [jax.ShapeDtypeStruct((8, C2), jnp.float32)],
+        out_shape=[jax.ShapeDtypeStruct((size, C2), bf16) for size in sizes]
+        + [jax.ShapeDtypeStruct((8, C2), f32)],
         in_specs=[pl.BlockSpec(memory_space=pltpu.SMEM)] + [vmem] * (n + 6 + len(kept)),
         out_specs=[vmem] * (n + 1),
         scratch_shapes=[
-            pltpu.VMEM((groups, total + 2, 8, C2), jnp.float32),
-            pltpu.VMEM((2, rows, C2), jnp.float32),
-            pltpu.VMEM((groups, total, 8, C2), jnp.float32),
-            pltpu.VMEM((rows, rows), jnp.float32),
-            pltpu.VMEM((HEADS * rows, C2), jnp.bfloat16),
-            pltpu.VMEM((2, rows, HEADS * rows), jnp.bfloat16),
-            pltpu.VMEM((2, HEADS * rows, C2), jnp.bfloat16),
+            pltpu.VMEM((groups, total + 2, 8, C2), f32),
+            pltpu.VMEM((everything, C2), f32),
+            pltpu.VMEM((everything, C2), bf16),
+            pltpu.VMEM((everything, C2), bf16),
+            pltpu.VMEM((everything, C2), bf16),
+            pltpu.VMEM((everything, C2), bf16),
+            pltpu.VMEM((2, HEADS * rows, C2), bf16),
+            pltpu.VMEM((2, HEADS * rows, C2), bf16),
+            pltpu.VMEM((2, rows, HEADS * rows), bf16),
+            pltpu.VMEM((rows, rows), f32),
+            pltpu.VMEM((HEADS * rows, C2), bf16),
         ],
         compiler_params=pltpu.CompilerParams(vmem_limit_bytes=VMEM_LIMIT),
         cost_estimate=pl.CostEstimate(
-            flops=2 * groups * rows * C2 * (7 * C2 + 12 * rows),
+            flops=2 * everything * C2 * (7 * C2 + 12 * rows),
             bytes_accessed=4_000_000,
-            transcendentals=groups * rows * HEADS * rows,
+            transcendentals=everything * HEADS * rows,
         ),
     )(meta, *blocks, *weights, before, *kept)
     return res[:n], res[n]
@@ -402,12 +431,31 @@
     )(*blocks)
 
 
+def finish_kernel(scale, mine, *rest):
+    total = mine[...]
+    for other in rest[:-1]:
+        total = total + other[...]
+    rest[-1][0, 0] = jnp.max(total) * scale
+
+
+def finish(scale, mine, others):
+    vmem = pl.BlockSpec(memory_space=pltpu.VMEM)
+    return pl.pallas_call(
+        functools.partial(finish_kernel, scale),
+        out_shape=jax.ShapeDtypeStruct((1, 1), jnp.float32),
+        in_specs=[vmem] * (1 + len(others)),
+        out_specs=pl.BlockSpec(memory_space=pltpu.SMEM),
+        compiler_params=pltpu.CompilerParams(vmem_limit_bytes=VMEM_LIMIT // 16),
+        cost_estimate=pl.CostEstimate(flops=0, bytes_accessed=100_000, transcendentals=0),
+    )(mine, *others)
+
+
 def far_of(n):
-    return sorted(range(n // 2, n), key=lambda k: (-(k // 2), k))
+    return list(range(n // 2, n))
 
 
 def near_of(n):
-    return sorted(range(1, n // 2), key=lambda k: (-(k // 2), k))
+    return list(range(1, n // 2))
 
 
 def send(n, k, block):
@@ -419,28 +467,31 @@
     scenes = lax.axis_size("scene")
     frames = occ.shape[1]
     weights = (tw, wq, wk, wv, wo)
-    far, cols2, w2s = conv_far(n, lengths, occ, w1.T, w2)
-    moved = [None] * n
+    far0, far1, cols2, w2s = conv_far(n, lengths, occ, w1.T, w2)
+    moved0, moved1 = [None] * n, [None] * n
     for k in far_of(n):
-        moved[k] = send(n, k, far[k - n // 2])
+        moved0[k] = send(n, k, far0[k - n // 2])
     near = conv_near(n, lengths, cols2, w2s)
-    moved[0] = near[0]
+    moved0[0] = moved1[0] = near[0]
     for k in near_of(n):
-        moved[k] = send(n, k, near[k])
+        moved0[k] = moved1[k] = send(n, k, near[k])
+    for k in far_of(n):
+        moved1[k] = send(n, k, far1[k - n // 2])
     squares = jnp.zeros((8, C2), jnp.float32)
-    first, squares = attend(n, 0, lengths, moved, weights, squares, [])
+    first, squares = attend(n, 0, lengths, moved0, weights, squares, [])
     early = {k: send(n, k, first[k]) for k in far_of(n)}
-    second, _ = attend(n, 1, lengths, moved, weights, squares, list(first[: n // 2]))
+    second, _ = attend(n, 1, lengths, moved1, weights, squares, list(first[: n // 2]))
     late = [second[0]] + [None] * (n - 1)
     for k in far_of(n) + near_of(n):
         late[k] = send(n, k, second[k])
     mine = tally(n, late)
-    total = mine
+    others = []
     for step in range(1, scenes):
-        total = total + lax.ppermute(mine, "scene", [(i, i ^ step) for i in range(scenes)])
+        others.append(lax.ppermute(mine, "scene", [(i, i ^ step) for i in range(scenes)]))
     encoded = gather(n, frames, [early[k] for k in range(n // 2, n)], late)
-    slot_count = float(scenes * n * frames * CELLS * C2)
-    return (encoded[None], 0.5 * total[0, 0] / slot_count)
+    scale = 0.5 / float(scenes * n * frames * CELLS * C2)
+    loss = finish(scale, mine, others)
+    return (encoded[None], loss.reshape(()))
 
 
 def solution(mesh):

time: 85.4 us -> 76.4 us (0.89)
  waiting for transfers between devices: 23 us -> 13.5 us
  starting transfers between devices: 35.9 us -> 38.5 us
  between operations: 3.21 us -> 1.58 us
    ppermute x18 -> x22, waiting for transfers between devices: 23 us -> 13.5 us  [send(): return lax.ppermute(block, 'frame', [(i, i ^ k) for i in range(n)])]
    ppermute x18 -> x22, starting transfers between devices: 33.9 us -> 36.5 us  [send(): return lax.ppermute(block, 'frame', [(i, i ^ k) for i in range(n)])]
  transfers between devices with their start and end apart: 21 -> 25, of which waited for: 7 -> 7; matrix products, arithmetic and copies ran while one was open for 0% -> 0% of each run, Pallas kernels for 2% -> 11%
where the time goes in v1:
time: 76.4 us; the launch traced here: 76.3 us
  starting transfers between devices  38.5 us (50%)
  Pallas kernels  22.7 us (30%)
  waiting for transfers between devices  13.5 us (18%)
  between operations  1.58 us (2%)
    ppermute x22, starting transfers between devices, send(): return lax.ppermute(block, 'frame', [(i, i ^ k) for i in range(n)])  36.5 us
    ppermute x22, waiting for transfers between devices, send(): return lax.ppermute(block, 'frame', [(i, i ^ k) for i in range(n)])  13.5 us
    pallas_call x2, Pallas kernels, attend(): pl.pallas_call(functools.partial(attend_kernel, n, half), out_shape=[jax....  10.3 us
    pallas_call x1, Pallas kernels, conv_far(): pl.pallas_call(functools.partial(conv_kernel, n), out_shape=[jax.ShapeDty...  8.07 us
    pallas_call x1, Pallas kernels, conv_near(): pl.pallas_call(functools.partial(near_kernel, n), out_shape=[jax.ShapeDty...  2.3 us
    ppermute x3, starting transfers between devices, shards(): lax.ppermute(mine, 'scene', [(i, i ^ step) for i in range(scenes)])  1.91 us
  transfers between devices with their start and end apart: 25, of which 7 were waited for; matrix products, arithmetic and copies ran while one was open for 0% of the time, Pallas kernels for 11%

profile of v1, /device:TPU:0, one launch (start us, length us, event | category | flops | bytes accessed | tf_op | source)
XLA Modules:
  0.0 76.3 jit_solution(13182020872300406507)
XLA Ops:
  1.3 8.1 %shard_map.104 = (bf16[4,32,256]{2,1,0:T(8,128)(2,1)S(1)}, bf16[4,32,256]{2,1,0:T(8,128)(2,1)S(1)}, bf16[4,32,256]{2,1,0:T(8,128)(2,1)S(1)}, bf16[4,32,256]{2,1,...) custom-call(s32[1]{0:T(128)S(6)} %copy.11.meta, ...), custom_call_target="tpu_custom_call" | custom-call | flops 2717908992 | bytes 4000000 | tf_op jit(solution)/shard_map/pallas_call | solution.py:176
  9.3 4.1 %collective-permute-start.3 = (bf16[4,32,256]{2,1,0:T(8,128)(2,1)S(1)}, bf16[4,32,256]{2,1,0:T(8,128)(2,1)S(1)}, u32[]{:S(2)}, u32[]{:S(2)}) collective-permute-start(bf16[4,32,256]{2,1,0:T(8,128)(2,1)S(1)} %get-tuple-element.39), channel_id=1, source_target_pairs={{0,4},{1,5},{2,6},{3,7},{4,0},{5,1},{6,2},{7,3},{8,12},{9,13},{10,... | collective-permute-start | bytes 196616 | tf_op jit(solution)/shard_map/ppermute | solution.py:462
  14.8 2.3 %shard_map.105 = (bf16[4,64,256]{2,1,0:T(8,128)(2,1)S(1)}, bf16[4,64,256]{2,1,0:T(8,128)(2,1)S(1)}, bf16[4,64,256]{2,1,0:T(8,128)(2,1)S(1)}, bf16[4,64,256]{2,1,0:T(8,128)(2,1)S(1)}) custom-call(s32[1]{0:T(128)S(6)} %copy.11.meta, bf16[4,640,1152]{2,1,0:T(8,128)(2,1)S(1)} %get-tuple-element.33.cols2, bf16[3,1152,256]{2,1,0:T(8,128)(2,1)S(1)} %get-tuple-element.34.w2s), custom_call_target="tpu_custom_call" | custom-call | flops 1811939328 | bytes 4000000 | tf_op jit(solution)/shard_map/pallas_call | solution.py:211
  17.4 1.8 %collective-permute-start.1 = (bf16[4,64,256]{2,1,0:T(8,128)(2,1)S(1)}, bf16[4,64,256]{2,1,0:T(8,128)(2,1)S(1)}, u32[]{:S(2)}, u32[]{:S(2)}) collective-permute-start(bf16[4,64,256]{2,1,0:T(8,128)(2,1)S(1)} %get-tuple-element.37), channel_id=1, source_target_pairs={{0,2},{1,3},{2,0},{3,1},{4,6},{5,7},{6,4},{7,5},{8,10},{9,11},{10,... | collective-permute-start | bytes 393224 | tf_op jit(solution)/shard_map/ppermute | solution.py:462
  19.3 1.4 %collective-permute-start.2 = (bf16[4,64,256]{2,1,0:T(8,128)(2,1)S(1)}, bf16[4,64,256]{2,1,0:T(8,128)(2,1)S(1)}, u32[]{:S(2)}, u32[]{:S(2)}) collective-permute-start(bf16[4,64,256]{2,1,0:T(8,128)(2,1)S(1)} %get-tuple-element.38), channel_id=1, source_target_pairs={{0,3},{1,2},{2,1},{3,0},{4,7},{5,6},{6,5},{7,4},{8,11},{9,10},{10,... | collective-permute-start | bytes 393224 | tf_op jit(solution)/shard_map/ppermute | solution.py:462
  20.6 3.6 %collective-permute-start.5 = (bf16[4,32,256]{2,1,0:T(8,128)(2,1)S(1)}, bf16[4,32,256]{2,1,0:T(8,128)(2,1)S(1)}, u32[]{:S(2)}, u32[]{:S(2)}) collective-permute-start(bf16[4,32,256]{2,1,0:T(8,128)(2,1)S(1)} %get-tuple-element.41), channel_id=1, source_target_pairs={{0,6},{1,7},{2,4},{3,5},{4,2},{5,3},{6,0},{7,1},{8,14},{9,15},{10,... | collective-permute-start | bytes 196616 | tf_op jit(solution)/shard_map/ppermute | solution.py:462
  24.3 5.7 %collective-permute-done.5.rest_6_ = bf16[4,32,256]{2,1,0:T(8,128)(2,1)S(1)} collective-permute-done((bf16[4,32,256]{2,1,0:T(8,128)(2,1)S(1)}, bf16[4,32,256]{2,1,0:T(8,128)(2,1)S(1)}, u32[]{:S(2)}, u32[]{:S(2)}) %collective-permute-start.5) | collective-permute-done | bytes 65568 | tf_op jit(solution)/shard_map/ppermute | solution.py:462
  30.0 1.4 %collective-permute-done.6.rest_7_ = bf16[4,32,256]{2,1,0:T(8,128)(2,1)S(1)} collective-permute-done((bf16[4,32,256]{2,1,0:T(8,128)(2,1)S(1)}, bf16[4,32,256]{2,1,0:T(8,128)(2,1)S(1)}, u32[]{:S(2)}, u32[]{:S(2)}) %collective-permute-start.6) | collective-permute-done | bytes 65568 | tf_op jit(solution)/shard_map/ppermute | solution.py:462
  31.4 2.0 %collective-permute-start.12 = (bf16[4,32,256]{2,1,0:T(8,128)(2,1)S(1)}, bf16[4,32,256]{2,1,0:T(8,128)(2,1)S(1)}, u32[]{:S(2)}, u32[]{:S(2)}) collective-permute-start(bf16[4,32,256]{2,1,0:T(8,128)(2,1)S(1)} %get-tuple-element.48), channel_id=1, source_target_pairs={{0,5},{1,4},{2,7},{3,6},{4,1},{5,0},{6,3},{7,2},{8,13},{9,12},{10,... | collective-permute-start | bytes 196616 | tf_op jit(solution)/shard_map/ppermute | solution.py:462
  34.4 3.3 %collective-permute-start.14 = (bf16[4,32,256]{2,1,0:T(8,128)(2,1)S(1)}, bf16[4,32,256]{2,1,0:T(8,128)(2,1)S(1)}, u32[]{:S(2)}, u32[]{:S(2)}) collective-permute-start(bf16[4,32,256]{2,1,0:T(8,128)(2,1)S(1)} %get-tuple-element.50), channel_id=1, source_target_pairs={{0,7},{1,6},{2,5},{3,4},{4,3},{5,2},{6,1},{7,0},{8,15},{9,14},{10,... | collective-permute-start | bytes 196616 | tf_op jit(solution)/shard_map/ppermute | solution.py:462
  37.7 4.7 %shard_map.106 = (bf16[128,256]{1,0:T(8,128)(2,1)S(1)}, bf16[128,256]{1,0:T(8,128)(2,1)S(1)}, bf16[128,256]{1,0:T(8,128)(2,1)S(1)}, bf16[128,256]{1,0:T(8,128)(2...) custom-call(s32[1]{0:T(128)S(6)} %copy.11.meta, ...), custom_call_target="tpu_custom_call" | custom-call | flops 1744830464 | bytes 4000000 | tf_op jit(solution)/shard_map/pallas_call | solution.py:348
  42.5 5.5 %shard_map.107 = (bf16[272,256]{1,0:T(8,128)(2,1)S(1)}, bf16[272,256]{1,0:T(8,128)(2,1)S(1)}, bf16[272,256]{1,0:T(8,128)(2,1)S(1)}, bf16[272,256]{1,0:T(8,128)(2...) custom-call(s32[1]{0:T(128)S(6)} %copy.11.meta, ...), custom_call_target="tpu_custom_call" | custom-call | flops 1744830464 | bytes 4000000 | tf_op jit(solution)/shard_map/pallas_call | solution.py:348
  48.0 1.7 %collective-permute-start.18 = (bf16[144,256]{1,0:T(8,128)(2,1)S(1)}, bf16[144,256]{1,0:T(8,128)(2,1)S(1)}, u32[]{:S(2)}, u32[]{:S(2)}) collective-permute-start(bf16[144,256]{1,0:T(8,128)(2,1)S(1)} %get-tuple-element.60), channel_id=1, source_target_pairs={{0,4},{1,5},{2,6},{3,7},{4,0},{5,1},{6,2},{7,3},{8,12},{9,13},{10,... | collective-permute-start | bytes 221192 | tf_op jit(solution)/shard_map/ppermute | solution.py:462
  49.7 1.8 %collective-permute-start.19 = (bf16[144,256]{1,0:T(8,128)(2,1)S(1)}, bf16[144,256]{1,0:T(8,128)(2,1)S(1)}, u32[]{:S(2)}, u32[]{:S(2)}) collective-permute-start(bf16[144,256]{1,0:T(8,128)(2,1)S(1)} %get-tuple-element.61), channel_id=1, source_target_pairs={{0,5},{1,4},{2,7},{3,6},{4,1},{5,0},{6,3},{7,2},{8,13},{9,12},{10,... | collective-permute-start | bytes 221192 | tf_op jit(solution)/shard_map/ppermute | solution.py:462
  52.7 2.3 %collective-permute-start.17 = (bf16[272,256]{1,0:T(8,128)(2,1)S(1)}, bf16[272,256]{1,0:T(8,128)(2,1)S(1)}, u32[]{:S(2)}, u32[]{:S(2)}) collective-permute-start(bf16[272,256]{1,0:T(8,128)(2,1)S(1)} %get-tuple-element.59), channel_id=1, source_target_pairs={{0,3},{1,2},{2,1},{3,0},{4,7},{5,6},{6,5},{7,4},{8,11},{9,10},{10,... | collective-permute-start | bytes 417800 | tf_op jit(solution)/shard_map/ppermute | solution.py:462
  55.0 1.7 %collective-permute-start.20 = (bf16[144,256]{1,0:T(8,128)(2,1)S(1)}, bf16[144,256]{1,0:T(8,128)(2,1)S(1)}, u32[]{:S(2)}, u32[]{:S(2)}) collective-permute-start(bf16[144,256]{1,0:T(8,128)(2,1)S(1)} %get-tuple-element.62), channel_id=1, source_target_pairs={{0,6},{1,7},{2,4},{3,5},{4,2},{5,3},{6,0},{7,1},{8,14},{9,15},{10,... | collective-permute-start | bytes 221192 | tf_op jit(solution)/shard_map/ppermute | solution.py:462
  57.5 1.7 %collective-permute-start.21 = (bf16[144,256]{1,0:T(8,128)(2,1)S(1)}, bf16[144,256]{1,0:T(8,128)(2,1)S(1)}, u32[]{:S(2)}, u32[]{:S(2)}) collective-permute-start(bf16[144,256]{1,0:T(8,128)(2,1)S(1)} %get-tuple-element.63), channel_id=1, source_target_pairs={{0,7},{1,6},{2,5},{3,4},{4,3},{5,2},{6,1},{7,0},{8,15},{9,14},{10,... | collective-permute-start | bytes 221192 | tf_op jit(solution)/shard_map/ppermute | solution.py:462
  59.2 3.5 %collective-permute-done.20.rest_10_.rest_6_ = bf16[144,256]{1,0:T(8,128)(2,1)S(1)} collective-permute-done((bf16[144,256]{1,0:T(8,128)(2,1)S(1)}, bf16[144,256]{1,0:T(8,128)(2,1)S(1)}, u32[]{:S(2)}, u32[]{:S(2)}) %collective-permute-start.20) | collective-permute-done | bytes 73760 | tf_op jit(solution)/shard_map/ppermute | solution.py:462
  62.7 2.1 %collective-permute-start.10 = (bf16[128,256]{1,0:T(8,128)(2,1)S(1)}, bf16[128,256]{1,0:T(8,128)(2,1)S(1)}, u32[]{:S(2)}, u32[]{:S(2)}) collective-permute-start(bf16[128,256]{1,0:T(8,128)(2,1)S(1)} %get-tuple-element.46), channel_id=1, source_target_pairs={{0,7},{1,6},{2,5},{3,4},{4,3},{5,2},{6,1},{7,0},{8,15},{9,14},{10,... | collective-permute-start | bytes 196616 | tf_op jit(solution)/shard_map/ppermute | solution.py:462
  65.2 1.8 %collective-permute-start.7 = (bf16[128,256]{1,0:T(8,128)(2,1)S(1)}, bf16[128,256]{1,0:T(8,128)(2,1)S(1)}, u32[]{:S(2)}, u32[]{:S(2)}) collective-permute-start(bf16[128,256]{1,0:T(8,128)(2,1)S(1)} %get-tuple-element.43), channel_id=1, source_target_pairs={{0,4},{1,5},{2,6},{3,7},{4,0},{5,1},{6,2},{7,3},{8,12},{9,13},{10,... | collective-permute-start | bytes 196616 | tf_op jit(solution)/shard_map/ppermute | solution.py:462
  67.9 2.5 %collective-permute-start.9 = (bf16[128,256]{1,0:T(8,128)(2,1)S(1)}, bf16[128,256]{1,0:T(8,128)(2,1)S(1)}, u32[]{:S(2)}, u32[]{:S(2)}) collective-permute-start(bf16[128,256]{1,0:T(8,128)(2,1)S(1)} %get-tuple-element.45), channel_id=1, source_target_pairs={{0,6},{1,7},{2,4},{3,5},{4,2},{5,3},{6,0},{7,1},{8,14},{9,15},{10,... | collective-permute-start | bytes 196616 | tf_op jit(solution)/shard_map/ppermute | solution.py:462
  70.5 1.6 %collective-permute-start.23 = (f32[8,128]{1,0:T(8,128)S(1)}, f32[8,128]{1,0:T(8,128)S(1)}, u32[]{:S(2)}, u32[]{:S(2)}) collective-permute-start(f32[8,128]{1,0:T(8,128)S(1)} %shard_map.109.mine), channel_id=1, source_target_pairs={{0,16},{8,24},{16,0},{24,8},{1,17},{9,25},{17,1},{25,9},{2,18},{10... | collective-permute-start | bytes 12296 | tf_op jit(solution)/shard_map/ppermute | solution.py:490
  72.3 1.3 %collective-permute-done.8.rest_1_ = bf16[128,256]{1,0:T(8,128)(2,1)S(1)} collective-permute-done((bf16[128,256]{1,0:T(8,128)(2,1)S(1)}, bf16[128,256]{1,0:T(8,128)(2,1)S(1)}, u32[]{:S(2)}, u32[]{:S(2)}) %collective-permute-start.8) | collective-permute-done | bytes 65568 | tf_op jit(solution)/shard_map/ppermute | solution.py:462
  74.1 1.4 %shard_map.108 = bf16[4,256,512]{2,1,0:T(8,128)(2,1)} custom-call(bf16[128,256]{1,0:T(8,128)(2,1)S(1)} %collective-permute-done.7.rest_0_, bf16[128,256]{1,0:T(8,128)(2,1)S(1)} %collective-permute-done.8.rest_1_, bf16[128,256]{1,0:T(8,128)(2,1)S(1)} %collective-permute-done.9.rest_2_, bf16[128,256]{1,0:T(8,128)(2,1)S(1)} %collective-permute-done.10.rest_3_, ...), custom_call_target="tpu_custom_call" | custom-call | bytes 4000000 | tf_op jit(solution)/shard_map/pallas_call | solution.py:400
  (44 shorter events, 7.3 us)
Async XLA Ops:
  9.3 11.3 %collective-permute-start.3 = (bf16[4,32,256]{2,1,0:T(8,128)(2,1)S(1)}, bf16[4,32,256]{2,1,0:T(8,128)(2,1)S(1)}, u32[]{:S(2)}, u32[]{:S(2)}) collective-permute-start(bf16[4,32,256]{2,1,0:T(8,128)(2,1)S(1)} %get-tuple-element.39), channel_id=1, source_target_pairs={{0,4},{1,5},{2,6},{3,7},{4,0},{5,1},{6,2},{7,3},{8,12},{9,13},{10,... | collective-permute-start | bytes 196616 | tf_op jit(solution)/shard_map/ppermute | solution.py:462
  13.5 10.8 %collective-permute-start.4 = (bf16[4,32,256]{2,1,0:T(8,128)(2,1)S(1)}, bf16[4,32,256]{2,1,0:T(8,128)(2,1)S(1)}, u32[]{:S(2)}, u32[]{:S(2)}) collective-permute-start(bf16[4,32,256]{2,1,0:T(8,128)(2,1)S(1)} %get-tuple-element.40), channel_id=1, source_target_pairs={{0,5},{1,4},{2,7},{3,6},{4,1},{5,0},{6,3},{7,2},{8,13},{9,12},{10,... | collective-permute-start | bytes 196616 | tf_op jit(solution)/shard_map/ppermute | solution.py:462
  17.1 16.4 %collective-permute-start = (bf16[4,64,256]{2,1,0:T(8,128)(2,1)S(1)}, bf16[4,64,256]{2,1,0:T(8,128)(2,1)S(1)}, u32[]{:S(2)}, u32[]{:S(2)}) collective-permute-start(bf16[4,64,256]{2,1,0:T(8,128)(2,1)S(1)} %get-tuple-element.36), channel_id=1, source_target_pairs={{0,1},{1,0},{2,3},{3,2},{4,5},{5,4},{6,7},{7,6},{8,9},{9,8},{10,11... | collective-permute-start | bytes 393224 | tf_op jit(solution)/shard_map/ppermute | solution.py:462
  17.4 16.9 %collective-permute-start.1 = (bf16[4,64,256]{2,1,0:T(8,128)(2,1)S(1)}, bf16[4,64,256]{2,1,0:T(8,128)(2,1)S(1)}, u32[]{:S(2)}, u32[]{:S(2)}) collective-permute-start(bf16[4,64,256]{2,1,0:T(8,128)(2,1)S(1)} %get-tuple-element.37), channel_id=1, source_target_pairs={{0,2},{1,3},{2,0},{3,1},{4,6},{5,7},{6,4},{7,5},{8,10},{9,11},{10,... | collective-permute-start | bytes 393224 | tf_op jit(solution)/shard_map/ppermute | solution.py:462
  19.3 18.4 %collective-permute-start.2 = (bf16[4,64,256]{2,1,0:T(8,128)(2,1)S(1)}, bf16[4,64,256]{2,1,0:T(8,128)(2,1)S(1)}, u32[]{:S(2)}, u32[]{:S(2)}) collective-permute-start(bf16[4,64,256]{2,1,0:T(8,128)(2,1)S(1)} %get-tuple-element.38), channel_id=1, source_target_pairs={{0,3},{1,2},{2,1},{3,0},{4,7},{5,6},{6,5},{7,4},{8,11},{9,10},{10,... | collective-permute-start | bytes 393224 | tf_op jit(solution)/shard_map/ppermute | solution.py:462
  20.6 9.4 %collective-permute-start.5 = (bf16[4,32,256]{2,1,0:T(8,128)(2,1)S(1)}, bf16[4,32,256]{2,1,0:T(8,128)(2,1)S(1)}, u32[]{:S(2)}, u32[]{:S(2)}) collective-permute-start(bf16[4,32,256]{2,1,0:T(8,128)(2,1)S(1)} %get-tuple-element.41), channel_id=1, source_target_pairs={{0,6},{1,7},{2,4},{3,5},{4,2},{5,3},{6,0},{7,1},{8,14},{9,15},{10,... | collective-permute-start | bytes 196616 | tf_op jit(solution)/shard_map/ppermute | solution.py:462
  24.2 7.2 %collective-permute-start.6 = (bf16[4,32,256]{2,1,0:T(8,128)(2,1)S(1)}, bf16[4,32,256]{2,1,0:T(8,128)(2,1)S(1)}, u32[]{:S(2)}, u32[]{:S(2)}) collective-permute-start(bf16[4,32,256]{2,1,0:T(8,128)(2,1)S(1)} %get-tuple-element.42), channel_id=1, source_target_pairs={{0,7},{1,6},{2,5},{3,4},{4,3},{5,2},{6,1},{7,0},{8,15},{9,14},{10,... | collective-permute-start | bytes 196616 | tf_op jit(solution)/shard_map/ppermute | solution.py:462
  30.0 12.4 %collective-permute-start.11 = (bf16[4,32,256]{2,1,0:T(8,128)(2,1)S(1)}, bf16[4,32,256]{2,1,0:T(8,128)(2,1)S(1)}, u32[]{:S(2)}, u32[]{:S(2)}) collective-permute-start(bf16[4,32,256]{2,1,0:T(8,128)(2,1)S(1)} %get-tuple-element.47), channel_id=1, source_target_pairs={{0,4},{1,5},{2,6},{3,7},{4,0},{5,1},{6,2},{7,3},{8,12},{9,13},{10,... | collective-permute-start | bytes 196616 | tf_op jit(solution)/shard_map/ppermute | solution.py:462
  31.4 11.1 %collective-permute-start.12 = (bf16[4,32,256]{2,1,0:T(8,128)(2,1)S(1)}, bf16[4,32,256]{2,1,0:T(8,128)(2,1)S(1)}, u32[]{:S(2)}, u32[]{:S(2)}) collective-permute-start(bf16[4,32,256]{2,1,0:T(8,128)(2,1)S(1)} %get-tuple-element.48), channel_id=1, source_target_pairs={{0,5},{1,4},{2,7},{3,6},{4,1},{5,0},{6,3},{7,2},{8,13},{9,12},{10,... | collective-permute-start | bytes 196616 | tf_op jit(solution)/shard_map/ppermute | solution.py:462
  33.5 9.0 %collective-permute-start.13 = (bf16[4,32,256]{2,1,0:T(8,128)(2,1)S(1)}, bf16[4,32,256]{2,1,0:T(8,128)(2,1)S(1)}, u32[]{:S(2)}, u32[]{:S(2)}) collective-permute-start(bf16[4,32,256]{2,1,0:T(8,128)(2,1)S(1)} %get-tuple-element.49), channel_id=1, source_target_pairs={{0,6},{1,7},{2,4},{3,5},{4,2},{5,3},{6,0},{7,1},{8,14},{9,15},{10,... | collective-permute-start | bytes 196616 | tf_op jit(solution)/shard_map/ppermute | solution.py:462
  34.4 8.1 %collective-permute-start.14 = (bf16[4,32,256]{2,1,0:T(8,128)(2,1)S(1)}, bf16[4,32,256]{2,1,0:T(8,128)(2,1)S(1)}, u32[]{:S(2)}, u32[]{:S(2)}) collective-permute-start(bf16[4,32,256]{2,1,0:T(8,128)(2,1)S(1)} %get-tuple-element.50), channel_id=1, source_target_pairs={{0,7},{1,6},{2,5},{3,4},{4,3},{5,2},{6,1},{7,0},{8,15},{9,14},{10,... | collective-permute-start | bytes 196616 | tf_op jit(solution)/shard_map/ppermute | solution.py:462
  48.0 6.9 %collective-permute-start.18 = (bf16[144,256]{1,0:T(8,128)(2,1)S(1)}, bf16[144,256]{1,0:T(8,128)(2,1)S(1)}, u32[]{:S(2)}, u32[]{:S(2)}) collective-permute-start(bf16[144,256]{1,0:T(8,128)(2,1)S(1)} %get-tuple-element.60), channel_id=1, source_target_pairs={{0,4},{1,5},{2,6},{3,7},{4,0},{5,1},{6,2},{7,3},{8,12},{9,13},{10,... | collective-permute-start | bytes 221192 | tf_op jit(solution)/shard_map/ppermute | solution.py:462
  49.7 7.7 %collective-permute-start.19 = (bf16[144,256]{1,0:T(8,128)(2,1)S(1)}, bf16[144,256]{1,0:T(8,128)(2,1)S(1)}, u32[]{:S(2)}, u32[]{:S(2)}) collective-permute-start(bf16[144,256]{1,0:T(8,128)(2,1)S(1)} %get-tuple-element.61), channel_id=1, source_target_pairs={{0,5},{1,4},{2,7},{3,6},{4,1},{5,0},{6,3},{7,2},{8,13},{9,12},{10,... | collective-permute-start | bytes 221192 | tf_op jit(solution)/shard_map/ppermute | solution.py:462
  51.5 15.4 %collective-permute-start.15 = (bf16[272,256]{1,0:T(8,128)(2,1)S(1)}, bf16[272,256]{1,0:T(8,128)(2,1)S(1)}, u32[]{:S(2)}, u32[]{:S(2)}) collective-permute-start(bf16[272,256]{1,0:T(8,128)(2,1)S(1)} %get-tuple-element.57), channel_id=1, source_target_pairs={{0,1},{1,0},{2,3},{3,2},{4,5},{5,4},{6,7},{7,6},{8,9},{9,8},{10,11... | collective-permute-start | bytes 417800 | tf_op jit(solution)/shard_map/ppermute | solution.py:462
  52.4 15.5 %collective-permute-start.16 = (bf16[272,256]{1,0:T(8,128)(2,1)S(1)}, bf16[272,256]{1,0:T(8,128)(2,1)S(1)}, u32[]{:S(2)}, u32[]{:S(2)}) collective-permute-start(bf16[272,256]{1,0:T(8,128)(2,1)S(1)} %get-tuple-element.58), channel_id=1, source_target_pairs={{0,2},{1,3},{2,0},{3,1},{4,6},{5,7},{6,4},{7,5},{8,10},{9,11},{10,... | collective-permute-start | bytes 417800 | tf_op jit(solution)/shard_map/ppermute | solution.py:462
  52.7 17.7 %collective-permute-start.17 = (bf16[272,256]{1,0:T(8,128)(2,1)S(1)}, bf16[272,256]{1,0:T(8,128)(2,1)S(1)}, u32[]{:S(2)}, u32[]{:S(2)}) collective-permute-start(bf16[272,256]{1,0:T(8,128)(2,1)S(1)} %get-tuple-element.59), channel_id=1, source_target_pairs={{0,3},{1,2},{2,1},{3,0},{4,7},{5,6},{6,5},{7,4},{8,11},{9,10},{10,... | collective-permute-start | bytes 417800 | tf_op jit(solution)/shard_map/ppermute | solution.py:462
  55.0 7.7 %collective-permute-start.20 = (bf16[144,256]{1,0:T(8,128)(2,1)S(1)}, bf16[144,256]{1,0:T(8,128)(2,1)S(1)}, u32[]{:S(2)}, u32[]{:S(2)}) collective-permute-start(bf16[144,256]{1,0:T(8,128)(2,1)S(1)} %get-tuple-element.62), channel_id=1, source_target_pairs={{0,6},{1,7},{2,4},{3,5},{4,2},{5,3},{6,0},{7,1},{8,14},{9,15},{10,... | collective-permute-start | bytes 221192 | tf_op jit(solution)/shard_map/ppermute | solution.py:462
  57.5 7.7 %collective-permute-start.21 = (bf16[144,256]{1,0:T(8,128)(2,1)S(1)}, bf16[144,256]{1,0:T(8,128)(2,1)S(1)}, u32[]{:S(2)}, u32[]{:S(2)}) collective-permute-start(bf16[144,256]{1,0:T(8,128)(2,1)S(1)} %get-tuple-element.63), channel_id=1, source_target_pairs={{0,7},{1,6},{2,5},{3,4},{4,3},{5,2},{6,1},{7,0},{8,15},{9,14},{10,... | collective-permute-start | bytes 221192 | tf_op jit(solution)/shard_map/ppermute | solution.py:462
  62.7 7.8 %collective-permute-start.10 = (bf16[128,256]{1,0:T(8,128)(2,1)S(1)}, bf16[128,256]{1,0:T(8,128)(2,1)S(1)}, u32[]{:S(2)}, u32[]{:S(2)}) collective-permute-start(bf16[128,256]{1,0:T(8,128)(2,1)S(1)} %get-tuple-element.46), channel_id=1, source_target_pairs={{0,7},{1,6},{2,5},{3,4},{4,3},{5,2},{6,1},{7,0},{8,15},{9,14},{10,... | collective-permute-start | bytes 196616 | tf_op jit(solution)/shard_map/ppermute | solution.py:462
  65.2 6.9 %collective-permute-start.7 = (bf16[128,256]{1,0:T(8,128)(2,1)S(1)}, bf16[128,256]{1,0:T(8,128)(2,1)S(1)}, u32[]{:S(2)}, u32[]{:S(2)}) collective-permute-start(bf16[128,256]{1,0:T(8,128)(2,1)S(1)} %get-tuple-element.43), channel_id=1, source_target_pairs={{0,4},{1,5},{2,6},{3,7},{4,0},{5,1},{6,2},{7,3},{8,12},{9,13},{10,... | collective-permute-start | bytes 196616 | tf_op jit(solution)/shard_map/ppermute | solution.py:462
  66.9 6.7 %collective-permute-start.8 = (bf16[128,256]{1,0:T(8,128)(2,1)S(1)}, bf16[128,256]{1,0:T(8,128)(2,1)S(1)}, u32[]{:S(2)}, u32[]{:S(2)}) collective-permute-start(bf16[128,256]{1,0:T(8,128)(2,1)S(1)} %get-tuple-element.44), channel_id=1, source_target_pairs={{0,5},{1,4},{2,7},{3,6},{4,1},{5,0},{6,3},{7,2},{8,13},{9,12},{10,... | collective-permute-start | bytes 196616 | tf_op jit(solution)/shard_map/ppermute | solution.py:462
  67.9 6.1 %collective-permute-start.9 = (bf16[128,256]{1,0:T(8,128)(2,1)S(1)}, bf16[128,256]{1,0:T(8,128)(2,1)S(1)}, u32[]{:S(2)}, u32[]{:S(2)}) collective-permute-start(bf16[128,256]{1,0:T(8,128)(2,1)S(1)} %get-tuple-element.45), channel_id=1, source_target_pairs={{0,6},{1,7},{2,4},{3,5},{4,2},{5,3},{6,0},{7,1},{8,14},{9,15},{10,... | collective-permute-start | bytes 196616 | tf_op jit(solution)/shard_map/ppermute | solution.py:462
  70.4 5.0 %collective-permute-start.22 = (f32[8,128]{1,0:T(8,128)S(1)}, f32[8,128]{1,0:T(8,128)S(1)}, u32[]{:S(2)}, u32[]{:S(2)}) collective-permute-start(f32[8,128]{1,0:T(8,128)S(1)} %shard_map.109.mine), channel_id=1, source_target_pairs={{0,8},{8,0},{16,24},{24,16},{1,9},{9,1},{17,25},{25,17},{2,10},{10... | collective-permute-start | bytes 12296 | tf_op jit(solution)/shard_map/ppermute | solution.py:490
  70.5 4.9 %collective-permute-start.23 = (f32[8,128]{1,0:T(8,128)S(1)}, f32[8,128]{1,0:T(8,128)S(1)}, u32[]{:S(2)}, u32[]{:S(2)}) collective-permute-start(f32[8,128]{1,0:T(8,128)S(1)} %shard_map.109.mine), channel_id=1, source_target_pairs={{0,16},{8,24},{16,0},{24,8},{1,17},{9,25},{17,1},{25,9},{2,18},{10... | collective-permute-start | bytes 12296 | tf_op jit(solution)/shard_map/ppermute | solution.py:490
  (6 other events, 118.1 us)

commit v2 on v1

--- a/solution.py
+++ b/solution.py
@@ -240,14 +240,13 @@
     rest = rest[n + 6 :]
     kept, rest = rest[: n // 2 * half], rest[n // 2 * half :]
     outs, squares = rest[:n], rest[n]
-    seen, resid, q_s, k_s, v_s, a_s, kb, vb, p_s, bias, ones = rest[n + 1 :]
+    seen, resid, q_s, k_s, v_s, a_s, kb, vb, p_s, bias, s_s, ones = rest[n + 1 :]
     me, length = lax.axis_index("frame"), meta[0]
     frames, count = blocks[0].shape[0], blocks[0].shape[1] // HALVES
     first_cell = [half * count if k < n // 2 else 0 for k in range(n)]
     groups = count // 8
     total = n * frames
     rows = total * 4
-    everything = 2 * groups * rows
     f32, bf16 = jnp.float32, jnp.bfloat16
     head_of = lax.broadcasted_iota(jnp.int32, (rows, C2), 1) // HD
 
@@ -264,54 +263,82 @@
 
     at = lax.broadcasted_iota(jnp.int32, (rows, rows), 0)
     to = lax.broadcasted_iota(jnp.int32, (rows, rows), 1)
-    bias[...] = jnp.where((at % 4 == to % 4) & (to // 4 < length), 0.0, NEG)
+    bias[...] = jnp.where((at & 3 == to & 3) & (to >> 2 < length), 0.0, NEG)
     for h in range(HEADS):
         ones[h * rows : (h + 1) * rows, :] = jnp.where(head_of == h, 1.0, 0.0).astype(bf16)
-
-    for g in range(groups):
+    valid = lax.broadcasted_iota(jnp.int32, (rows, C2), 0) >> 2 < length
+    none = jnp.zeros((rows, C2), bf16)
+
+    def project(g):
         summed = jnp.zeros((total * 8, C2), f32)
         for j in range(3):
             mix = seen[g, j : j + total].reshape(total * 8, C2).astype(bf16)
             summed = summed + nt_dot(mix, tw[j])
         res = (seen[g, 1 : total + 1].reshape(total * 8, C2) + silu(summed)).astype(bf16)
         res = res.astype(f32).reshape(total // 2, 2, 8, C2)
-        low, high = swap_cells(res[:, 0], res[:, 1])
-        for part, value in ((0, low), (1, high)):
+        for part, value in enumerate(swap_cells(res[:, 0], res[:, 1])):
             value = value.reshape(rows, C2)
             start = (2 * g + part) * rows
             resid[start : start + rows, :] = value
             mean = jnp.sum(value * value, axis=1, keepdims=True) * (1.0 / C2)
             a_s[start : start + rows, :] = (value * lax.rsqrt(mean + NORM_EPS)).astype(bf16)
-    normed = a_s[...]
-    q_s[...] = (nt_dot(normed, wq[...]).astype(bf16) * HD ** (-0.5)).astype(bf16)
-    k_s[...] = nt_dot(normed, wk[...]).astype(bf16)
-    v_s[...] = nt_dot(normed, wv[...]).astype(bf16)
-
-    none = jnp.zeros((rows, C2), bf16)
-    for b in range(2 * groups):
-        slot = b % 2
+
+    def qkv(start, size):
+        some = slice(start, start + size)
+        q_s[some, :] = (nt_dot(a_s[some, :], wq[...]).astype(bf16) * HD ** (-0.5)).astype(bf16)
+        k_s[some, :] = nt_dot(a_s[some, :], wk[...]).astype(bf16)
+        v_s[some, :] = nt_dot(a_s[some, :], wv[...]).astype(bf16)
+
+    def score(b):
         here = slice(b * rows, (b + 1) * rows)
         keys, values = k_s[here, :], v_s[here, :]
         for h in range(HEADS):
-            kb[slot, h * rows : (h + 1) * rows, :] = jnp.where(head_of == h, keys, none)
-            vb[slot, h * rows : (h + 1) * rows, :] = jnp.where(head_of == h, values, none)
-        s = nt_dot(q_s[here, :], kb[slot])
+            kb[b % 3, h * rows : (h + 1) * rows, :] = jnp.where(head_of == h, keys, none)
+            vb[b % 3, h * rows : (h + 1) * rows, :] = jnp.where(head_of == h, values, none)
+        s_s[b % 3] = nt_dot(q_s[here, :], kb[b % 3])
+
+    def soften(b):
         for h in range(HEADS):
-            mine = s[:, h * rows : (h + 1) * rows] + bias[...]
+            mine = s_s[b % 3, :, h * rows : (h + 1) * rows] + bias[...]
             top = jnp.max(mine, axis=1, keepdims=True)
-            p_s[slot, :, h * rows : (h + 1) * rows] = jnp.exp(mine - top).astype(bf16)
-        weighted = jnp.dot(p_s[slot], vb[slot], preferred_element_type=f32)
-        sums = jnp.dot(p_s[slot], ones[...], preferred_element_type=f32)
+            p_s[b % 3, :, h * rows : (h + 1) * rows] = jnp.exp(mine - top).astype(bf16)
+
+    def weigh(b):
+        here = slice(b * rows, (b + 1) * rows)
+        weighted = jnp.dot(p_s[b % 3], vb[b % 3], preferred_element_type=f32)
+        sums = jnp.dot(p_s[b % 3], ones[...], preferred_element_type=f32)
         a_s[here, :] = (weighted / sums).astype(bf16)
 
-    full = resid[...] + nt_dot(a_s[...], wo[...])
-    t = lax.broadcasted_iota(jnp.int32, (everything, C2), 0) % rows // 4
-    full = jnp.where(t < length, full, 0.0).astype(bf16).astype(f32)
-    squares[...] = before[...] + jnp.sum((full * full).reshape(everything // 8, 8, C2), axis=0)
-    full = full.reshape(groups, 2, total // 2, 8, C2)
+    def emit(g):
+        parts = []
+        add = jnp.zeros((8, C2), f32)
+        for part in range(2):
+            here = slice((2 * g + part) * rows, (2 * g + part + 1) * rows)
+            full = resid[here, :] + nt_dot(a_s[here, :], wo[...])
+            full = jnp.where(valid, full, 0.0).astype(bf16).astype(f32)
+            add = add + jnp.sum((full * full).reshape(rows // 8, 8, C2), axis=0)
+            parts.append(full.reshape(total // 2, 8, C2))
+        squares[...] = squares[...] + add
+        even, odd = swap_cells(*parts)
+        seen[g, 0:total] = jnp.stack([even, odd], axis=1).reshape(total, 8, C2)
+
+    squares[...] = before[...]
+    last = 2 * groups - 1
     for g in range(groups):
-        even, odd = swap_cells(full[g, 0], full[g, 1])
-        seen[g, 0:total] = jnp.stack([even, odd], axis=1).reshape(total, 8, C2)
+        project(g)
+    for b in range(0, 2 * groups, 4):
+        qkv(b * rows, min(4, 2 * groups - b) * rows)
+    score(0)
+    for b in range(2 * groups):
+        if b < last:
+            score(b + 1)
+        soften(b)
+        if b > 0:
+            weigh(b - 1)
+        if b > 1 and b % 2 == 0:
+            emit(b // 2 - 1)
+    weigh(last)
+    emit(groups - 1)
 
     for k in range(n):
         first = (me ^ k) * frames
@@ -358,10 +385,11 @@
             pltpu.VMEM((everything, C2), bf16),
             pltpu.VMEM((everything, C2), bf16),
             pltpu.VMEM((everything, C2), bf16),
-            pltpu.VMEM((2, HEADS * rows, C2), bf16),
-            pltpu.VMEM((2, HEADS * rows, C2), bf16),
-            pltpu.VMEM((2, rows, HEADS * rows), bf16),
+            pltpu.VMEM((3, HEADS * rows, C2), bf16),
+            pltpu.VMEM((3, HEADS * rows, C2), bf16),
+            pltpu.VMEM((3, rows, HEADS * rows), bf16),
             pltpu.VMEM((rows, rows), f32),
+            pltpu.VMEM((3, rows, HEADS * rows), f32),
             pltpu.VMEM((HEADS * rows, C2), bf16),
         ],
         compiler_params=pltpu.CompilerParams(vmem_limit_bytes=VMEM_LIMIT),

time: 76.4 us -> 74.7 us (0.978)
  Pallas kernels: 22.7 us -> 19.5 us
  starting transfers between devices: 38.5 us -> 39.7 us
    pallas_call x2, Pallas kernels: 10.3 us -> 7.08 us  [attend(): pl.pallas_call(functools.partial(attend_kernel, n, half), out_shape=[jax....]
    ppermute x22, starting transfers between devices: 36.5 us -> 37.8 us  [send(): return lax.ppermute(block, 'frame', [(i, i ^ k) for i in range(n)])]
  transfers between devices with their start and end apart: 25 -> 25, of which waited for: 7 -> 9; matrix products, arithmetic and copies ran while one was open for 0% -> 0% of each run, Pallas kernels for 11% -> 9%
where the time goes in v2:
time: 74.7 us; the launch traced here: 74.5 us
  starting transfers between devices  39.7 us (53%)
  Pallas kernels  19.5 us (26%)
  waiting for transfers between devices  13.8 us (18%)
  between operations  1.57 us (2%)
    ppermute x22, starting transfers between devices, send(): return lax.ppermute(block, 'frame', [(i, i ^ k) for i in range(n)])  37.8 us
    ppermute x22, waiting for transfers between devices, send(): return lax.ppermute(block, 'frame', [(i, i ^ k) for i in range(n)])  13.7 us
    pallas_call x1, Pallas kernels, conv_far(): pl.pallas_call(functools.partial(conv_kernel, n), out_shape=[jax.ShapeDty...  8.07 us
    pallas_call x2, Pallas kernels, attend(): pl.pallas_call(functools.partial(attend_kernel, n, half), out_shape=[jax....  7.08 us
    pallas_call x1, Pallas kernels, conv_near(): pl.pallas_call(functools.partial(near_kernel, n), out_shape=[jax.ShapeDty...  2.3 us
    ppermute x3, starting transfers between devices, shards(): lax.ppermute(mine, 'scene', [(i, i ^ step) for i in range(scenes)])  1.91 us
  transfers between devices with their start and end apart: 25, of which 9 were waited for; matrix products, arithmetic and copies ran while one was open for 0% of the time, Pallas kernels for 9%

profile of v2, /device:TPU:0, one launch (start us, length us, event | category | flops | bytes accessed | tf_op | source)
XLA Modules:
  0.0 74.5 jit_solution(10559507257966719182)
XLA Ops:
  1.3 8.1 %shard_map.104 = (bf16[4,32,256]{2,1,0:T(8,128)(2,1)S(1)}, bf16[4,32,256]{2,1,0:T(8,128)(2,1)S(1)}, bf16[4,32,256]{2,1,0:T(8,128)(2,1)S(1)}, bf16[4,32,256]{2,1,...) custom-call(s32[1]{0:T(128)S(6)} %copy.11.meta, ...), custom_call_target="tpu_custom_call" | custom-call | flops 2717908992 | bytes 4000000 | tf_op jit(solution)/shard_map/pallas_call | solution.py:176
  9.3 4.1 %collective-permute-start.3 = (bf16[4,32,256]{2,1,0:T(8,128)(2,1)S(1)}, bf16[4,32,256]{2,1,0:T(8,128)(2,1)S(1)}, u32[]{:S(2)}, u32[]{:S(2)}) collective-permute-start(bf16[4,32,256]{2,1,0:T(8,128)(2,1)S(1)} %get-tuple-element.39), channel_id=1, source_target_pairs={{0,4},{1,5},{2,6},{3,7},{4,0},{5,1},{6,2},{7,3},{8,12},{9,13},{10,... | collective-permute-start | bytes 196616 | tf_op jit(solution)/shard_map/ppermute | solution.py:490
  14.8 2.3 %shard_map.105 = (bf16[4,64,256]{2,1,0:T(8,128)(2,1)S(1)}, bf16[4,64,256]{2,1,0:T(8,128)(2,1)S(1)}, bf16[4,64,256]{2,1,0:T(8,128)(2,1)S(1)}, bf16[4,64,256]{2,1,0:T(8,128)(2,1)S(1)}) custom-call(s32[1]{0:T(128)S(6)} %copy.11.meta, bf16[4,640,1152]{2,1,0:T(8,128)(2,1)S(1)} %get-tuple-element.33.cols2, bf16[3,1152,256]{2,1,0:T(8,128)(2,1)S(1)} %get-tuple-element.34.w2s), custom_call_target="tpu_custom_call" | custom-call | flops 1811939328 | bytes 4000000 | tf_op jit(solution)/shard_map/pallas_call | solution.py:211
  17.4 1.8 %collective-permute-start.1 = (bf16[4,64,256]{2,1,0:T(8,128)(2,1)S(1)}, bf16[4,64,256]{2,1,0:T(8,128)(2,1)S(1)}, u32[]{:S(2)}, u32[]{:S(2)}) collective-permute-start(bf16[4,64,256]{2,1,0:T(8,128)(2,1)S(1)} %get-tuple-element.37), channel_id=1, source_target_pairs={{0,2},{1,3},{2,0},{3,1},{4,6},{5,7},{6,4},{7,5},{8,10},{9,11},{10,... | collective-permute-start | bytes 393224 | tf_op jit(solution)/shard_map/ppermute | solution.py:490
  19.3 1.4 %collective-permute-start.2 = (bf16[4,64,256]{2,1,0:T(8,128)(2,1)S(1)}, bf16[4,64,256]{2,1,0:T(8,128)(2,1)S(1)}, u32[]{:S(2)}, u32[]{:S(2)}) collective-permute-start(bf16[4,64,256]{2,1,0:T(8,128)(2,1)S(1)} %get-tuple-element.38), channel_id=1, source_target_pairs={{0,3},{1,2},{2,1},{3,0},{4,7},{5,6},{6,5},{7,4},{8,11},{9,10},{10,... | collective-permute-start | bytes 393224 | tf_op jit(solution)/shard_map/ppermute | solution.py:490
  20.6 3.6 %collective-permute-start.5 = (bf16[4,32,256]{2,1,0:T(8,128)(2,1)S(1)}, bf16[4,32,256]{2,1,0:T(8,128)(2,1)S(1)}, u32[]{:S(2)}, u32[]{:S(2)}) collective-permute-start(bf16[4,32,256]{2,1,0:T(8,128)(2,1)S(1)} %get-tuple-element.41), channel_id=1, source_target_pairs={{0,6},{1,7},{2,4},{3,5},{4,2},{5,3},{6,0},{7,1},{8,14},{9,15},{10,... | collective-permute-start | bytes 196616 | tf_op jit(solution)/shard_map/ppermute | solution.py:490
  24.3 5.7 %collective-permute-done.5.rest_6_ = bf16[4,32,256]{2,1,0:T(8,128)(2,1)S(1)} collective-permute-done((bf16[4,32,256]{2,1,0:T(8,128)(2,1)S(1)}, bf16[4,32,256]{2,1,0:T(8,128)(2,1)S(1)}, u32[]{:S(2)}, u32[]{:S(2)}) %collective-permute-start.5) | collective-permute-done | bytes 65568 | tf_op jit(solution)/shard_map/ppermute | solution.py:490
  30.0 1.4 %collective-permute-done.6.rest_7_ = bf16[4,32,256]{2,1,0:T(8,128)(2,1)S(1)} collective-permute-done((bf16[4,32,256]{2,1,0:T(8,128)(2,1)S(1)}, bf16[4,32,256]{2,1,0:T(8,128)(2,1)S(1)}, u32[]{:S(2)}, u32[]{:S(2)}) %collective-permute-start.6) | collective-permute-done | bytes 65568 | tf_op jit(solution)/shard_map/ppermute | solution.py:490
  31.4 2.0 %collective-permute-start.12 = (bf16[4,32,256]{2,1,0:T(8,128)(2,1)S(1)}, bf16[4,32,256]{2,1,0:T(8,128)(2,1)S(1)}, u32[]{:S(2)}, u32[]{:S(2)}) collective-permute-start(bf16[4,32,256]{2,1,0:T(8,128)(2,1)S(1)} %get-tuple-element.48), channel_id=1, source_target_pairs={{0,5},{1,4},{2,7},{3,6},{4,1},{5,0},{6,3},{7,2},{8,13},{9,12},{10,... | collective-permute-start | bytes 196616 | tf_op jit(solution)/shard_map/ppermute | solution.py:490
  34.4 3.3 %collective-permute-start.14 = (bf16[4,32,256]{2,1,0:T(8,128)(2,1)S(1)}, bf16[4,32,256]{2,1,0:T(8,128)(2,1)S(1)}, u32[]{:S(2)}, u32[]{:S(2)}) collective-permute-start(bf16[4,32,256]{2,1,0:T(8,128)(2,1)S(1)} %get-tuple-element.50), channel_id=1, source_target_pairs={{0,7},{1,6},{2,5},{3,4},{4,3},{5,2},{6,1},{7,0},{8,15},{9,14},{10,... | collective-permute-start | bytes 196616 | tf_op jit(solution)/shard_map/ppermute | solution.py:490
  37.7 3.2 %shard_map.106 = (bf16[128,256]{1,0:T(8,128)(2,1)S(1)}, bf16[128,256]{1,0:T(8,128)(2,1)S(1)}, bf16[128,256]{1,0:T(8,128)(2,1)S(1)}, bf16[128,256]{1,0:T(8,128)(2...) custom-call(s32[1]{0:T(128)S(6)} %copy.11.meta, ...), custom_call_target="tpu_custom_call" | custom-call | flops 1744830464 | bytes 4000000 | tf_op jit(solution)/shard_map/pallas_call | solution.py:375
  41.4 3.9 %shard_map.107 = (bf16[272,256]{1,0:T(8,128)(2,1)S(1)}, bf16[272,256]{1,0:T(8,128)(2,1)S(1)}, bf16[272,256]{1,0:T(8,128)(2,1)S(1)}, bf16[272,256]{1,0:T(8,128)(2...) custom-call(s32[1]{0:T(128)S(6)} %copy.11.meta, ...), custom_call_target="tpu_custom_call" | custom-call | flops 1744830464 | bytes 4000000 | tf_op jit(solution)/shard_map/pallas_call | solution.py:375
  45.3 2.8 %collective-permute-start.18 = (bf16[144,256]{1,0:T(8,128)(2,1)S(1)}, bf16[144,256]{1,0:T(8,128)(2,1)S(1)}, u32[]{:S(2)}, u32[]{:S(2)}) collective-permute-start(bf16[144,256]{1,0:T(8,128)(2,1)S(1)} %get-tuple-element.60), channel_id=1, source_target_pairs={{0,4},{1,5},{2,6},{3,7},{4,0},{5,1},{6,2},{7,3},{8,12},{9,13},{10,... | collective-permute-start | bytes 221192 | tf_op jit(solution)/shard_map/ppermute | solution.py:490
  48.3 1.4 %collective-permute-start.15 = (bf16[272,256]{1,0:T(8,128)(2,1)S(1)}, bf16[272,256]{1,0:T(8,128)(2,1)S(1)}, u32[]{:S(2)}, u32[]{:S(2)}) collective-permute-start(bf16[272,256]{1,0:T(8,128)(2,1)S(1)} %get-tuple-element.57), channel_id=1, source_target_pairs={{0,1},{1,0},{2,3},{3,2},{4,5},{5,4},{6,7},{7,6},{8,9},{9,8},{10,11... | collective-permute-start | bytes 417800 | tf_op jit(solution)/shard_map/ppermute | solution.py:490
  49.7 1.4 %collective-permute-start.16 = (bf16[272,256]{1,0:T(8,128)(2,1)S(1)}, bf16[272,256]{1,0:T(8,128)(2,1)S(1)}, u32[]{:S(2)}, u32[]{:S(2)}) collective-permute-start(bf16[272,256]{1,0:T(8,128)(2,1)S(1)} %get-tuple-element.58), channel_id=1, source_target_pairs={{0,2},{1,3},{2,0},{3,1},{4,6},{5,7},{6,4},{7,5},{8,10},{9,11},{10,... | collective-permute-start | bytes 417800 | tf_op jit(solution)/shard_map/ppermute | solution.py:490
  51.9 3.2 %collective-permute-start.20 = (bf16[144,256]{1,0:T(8,128)(2,1)S(1)}, bf16[144,256]{1,0:T(8,128)(2,1)S(1)}, u32[]{:S(2)}, u32[]{:S(2)}) collective-permute-start(bf16[144,256]{1,0:T(8,128)(2,1)S(1)} %get-tuple-element.62), channel_id=1, source_target_pairs={{0,6},{1,7},{2,4},{3,5},{4,2},{5,3},{6,0},{7,1},{8,14},{9,15},{10,... | collective-permute-start | bytes 221192 | tf_op jit(solution)/shard_map/ppermute | solution.py:490
  55.9 1.8 %collective-permute-start.21 = (bf16[144,256]{1,0:T(8,128)(2,1)S(1)}, bf16[144,256]{1,0:T(8,128)(2,1)S(1)}, u32[]{:S(2)}, u32[]{:S(2)}) collective-permute-start(bf16[144,256]{1,0:T(8,128)(2,1)S(1)} %get-tuple-element.63), channel_id=1, source_target_pairs={{0,7},{1,6},{2,5},{3,4},{4,3},{5,2},{6,1},{7,0},{8,15},{9,14},{10,... | collective-permute-start | bytes 221192 | tf_op jit(solution)/shard_map/ppermute | solution.py:490
  57.7 3.3 %collective-permute-done.20.rest_10_.rest_6_ = bf16[144,256]{1,0:T(8,128)(2,1)S(1)} collective-permute-done((bf16[144,256]{1,0:T(8,128)(2,1)S(1)}, bf16[144,256]{1,0:T(8,128)(2,1)S(1)}, u32[]{:S(2)}, u32[]{:S(2)}) %collective-permute-start.20) | collective-permute-done | bytes 73760 | tf_op jit(solution)/shard_map/ppermute | solution.py:490
  61.0 2.2 %collective-permute-start.10 = (bf16[128,256]{1,0:T(8,128)(2,1)S(1)}, bf16[128,256]{1,0:T(8,128)(2,1)S(1)}, u32[]{:S(2)}, u32[]{:S(2)}) collective-permute-start(bf16[128,256]{1,0:T(8,128)(2,1)S(1)} %get-tuple-element.46), channel_id=1, source_target_pairs={{0,7},{1,6},{2,5},{3,4},{4,3},{5,2},{6,1},{7,0},{8,15},{9,14},{10,... | collective-permute-start | bytes 196616 | tf_op jit(solution)/shard_map/ppermute | solution.py:490
  63.5 2.2 %collective-permute-start.7 = (bf16[128,256]{1,0:T(8,128)(2,1)S(1)}, bf16[128,256]{1,0:T(8,128)(2,1)S(1)}, u32[]{:S(2)}, u32[]{:S(2)}) collective-permute-start(bf16[128,256]{1,0:T(8,128)(2,1)S(1)} %get-tuple-element.43), channel_id=1, source_target_pairs={{0,4},{1,5},{2,6},{3,7},{4,0},{5,1},{6,2},{7,3},{8,12},{9,13},{10,... | collective-permute-start | bytes 196616 | tf_op jit(solution)/shard_map/ppermute | solution.py:490
  66.3 2.4 %collective-permute-start.9 = (bf16[128,256]{1,0:T(8,128)(2,1)S(1)}, bf16[128,256]{1,0:T(8,128)(2,1)S(1)}, u32[]{:S(2)}, u32[]{:S(2)}) collective-permute-start(bf16[128,256]{1,0:T(8,128)(2,1)S(1)} %get-tuple-element.45), channel_id=1, source_target_pairs={{0,6},{1,7},{2,4},{3,5},{4,2},{5,3},{6,0},{7,1},{8,14},{9,15},{10,... | collective-permute-start | bytes 196616 | tf_op jit(solution)/shard_map/ppermute | solution.py:490
  68.8 1.6 %collective-permute-start.23 = (f32[8,128]{1,0:T(8,128)S(1)}, f32[8,128]{1,0:T(8,128)S(1)}, u32[]{:S(2)}, u32[]{:S(2)}) collective-permute-start(f32[8,128]{1,0:T(8,128)S(1)} %shard_map.109.mine), channel_id=1, source_target_pairs={{0,16},{8,24},{16,0},{24,8},{1,17},{9,25},{17,1},{25,9},{2,18},{10... | collective-permute-start | bytes 12296 | tf_op jit(solution)/shard_map/ppermute | solution.py:518
  70.6 1.4 %collective-permute-done.8.rest_1_ = bf16[128,256]{1,0:T(8,128)(2,1)S(1)} collective-permute-done((bf16[128,256]{1,0:T(8,128)(2,1)S(1)}, bf16[128,256]{1,0:T(8,128)(2,1)S(1)}, u32[]{:S(2)}, u32[]{:S(2)}) %collective-permute-start.8) | collective-permute-done | bytes 65568 | tf_op jit(solution)/shard_map/ppermute | solution.py:490
  72.4 1.4 %shard_map.108 = bf16[4,256,512]{2,1,0:T(8,128)(2,1)} custom-call(bf16[128,256]{1,0:T(8,128)(2,1)S(1)} %collective-permute-done.7.rest_0_, bf16[128,256]{1,0:T(8,128)(2,1)S(1)} %collective-permute-done.8.rest_1_, bf16[128,256]{1,0:T(8,128)(2,1)S(1)} %collective-permute-done.9.rest_2_, bf16[128,256]{1,0:T(8,128)(2,1)S(1)} %collective-permute-done.10.rest_3_, ...), custom_call_target="tpu_custom_call" | custom-call | bytes 4000000 | tf_op jit(solution)/shard_map/pallas_call | solution.py:428
  (44 shorter events, 6.9 us)
Async XLA Ops:
  9.3 11.3 %collective-permute-start.3 = (bf16[4,32,256]{2,1,0:T(8,128)(2,1)S(1)}, bf16[4,32,256]{2,1,0:T(8,128)(2,1)S(1)}, u32[]{:S(2)}, u32[]{:S(2)}) collective-permute-start(bf16[4,32,256]{2,1,0:T(8,128)(2,1)S(1)} %get-tuple-element.39), channel_id=1, source_target_pairs={{0,4},{1,5},{2,6},{3,7},{4,0},{5,1},{6,2},{7,3},{8,12},{9,13},{10,... | collective-permute-start | bytes 196616 | tf_op jit(solution)/shard_map/ppermute | solution.py:490
  13.5 10.8 %collective-permute-start.4 = (bf16[4,32,256]{2,1,0:T(8,128)(2,1)S(1)}, bf16[4,32,256]{2,1,0:T(8,128)(2,1)S(1)}, u32[]{:S(2)}, u32[]{:S(2)}) collective-permute-start(bf16[4,32,256]{2,1,0:T(8,128)(2,1)S(1)} %get-tuple-element.40), channel_id=1, source_target_pairs={{0,5},{1,4},{2,7},{3,6},{4,1},{5,0},{6,3},{7,2},{8,13},{9,12},{10,... | collective-permute-start | bytes 196616 | tf_op jit(solution)/shard_map/ppermute | solution.py:490
  17.1 16.4 %collective-permute-start = (bf16[4,64,256]{2,1,0:T(8,128)(2,1)S(1)}, bf16[4,64,256]{2,1,0:T(8,128)(2,1)S(1)}, u32[]{:S(2)}, u32[]{:S(2)}) collective-permute-start(bf16[4,64,256]{2,1,0:T(8,128)(2,1)S(1)} %get-tuple-element.36), channel_id=1, source_target_pairs={{0,1},{1,0},{2,3},{3,2},{4,5},{5,4},{6,7},{7,6},{8,9},{9,8},{10,11... | collective-permute-start | bytes 393224 | tf_op jit(solution)/shard_map/ppermute | solution.py:490
  17.4 16.9 %collective-permute-start.1 = (bf16[4,64,256]{2,1,0:T(8,128)(2,1)S(1)}, bf16[4,64,256]{2,1,0:T(8,128)(2,1)S(1)}, u32[]{:S(2)}, u32[]{:S(2)}) collective-permute-start(bf16[4,64,256]{2,1,0:T(8,128)(2,1)S(1)} %get-tuple-element.37), channel_id=1, source_target_pairs={{0,2},{1,3},{2,0},{3,1},{4,6},{5,7},{6,4},{7,5},{8,10},{9,11},{10,... | collective-permute-start | bytes 393224 | tf_op jit(solution)/shard_map/ppermute | solution.py:490
  19.3 18.4 %collective-permute-start.2 = (bf16[4,64,256]{2,1,0:T(8,128)(2,1)S(1)}, bf16[4,64,256]{2,1,0:T(8,128)(2,1)S(1)}, u32[]{:S(2)}, u32[]{:S(2)}) collective-permute-start(bf16[4,64,256]{2,1,0:T(8,128)(2,1)S(1)} %get-tuple-element.38), channel_id=1, source_target_pairs={{0,3},{1,2},{2,1},{3,0},{4,7},{5,6},{6,5},{7,4},{8,11},{9,10},{10,... | collective-permute-start | bytes 393224 | tf_op jit(solution)/shard_map/ppermute | solution.py:490
  20.6 9.4 %collective-permute-start.5 = (bf16[4,32,256]{2,1,0:T(8,128)(2,1)S(1)}, bf16[4,32,256]{2,1,0:T(8,128)(2,1)S(1)}, u32[]{:S(2)}, u32[]{:S(2)}) collective-permute-start(bf16[4,32,256]{2,1,0:T(8,128)(2,1)S(1)} %get-tuple-element.41), channel_id=1, source_target_pairs={{0,6},{1,7},{2,4},{3,5},{4,2},{5,3},{6,0},{7,1},{8,14},{9,15},{10,... | collective-permute-start | bytes 196616 | tf_op jit(solution)/shard_map/ppermute | solution.py:490
  24.2 7.2 %collective-permute-start.6 = (bf16[4,32,256]{2,1,0:T(8,128)(2,1)S(1)}, bf16[4,32,256]{2,1,0:T(8,128)(2,1)S(1)}, u32[]{:S(2)}, u32[]{:S(2)}) collective-permute-start(bf16[4,32,256]{2,1,0:T(8,128)(2,1)S(1)} %get-tuple-element.42), channel_id=1, source_target_pairs={{0,7},{1,6},{2,5},{3,4},{4,3},{5,2},{6,1},{7,0},{8,15},{9,14},{10,... | collective-permute-start | bytes 196616 | tf_op jit(solution)/shard_map/ppermute | solution.py:490
  30.0 10.9 %collective-permute-start.11 = (bf16[4,32,256]{2,1,0:T(8,128)(2,1)S(1)}, bf16[4,32,256]{2,1,0:T(8,128)(2,1)S(1)}, u32[]{:S(2)}, u32[]{:S(2)}) collective-permute-start(bf16[4,32,256]{2,1,0:T(8,128)(2,1)S(1)} %get-tuple-element.47), channel_id=1, source_target_pairs={{0,4},{1,5},{2,6},{3,7},{4,0},{5,1},{6,2},{7,3},{8,12},{9,13},{10,... | collective-permute-start | bytes 196616 | tf_op jit(solution)/shard_map/ppermute | solution.py:490
  31.4 9.5 %collective-permute-start.12 = (bf16[4,32,256]{2,1,0:T(8,128)(2,1)S(1)}, bf16[4,32,256]{2,1,0:T(8,128)(2,1)S(1)}, u32[]{:S(2)}, u32[]{:S(2)}) collective-permute-start(bf16[4,32,256]{2,1,0:T(8,128)(2,1)S(1)} %get-tuple-element.48), channel_id=1, source_target_pairs={{0,5},{1,4},{2,7},{3,6},{4,1},{5,0},{6,3},{7,2},{8,13},{9,12},{10,... | collective-permute-start | bytes 196616 | tf_op jit(solution)/shard_map/ppermute | solution.py:490
  33.5 7.4 %collective-permute-start.13 = (bf16[4,32,256]{2,1,0:T(8,128)(2,1)S(1)}, bf16[4,32,256]{2,1,0:T(8,128)(2,1)S(1)}, u32[]{:S(2)}, u32[]{:S(2)}) collective-permute-start(bf16[4,32,256]{2,1,0:T(8,128)(2,1)S(1)} %get-tuple-element.49), channel_id=1, source_target_pairs={{0,6},{1,7},{2,4},{3,5},{4,2},{5,3},{6,0},{7,1},{8,14},{9,15},{10,... | collective-permute-start | bytes 196616 | tf_op jit(solution)/shard_map/ppermute | solution.py:490
  34.4 7.1 %collective-permute-start.14 = (bf16[4,32,256]{2,1,0:T(8,128)(2,1)S(1)}, bf16[4,32,256]{2,1,0:T(8,128)(2,1)S(1)}, u32[]{:S(2)}, u32[]{:S(2)}) collective-permute-start(bf16[4,32,256]{2,1,0:T(8,128)(2,1)S(1)} %get-tuple-element.50), channel_id=1, source_target_pairs={{0,7},{1,6},{2,5},{3,4},{4,3},{5,2},{6,1},{7,0},{8,15},{9,14},{10,... | collective-permute-start | bytes 196616 | tf_op jit(solution)/shard_map/ppermute | solution.py:490
  45.3 6.5 %collective-permute-start.18 = (bf16[144,256]{1,0:T(8,128)(2,1)S(1)}, bf16[144,256]{1,0:T(8,128)(2,1)S(1)}, u32[]{:S(2)}, u32[]{:S(2)}) collective-permute-start(bf16[144,256]{1,0:T(8,128)(2,1)S(1)} %get-tuple-element.60), channel_id=1, source_target_pairs={{0,4},{1,5},{2,6},{3,7},{4,0},{5,1},{6,2},{7,3},{8,12},{9,13},{10,... | collective-permute-start | bytes 221192 | tf_op jit(solution)/shard_map/ppermute | solution.py:490
  48.1 7.7 %collective-permute-start.19 = (bf16[144,256]{1,0:T(8,128)(2,1)S(1)}, bf16[144,256]{1,0:T(8,128)(2,1)S(1)}, u32[]{:S(2)}, u32[]{:S(2)}) collective-permute-start(bf16[144,256]{1,0:T(8,128)(2,1)S(1)} %get-tuple-element.61), channel_id=1, source_target_pairs={{0,5},{1,4},{2,7},{3,6},{4,1},{5,0},{6,3},{7,2},{8,13},{9,12},{10,... | collective-permute-start | bytes 221192 | tf_op jit(solution)/shard_map/ppermute | solution.py:490
  48.3 17.4 %collective-permute-start.15 = (bf16[272,256]{1,0:T(8,128)(2,1)S(1)}, bf16[272,256]{1,0:T(8,128)(2,1)S(1)}, u32[]{:S(2)}, u32[]{:S(2)}) collective-permute-start(bf16[272,256]{1,0:T(8,128)(2,1)S(1)} %get-tuple-element.57), channel_id=1, source_target_pairs={{0,1},{1,0},{2,3},{3,2},{4,5},{5,4},{6,7},{7,6},{8,9},{9,8},{10,11... | collective-permute-start | bytes 417800 | tf_op jit(solution)/shard_map/ppermute | solution.py:490
  49.7 16.6 %collective-permute-start.16 = (bf16[272,256]{1,0:T(8,128)(2,1)S(1)}, bf16[272,256]{1,0:T(8,128)(2,1)S(1)}, u32[]{:S(2)}, u32[]{:S(2)}) collective-permute-start(bf16[272,256]{1,0:T(8,128)(2,1)S(1)} %get-tuple-element.58), channel_id=1, source_target_pairs={{0,2},{1,3},{2,0},{3,1},{4,6},{5,7},{6,4},{7,5},{8,10},{9,11},{10,... | collective-permute-start | bytes 417800 | tf_op jit(solution)/shard_map/ppermute | solution.py:490
  51.1 17.6 %collective-permute-start.17 = (bf16[272,256]{1,0:T(8,128)(2,1)S(1)}, bf16[272,256]{1,0:T(8,128)(2,1)S(1)}, u32[]{:S(2)}, u32[]{:S(2)}) collective-permute-start(bf16[272,256]{1,0:T(8,128)(2,1)S(1)} %get-tuple-element.59), channel_id=1, source_target_pairs={{0,3},{1,2},{2,1},{3,0},{4,7},{5,6},{6,5},{7,4},{8,11},{9,10},{10,... | collective-permute-start | bytes 417800 | tf_op jit(solution)/shard_map/ppermute | solution.py:490
  51.9 9.2 %collective-permute-start.20 = (bf16[144,256]{1,0:T(8,128)(2,1)S(1)}, bf16[144,256]{1,0:T(8,128)(2,1)S(1)}, u32[]{:S(2)}, u32[]{:S(2)}) collective-permute-start(bf16[144,256]{1,0:T(8,128)(2,1)S(1)} %get-tuple-element.62), channel_id=1, source_target_pairs={{0,6},{1,7},{2,4},{3,5},{4,2},{5,3},{6,0},{7,1},{8,14},{9,15},{10,... | collective-permute-start | bytes 221192 | tf_op jit(solution)/shard_map/ppermute | solution.py:490
  55.9 7.6 %collective-permute-start.21 = (bf16[144,256]{1,0:T(8,128)(2,1)S(1)}, bf16[144,256]{1,0:T(8,128)(2,1)S(1)}, u32[]{:S(2)}, u32[]{:S(2)}) collective-permute-start(bf16[144,256]{1,0:T(8,128)(2,1)S(1)} %get-tuple-element.63), channel_id=1, source_target_pairs={{0,7},{1,6},{2,5},{3,4},{4,3},{5,2},{6,1},{7,0},{8,15},{9,14},{10,... | collective-permute-start | bytes 221192 | tf_op jit(solution)/shard_map/ppermute | solution.py:490
  61.0 7.8 %collective-permute-start.10 = (bf16[128,256]{1,0:T(8,128)(2,1)S(1)}, bf16[128,256]{1,0:T(8,128)(2,1)S(1)}, u32[]{:S(2)}, u32[]{:S(2)}) collective-permute-start(bf16[128,256]{1,0:T(8,128)(2,1)S(1)} %get-tuple-element.46), channel_id=1, source_target_pairs={{0,7},{1,6},{2,5},{3,4},{4,3},{5,2},{6,1},{7,0},{8,15},{9,14},{10,... | collective-permute-start | bytes 196616 | tf_op jit(solution)/shard_map/ppermute | solution.py:490
  63.5 6.9 %collective-permute-start.7 = (bf16[128,256]{1,0:T(8,128)(2,1)S(1)}, bf16[128,256]{1,0:T(8,128)(2,1)S(1)}, u32[]{:S(2)}, u32[]{:S(2)}) collective-permute-start(bf16[128,256]{1,0:T(8,128)(2,1)S(1)} %get-tuple-element.43), channel_id=1, source_target_pairs={{0,4},{1,5},{2,6},{3,7},{4,0},{5,1},{6,2},{7,3},{8,12},{9,13},{10,... | collective-permute-start | bytes 196616 | tf_op jit(solution)/shard_map/ppermute | solution.py:490
  65.7 6.3 %collective-permute-start.8 = (bf16[128,256]{1,0:T(8,128)(2,1)S(1)}, bf16[128,256]{1,0:T(8,128)(2,1)S(1)}, u32[]{:S(2)}, u32[]{:S(2)}) collective-permute-start(bf16[128,256]{1,0:T(8,128)(2,1)S(1)} %get-tuple-element.44), channel_id=1, source_target_pairs={{0,5},{1,4},{2,7},{3,6},{4,1},{5,0},{6,3},{7,2},{8,13},{9,12},{10,... | collective-permute-start | bytes 196616 | tf_op jit(solution)/shard_map/ppermute | solution.py:490
  66.3 6.1 %collective-permute-start.9 = (bf16[128,256]{1,0:T(8,128)(2,1)S(1)}, bf16[128,256]{1,0:T(8,128)(2,1)S(1)}, u32[]{:S(2)}, u32[]{:S(2)}) collective-permute-start(bf16[128,256]{1,0:T(8,128)(2,1)S(1)} %get-tuple-element.45), channel_id=1, source_target_pairs={{0,6},{1,7},{2,4},{3,5},{4,2},{5,3},{6,0},{7,1},{8,14},{9,15},{10,... | collective-permute-start | bytes 196616 | tf_op jit(solution)/shard_map/ppermute | solution.py:490
  68.7 5.0 %collective-permute-start.22 = (f32[8,128]{1,0:T(8,128)S(1)}, f32[8,128]{1,0:T(8,128)S(1)}, u32[]{:S(2)}, u32[]{:S(2)}) collective-permute-start(f32[8,128]{1,0:T(8,128)S(1)} %shard_map.109.mine), channel_id=1, source_target_pairs={{0,8},{8,0},{16,24},{24,16},{1,9},{9,1},{17,25},{25,17},{2,10},{10... | collective-permute-start | bytes 12296 | tf_op jit(solution)/shard_map/ppermute | solution.py:518
  68.8 4.9 %collective-permute-start.23 = (f32[8,128]{1,0:T(8,128)S(1)}, f32[8,128]{1,0:T(8,128)S(1)}, u32[]{:S(2)}, u32[]{:S(2)}) collective-permute-start(f32[8,128]{1,0:T(8,128)S(1)} %shard_map.109.mine), channel_id=1, source_target_pairs={{0,16},{8,24},{16,0},{24,8},{1,17},{9,25},{17,1},{25,9},{2,18},{10... | collective-permute-start | bytes 12296 | tf_op jit(solution)/shard_map/ppermute | solution.py:518
  (6 other events, 118.1 us)

commit v3 on v2

--- a/solution.py
+++ b/solution.py
@@ -65,21 +65,20 @@
     count = CELLS // n
     side = me // (n // 2)
     first = (1 - side if far else side) * half
-    acc = jnp.zeros((frames * half, C2), jnp.float32)
-    for kh in range(3):
-        start = pl.multiple_of(first + kh * ROW, ROW)
-        lhs = cols2[:, pl.ds(start, half), :].reshape(frames * half, 9 * C1)
-        acc = acc + jnp.dot(lhs, w2s[kh], preferred_element_type=jnp.float32)
-    y2[...] = acc
     for f in range(frames):
+        acc = jnp.zeros((half, C2), jnp.float32)
+        for kh in range(3):
+            start = pl.multiple_of(first + kh * ROW, ROW)
+            acc = acc + jnp.dot(
+                cols2[f, pl.ds(start, half), :], w2s[kh], preferred_element_type=jnp.float32
+            )
         valid = jnp.where(me * frames + f < meta[0], 1.0, 0.0)
-        for r in range(0, half, ROW):
-            rows = slice(f * half + r, f * half + r + ROW)
-            y2[rows, :] = silu(y2[rows, :]) * valid
+        y2[f * half : (f + 1) * half, :] = (silu(acc) * valid).astype(jnp.bfloat16)
+    for f in range(frames):
         for k in range(n // 2):
             at = (me ^ (k + n // 2 if far else k)) % (n // 2)
             start = pl.multiple_of(f * half + at * count, count)
-            block = y2[pl.ds(start, count), :].astype(jnp.bfloat16)
+            block = y2[pl.ds(start, count), :]
             if far:
                 outs[k][f] = block[: count // 2]
                 outs[k + n // 2][f] = block[count // 2 :]
@@ -122,8 +121,7 @@
             w1s[rows, 0:C1] = tap1(hp + 1, kw)
             w1s[rows, C1 : 2 * C1] = tap1(0, kw) if hp == 1 else zero
 
-    for f in range(frames):
-        copies[1 + f].wait()
+    def columns(f):
         for h in range(ROWS):
             upper = occ[f, :, h * 256 : h * 256 + 128]
             lower = occ[f, :, h * 256 + 128 : h * 256 + 256]
@@ -136,22 +134,36 @@
                 for i, part in enumerate(parts):
                     lanes = slice(kz * 384 + i * 128, kz * 384 + i * 128 + 128)
                     cols1[f, (h + 1) * ROW : (h + 2) * ROW, lanes] = part.reshape(ROW, 128).astype(bf16)
-        y1[f] = jnp.dot(cols1[f], w1s[...], preferred_element_type=jnp.float32)
-        if f == 0:
-            copies[1 + frames].wait()
-            copies[2 + frames].wait()
-        pieces = w2.shape[1] // 128
-        for j in range(f * pieces // frames, (f + 1) * pieces // frames):
-            for half in range(2):
-                t2[half, j * 128 : j * 128 + 128, :] = (
-                    w2[half * 128 : half * 128 + 128, j * 128 : j * 128 + 128].astype(jnp.float32).T
-                )
+
+    def widen(f):
         for h in range(ROWS):
             v = (
                 y1[f, (h + 1) * ROW : (h + 2) * ROW, 0:C1]
                 + y1[f, h * ROW : (h + 1) * ROW, C1 : 2 * C1]
             )
             store_cols(cols2, f, h, silu(v).reshape(8, ZD, C1))
+
+    pieces = w2.shape[1] // 128
+    parts = max(frames - 1, 1)
+    middle = (ROWS + 1) // 2 * ROW
+    for copy in copies[1 : 1 + frames]:
+        copy.wait()
+    columns(0)
+    for f in range(frames):
+        part = f - (frames - parts)
+        if part == 0:
+            copies[1 + frames].wait()
+            copies[2 + frames].wait()
+        for rows in (slice(0, middle), slice(middle, (ROWS + 1) * ROW)):
+            y1[f, rows, :] = jnp.dot(cols1[f, rows, :], w1s[...], preferred_element_type=jnp.float32)
+        if f + 1 < frames:
+            columns(f + 1)
+        for j in range(max(part, 0) * pieces // parts, max(part + 1, 0) * pieces // parts):
+            for half in range(2):
+                t2[half, j * 128 : j * 128 + 128, :] = (
+                    w2[half * 128 : half * 128 + 128, j * 128 : j * 128 + 128].astype(jnp.float32).T
+                )
+        widen(f)
     for kh in range(3):
         for kw in range(3):
             for kz in range(3):
@@ -191,7 +203,7 @@
             pltpu.VMEM((1152, 2 * C1), bf16),
             pltpu.VMEM((frames, (ROWS + 1) * ROW, 1152), bf16),
             pltpu.VMEM((frames, (ROWS + 1) * ROW, 2 * C1), f32),
-            pltpu.VMEM((frames * CELLS // 2, C2), f32),
+            pltpu.VMEM((frames * CELLS // 2, C2), bf16),
             pltpu.SemaphoreType.DMA((3 + frames,)),
         ],
         compiler_params=pltpu.CompilerParams(vmem_limit_bytes=40 << 20),
@@ -213,7 +225,7 @@
         out_shape=[jax.ShapeDtypeStruct((frames, count, C2), jnp.bfloat16)] * (n // 2),
         in_specs=[pl.BlockSpec(memory_space=pltpu.SMEM), vmem, vmem],
         out_specs=[vmem] * (n // 2),
-        scratch_shapes=[pltpu.VMEM((frames * CELLS // 2, C2), jnp.float32)],
+        scratch_shapes=[pltpu.VMEM((frames * CELLS // 2, C2), jnp.bfloat16)],
         compiler_params=pltpu.CompilerParams(vmem_limit_bytes=VMEM_LIMIT),
         cost_estimate=pl.CostEstimate(
             flops=2 * frames * CELLS * C2 * C1 * 27 // 2,

time: 74.7 us -> 73 us (0.977)
  Pallas kernels: 19.5 us -> 17.7 us
    pallas_call x1, Pallas kernels: 8.07 us -> 6.3 us  [conv_far(): pl.pallas_call(functools.partial(conv_kernel, n), out_shape=[jax.ShapeDty...]
where the time goes in v3:
time: 73 us; the launch traced here: 72.8 us
  starting transfers between devices  39.7 us (54%)
  Pallas kernels  17.7 us (24%)
  waiting for transfers between devices  13.8 us (19%)
  between operations  1.57 us (2%)
    ppermute x22, starting transfers between devices, send(): return lax.ppermute(block, 'frame', [(i, i ^ k) for i in range(n)])  37.8 us
    ppermute x22, waiting for transfers between devices, send(): return lax.ppermute(block, 'frame', [(i, i ^ k) for i in range(n)])  13.8 us
    pallas_call x2, Pallas kernels, attend(): pl.pallas_call(functools.partial(attend_kernel, n, half), out_shape=[jax....  7.08 us
    pallas_call x1, Pallas kernels, conv_far(): pl.pallas_call(functools.partial(conv_kernel, n), out_shape=[jax.ShapeDty...  6.3 us
    pallas_call x1, Pallas kernels, conv_near(): pl.pallas_call(functools.partial(near_kernel, n), out_shape=[jax.ShapeDty...  2.29 us
    ppermute x3, starting transfers between devices, shards(): lax.ppermute(mine, 'scene', [(i, i ^ step) for i in range(scenes)])  1.91 us
  transfers between devices with their start and end apart: 25, of which 9 were waited for; matrix products, arithmetic and copies ran while one was open for 0% of the time, Pallas kernels for 9%

profile of v3, /device:TPU:0, one launch (start us, length us, event | category | flops | bytes accessed | tf_op | source)
XLA Modules:
  0.0 72.8 jit_solution(11680035199471853855)
XLA Ops:
  1.3 6.3 %shard_map.104 = (bf16[4,32,256]{2,1,0:T(8,128)(2,1)S(1)}, bf16[4,32,256]{2,1,0:T(8,128)(2,1)S(1)}, bf16[4,32,256]{2,1,0:T(8,128)(2,1)S(1)}, bf16[4,32,256]{2,1,...) custom-call(s32[1]{0:T(128)S(6)} %copy.11.meta, ...), custom_call_target="tpu_custom_call" | custom-call | flops 2717908992 | bytes 4000000 | tf_op jit(solution)/shard_map/pallas_call | solution.py:188
  7.6 4.1 %collective-permute-start.3 = (bf16[4,32,256]{2,1,0:T(8,128)(2,1)S(1)}, bf16[4,32,256]{2,1,0:T(8,128)(2,1)S(1)}, u32[]{:S(2)}, u32[]{:S(2)}) collective-permute-start(bf16[4,32,256]{2,1,0:T(8,128)(2,1)S(1)} %get-tuple-element.39), channel_id=1, source_target_pairs={{0,4},{1,5},{2,6},{3,7},{4,0},{5,1},{6,2},{7,3},{8,12},{9,13},{10,... | collective-permute-start | bytes 196616 | tf_op jit(solution)/shard_map/ppermute | solution.py:502
  13.0 2.3 %shard_map.105 = (bf16[4,64,256]{2,1,0:T(8,128)(2,1)S(1)}, bf16[4,64,256]{2,1,0:T(8,128)(2,1)S(1)}, bf16[4,64,256]{2,1,0:T(8,128)(2,1)S(1)}, bf16[4,64,256]{2,1,0:T(8,128)(2,1)S(1)}) custom-call(s32[1]{0:T(128)S(6)} %copy.11.meta, bf16[4,640,1152]{2,1,0:T(8,128)(2,1)S(1)} %get-tuple-element.33.cols2, bf16[3,1152,256]{2,1,0:T(8,128)(2,1)S(1)} %get-tuple-element.34.w2s), custom_call_target="tpu_custom_call" | custom-call | flops 1811939328 | bytes 4000000 | tf_op jit(solution)/shard_map/pallas_call | solution.py:223
  15.6 1.8 %collective-permute-start.1 = (bf16[4,64,256]{2,1,0:T(8,128)(2,1)S(1)}, bf16[4,64,256]{2,1,0:T(8,128)(2,1)S(1)}, u32[]{:S(2)}, u32[]{:S(2)}) collective-permute-start(bf16[4,64,256]{2,1,0:T(8,128)(2,1)S(1)} %get-tuple-element.37), channel_id=1, source_target_pairs={{0,2},{1,3},{2,0},{3,1},{4,6},{5,7},{6,4},{7,5},{8,10},{9,11},{10,... | collective-permute-start | bytes 393224 | tf_op jit(solution)/shard_map/ppermute | solution.py:502
  17.5 1.4 %collective-permute-start.2 = (bf16[4,64,256]{2,1,0:T(8,128)(2,1)S(1)}, bf16[4,64,256]{2,1,0:T(8,128)(2,1)S(1)}, u32[]{:S(2)}, u32[]{:S(2)}) collective-permute-start(bf16[4,64,256]{2,1,0:T(8,128)(2,1)S(1)} %get-tuple-element.38), channel_id=1, source_target_pairs={{0,3},{1,2},{2,1},{3,0},{4,7},{5,6},{6,5},{7,4},{8,11},{9,10},{10,... | collective-permute-start | bytes 393224 | tf_op jit(solution)/shard_map/ppermute | solution.py:502
  18.9 3.6 %collective-permute-start.5 = (bf16[4,32,256]{2,1,0:T(8,128)(2,1)S(1)}, bf16[4,32,256]{2,1,0:T(8,128)(2,1)S(1)}, u32[]{:S(2)}, u32[]{:S(2)}) collective-permute-start(bf16[4,32,256]{2,1,0:T(8,128)(2,1)S(1)} %get-tuple-element.41), channel_id=1, source_target_pairs={{0,6},{1,7},{2,4},{3,5},{4,2},{5,3},{6,0},{7,1},{8,14},{9,15},{10,... | collective-permute-start | bytes 196616 | tf_op jit(solution)/shard_map/ppermute | solution.py:502
  22.6 5.7 %collective-permute-done.5.rest_6_ = bf16[4,32,256]{2,1,0:T(8,128)(2,1)S(1)} collective-permute-done((bf16[4,32,256]{2,1,0:T(8,128)(2,1)S(1)}, bf16[4,32,256]{2,1,0:T(8,128)(2,1)S(1)}, u32[]{:S(2)}, u32[]{:S(2)}) %collective-permute-start.5) | collective-permute-done | bytes 65568 | tf_op jit(solution)/shard_map/ppermute | solution.py:502
  28.3 1.4 %collective-permute-done.6.rest_7_ = bf16[4,32,256]{2,1,0:T(8,128)(2,1)S(1)} collective-permute-done((bf16[4,32,256]{2,1,0:T(8,128)(2,1)S(1)}, bf16[4,32,256]{2,1,0:T(8,128)(2,1)S(1)}, u32[]{:S(2)}, u32[]{:S(2)}) %collective-permute-start.6) | collective-permute-done | bytes 65568 | tf_op jit(solution)/shard_map/ppermute | solution.py:502
  29.7 2.0 %collective-permute-start.12 = (bf16[4,32,256]{2,1,0:T(8,128)(2,1)S(1)}, bf16[4,32,256]{2,1,0:T(8,128)(2,1)S(1)}, u32[]{:S(2)}, u32[]{:S(2)}) collective-permute-start(bf16[4,32,256]{2,1,0:T(8,128)(2,1)S(1)} %get-tuple-element.48), channel_id=1, source_target_pairs={{0,5},{1,4},{2,7},{3,6},{4,1},{5,0},{6,3},{7,2},{8,13},{9,12},{10,... | collective-permute-start | bytes 196616 | tf_op jit(solution)/shard_map/ppermute | solution.py:502
  32.6 3.3 %collective-permute-start.14 = (bf16[4,32,256]{2,1,0:T(8,128)(2,1)S(1)}, bf16[4,32,256]{2,1,0:T(8,128)(2,1)S(1)}, u32[]{:S(2)}, u32[]{:S(2)}) collective-permute-start(bf16[4,32,256]{2,1,0:T(8,128)(2,1)S(1)} %get-tuple-element.50), channel_id=1, source_target_pairs={{0,7},{1,6},{2,5},{3,4},{4,3},{5,2},{6,1},{7,0},{8,15},{9,14},{10,... | collective-permute-start | bytes 196616 | tf_op jit(solution)/shard_map/ppermute | solution.py:502
  36.0 3.2 %shard_map.106 = (bf16[128,256]{1,0:T(8,128)(2,1)S(1)}, bf16[128,256]{1,0:T(8,128)(2,1)S(1)}, bf16[128,256]{1,0:T(8,128)(2,1)S(1)}, bf16[128,256]{1,0:T(8,128)(2...) custom-call(s32[1]{0:T(128)S(6)} %copy.11.meta, ...), custom_call_target="tpu_custom_call" | custom-call | flops 1744830464 | bytes 4000000 | tf_op jit(solution)/shard_map/pallas_call | solution.py:387
  39.6 3.9 %shard_map.107 = (bf16[272,256]{1,0:T(8,128)(2,1)S(1)}, bf16[272,256]{1,0:T(8,128)(2,1)S(1)}, bf16[272,256]{1,0:T(8,128)(2,1)S(1)}, bf16[272,256]{1,0:T(8,128)(2...) custom-call(s32[1]{0:T(128)S(6)} %copy.11.meta, ...), custom_call_target="tpu_custom_call" | custom-call | flops 1744830464 | bytes 4000000 | tf_op jit(solution)/shard_map/pallas_call | solution.py:387
  43.6 2.8 %collective-permute-start.18 = (bf16[144,256]{1,0:T(8,128)(2,1)S(1)}, bf16[144,256]{1,0:T(8,128)(2,1)S(1)}, u32[]{:S(2)}, u32[]{:S(2)}) collective-permute-start(bf16[144,256]{1,0:T(8,128)(2,1)S(1)} %get-tuple-element.60), channel_id=1, source_target_pairs={{0,4},{1,5},{2,6},{3,7},{4,0},{5,1},{6,2},{7,3},{8,12},{9,13},{10,... | collective-permute-start | bytes 221192 | tf_op jit(solution)/shard_map/ppermute | solution.py:502
  46.5 1.4 %collective-permute-start.15 = (bf16[272,256]{1,0:T(8,128)(2,1)S(1)}, bf16[272,256]{1,0:T(8,128)(2,1)S(1)}, u32[]{:S(2)}, u32[]{:S(2)}) collective-permute-start(bf16[272,256]{1,0:T(8,128)(2,1)S(1)} %get-tuple-element.57), channel_id=1, source_target_pairs={{0,1},{1,0},{2,3},{3,2},{4,5},{5,4},{6,7},{7,6},{8,9},{9,8},{10,11... | collective-permute-start | bytes 417800 | tf_op jit(solution)/shard_map/ppermute | solution.py:502
  48.0 1.4 %collective-permute-start.16 = (bf16[272,256]{1,0:T(8,128)(2,1)S(1)}, bf16[272,256]{1,0:T(8,128)(2,1)S(1)}, u32[]{:S(2)}, u32[]{:S(2)}) collective-permute-start(bf16[272,256]{1,0:T(8,128)(2,1)S(1)} %get-tuple-element.58), channel_id=1, source_target_pairs={{0,2},{1,3},{2,0},{3,1},{4,6},{5,7},{6,4},{7,5},{8,10},{9,11},{10,... | collective-permute-start | bytes 417800 | tf_op jit(solution)/shard_map/ppermute | solution.py:502
  50.1 3.2 %collective-permute-start.20 = (bf16[144,256]{1,0:T(8,128)(2,1)S(1)}, bf16[144,256]{1,0:T(8,128)(2,1)S(1)}, u32[]{:S(2)}, u32[]{:S(2)}) collective-permute-start(bf16[144,256]{1,0:T(8,128)(2,1)S(1)} %get-tuple-element.62), channel_id=1, source_target_pairs={{0,6},{1,7},{2,4},{3,5},{4,2},{5,3},{6,0},{7,1},{8,14},{9,15},{10,... | collective-permute-start | bytes 221192 | tf_op jit(solution)/shard_map/ppermute | solution.py:502
  54.1 1.9 %collective-permute-start.21 = (bf16[144,256]{1,0:T(8,128)(2,1)S(1)}, bf16[144,256]{1,0:T(8,128)(2,1)S(1)}, u32[]{:S(2)}, u32[]{:S(2)}) collective-permute-start(bf16[144,256]{1,0:T(8,128)(2,1)S(1)} %get-tuple-element.63), channel_id=1, source_target_pairs={{0,7},{1,6},{2,5},{3,4},{4,3},{5,2},{6,1},{7,0},{8,15},{9,14},{10,... | collective-permute-start | bytes 221192 | tf_op jit(solution)/shard_map/ppermute | solution.py:502
  56.0 3.3 %collective-permute-done.20.rest_10_.rest_6_ = bf16[144,256]{1,0:T(8,128)(2,1)S(1)} collective-permute-done((bf16[144,256]{1,0:T(8,128)(2,1)S(1)}, bf16[144,256]{1,0:T(8,128)(2,1)S(1)}, u32[]{:S(2)}, u32[]{:S(2)}) %collective-permute-start.20) | collective-permute-done | bytes 73760 | tf_op jit(solution)/shard_map/ppermute | solution.py:502
  59.3 2.1 %collective-permute-start.10 = (bf16[128,256]{1,0:T(8,128)(2,1)S(1)}, bf16[128,256]{1,0:T(8,128)(2,1)S(1)}, u32[]{:S(2)}, u32[]{:S(2)}) collective-permute-start(bf16[128,256]{1,0:T(8,128)(2,1)S(1)} %get-tuple-element.46), channel_id=1, source_target_pairs={{0,7},{1,6},{2,5},{3,4},{4,3},{5,2},{6,1},{7,0},{8,15},{9,14},{10,... | collective-permute-start | bytes 196616 | tf_op jit(solution)/shard_map/ppermute | solution.py:502
  61.7 2.2 %collective-permute-start.7 = (bf16[128,256]{1,0:T(8,128)(2,1)S(1)}, bf16[128,256]{1,0:T(8,128)(2,1)S(1)}, u32[]{:S(2)}, u32[]{:S(2)}) collective-permute-start(bf16[128,256]{1,0:T(8,128)(2,1)S(1)} %get-tuple-element.43), channel_id=1, source_target_pairs={{0,4},{1,5},{2,6},{3,7},{4,0},{5,1},{6,2},{7,3},{8,12},{9,13},{10,... | collective-permute-start | bytes 196616 | tf_op jit(solution)/shard_map/ppermute | solution.py:502
  64.5 2.4 %collective-permute-start.9 = (bf16[128,256]{1,0:T(8,128)(2,1)S(1)}, bf16[128,256]{1,0:T(8,128)(2,1)S(1)}, u32[]{:S(2)}, u32[]{:S(2)}) collective-permute-start(bf16[128,256]{1,0:T(8,128)(2,1)S(1)} %get-tuple-element.45), channel_id=1, source_target_pairs={{0,6},{1,7},{2,4},{3,5},{4,2},{5,3},{6,0},{7,1},{8,14},{9,15},{10,... | collective-permute-start | bytes 196616 | tf_op jit(solution)/shard_map/ppermute | solution.py:502
  67.1 1.6 %collective-permute-start.23 = (f32[8,128]{1,0:T(8,128)S(1)}, f32[8,128]{1,0:T(8,128)S(1)}, u32[]{:S(2)}, u32[]{:S(2)}) collective-permute-start(f32[8,128]{1,0:T(8,128)S(1)} %shard_map.109.mine), channel_id=1, source_target_pairs={{0,16},{8,24},{16,0},{24,8},{1,17},{9,25},{17,1},{25,9},{2,18},{10... | collective-permute-start | bytes 12296 | tf_op jit(solution)/shard_map/ppermute | solution.py:530
  68.9 1.4 %collective-permute-done.8.rest_1_ = bf16[128,256]{1,0:T(8,128)(2,1)S(1)} collective-permute-done((bf16[128,256]{1,0:T(8,128)(2,1)S(1)}, bf16[128,256]{1,0:T(8,128)(2,1)S(1)}, u32[]{:S(2)}, u32[]{:S(2)}) %collective-permute-start.8) | collective-permute-done | bytes 65568 | tf_op jit(solution)/shard_map/ppermute | solution.py:502
  70.6 1.4 %shard_map.108 = bf16[4,256,512]{2,1,0:T(8,128)(2,1)} custom-call(bf16[128,256]{1,0:T(8,128)(2,1)S(1)} %collective-permute-done.7.rest_0_, bf16[128,256]{1,0:T(8,128)(2,1)S(1)} %collective-permute-done.8.rest_1_, bf16[128,256]{1,0:T(8,128)(2,1)S(1)} %collective-permute-done.9.rest_2_, bf16[128,256]{1,0:T(8,128)(2,1)S(1)} %collective-permute-done.10.rest_3_, ...), custom_call_target="tpu_custom_call" | custom-call | bytes 4000000 | tf_op jit(solution)/shard_map/pallas_call | solution.py:440
  (44 shorter events, 7.0 us)
Async XLA Ops:
  7.6 11.3 %collective-permute-start.3 = (bf16[4,32,256]{2,1,0:T(8,128)(2,1)S(1)}, bf16[4,32,256]{2,1,0:T(8,128)(2,1)S(1)}, u32[]{:S(2)}, u32[]{:S(2)}) collective-permute-start(bf16[4,32,256]{2,1,0:T(8,128)(2,1)S(1)} %get-tuple-element.39), channel_id=1, source_target_pairs={{0,4},{1,5},{2,6},{3,7},{4,0},{5,1},{6,2},{7,3},{8,12},{9,13},{10,... | collective-permute-start | bytes 196616 | tf_op jit(solution)/shard_map/ppermute | solution.py:502
  11.7 10.7 %collective-permute-start.4 = (bf16[4,32,256]{2,1,0:T(8,128)(2,1)S(1)}, bf16[4,32,256]{2,1,0:T(8,128)(2,1)S(1)}, u32[]{:S(2)}, u32[]{:S(2)}) collective-permute-start(bf16[4,32,256]{2,1,0:T(8,128)(2,1)S(1)} %get-tuple-element.40), channel_id=1, source_target_pairs={{0,5},{1,4},{2,7},{3,6},{4,1},{5,0},{6,3},{7,2},{8,13},{9,12},{10,... | collective-permute-start | bytes 196616 | tf_op jit(solution)/shard_map/ppermute | solution.py:502
  15.3 16.4 %collective-permute-start = (bf16[4,64,256]{2,1,0:T(8,128)(2,1)S(1)}, bf16[4,64,256]{2,1,0:T(8,128)(2,1)S(1)}, u32[]{:S(2)}, u32[]{:S(2)}) collective-permute-start(bf16[4,64,256]{2,1,0:T(8,128)(2,1)S(1)} %get-tuple-element.36), channel_id=1, source_target_pairs={{0,1},{1,0},{2,3},{3,2},{4,5},{5,4},{6,7},{7,6},{8,9},{9,8},{10,11... | collective-permute-start | bytes 393224 | tf_op jit(solution)/shard_map/ppermute | solution.py:502
  15.6 16.9 %collective-permute-start.1 = (bf16[4,64,256]{2,1,0:T(8,128)(2,1)S(1)}, bf16[4,64,256]{2,1,0:T(8,128)(2,1)S(1)}, u32[]{:S(2)}, u32[]{:S(2)}) collective-permute-start(bf16[4,64,256]{2,1,0:T(8,128)(2,1)S(1)} %get-tuple-element.37), channel_id=1, source_target_pairs={{0,2},{1,3},{2,0},{3,1},{4,6},{5,7},{6,4},{7,5},{8,10},{9,11},{10,... | collective-permute-start | bytes 393224 | tf_op jit(solution)/shard_map/ppermute | solution.py:502
  17.5 18.4 %collective-permute-start.2 = (bf16[4,64,256]{2,1,0:T(8,128)(2,1)S(1)}, bf16[4,64,256]{2,1,0:T(8,128)(2,1)S(1)}, u32[]{:S(2)}, u32[]{:S(2)}) collective-permute-start(bf16[4,64,256]{2,1,0:T(8,128)(2,1)S(1)} %get-tuple-element.38), channel_id=1, source_target_pairs={{0,3},{1,2},{2,1},{3,0},{4,7},{5,6},{6,5},{7,4},{8,11},{9,10},{10,... | collective-permute-start | bytes 393224 | tf_op jit(solution)/shard_map/ppermute | solution.py:502
  18.9 9.4 %collective-permute-start.5 = (bf16[4,32,256]{2,1,0:T(8,128)(2,1)S(1)}, bf16[4,32,256]{2,1,0:T(8,128)(2,1)S(1)}, u32[]{:S(2)}, u32[]{:S(2)}) collective-permute-start(bf16[4,32,256]{2,1,0:T(8,128)(2,1)S(1)} %get-tuple-element.41), channel_id=1, source_target_pairs={{0,6},{1,7},{2,4},{3,5},{4,2},{5,3},{6,0},{7,1},{8,14},{9,15},{10,... | collective-permute-start | bytes 196616 | tf_op jit(solution)/shard_map/ppermute | solution.py:502
  22.5 7.2 %collective-permute-start.6 = (bf16[4,32,256]{2,1,0:T(8,128)(2,1)S(1)}, bf16[4,32,256]{2,1,0:T(8,128)(2,1)S(1)}, u32[]{:S(2)}, u32[]{:S(2)}) collective-permute-start(bf16[4,32,256]{2,1,0:T(8,128)(2,1)S(1)} %get-tuple-element.42), channel_id=1, source_target_pairs={{0,7},{1,6},{2,5},{3,4},{4,3},{5,2},{6,1},{7,0},{8,15},{9,14},{10,... | collective-permute-start | bytes 196616 | tf_op jit(solution)/shard_map/ppermute | solution.py:502
  28.3 10.9 %collective-permute-start.11 = (bf16[4,32,256]{2,1,0:T(8,128)(2,1)S(1)}, bf16[4,32,256]{2,1,0:T(8,128)(2,1)S(1)}, u32[]{:S(2)}, u32[]{:S(2)}) collective-permute-start(bf16[4,32,256]{2,1,0:T(8,128)(2,1)S(1)} %get-tuple-element.47), channel_id=1, source_target_pairs={{0,4},{1,5},{2,6},{3,7},{4,0},{5,1},{6,2},{7,3},{8,12},{9,13},{10,... | collective-permute-start | bytes 196616 | tf_op jit(solution)/shard_map/ppermute | solution.py:502
  29.7 9.5 %collective-permute-start.12 = (bf16[4,32,256]{2,1,0:T(8,128)(2,1)S(1)}, bf16[4,32,256]{2,1,0:T(8,128)(2,1)S(1)}, u32[]{:S(2)}, u32[]{:S(2)}) collective-permute-start(bf16[4,32,256]{2,1,0:T(8,128)(2,1)S(1)} %get-tuple-element.48), channel_id=1, source_target_pairs={{0,5},{1,4},{2,7},{3,6},{4,1},{5,0},{6,3},{7,2},{8,13},{9,12},{10,... | collective-permute-start | bytes 196616 | tf_op jit(solution)/shard_map/ppermute | solution.py:502
  31.7 7.5 %collective-permute-start.13 = (bf16[4,32,256]{2,1,0:T(8,128)(2,1)S(1)}, bf16[4,32,256]{2,1,0:T(8,128)(2,1)S(1)}, u32[]{:S(2)}, u32[]{:S(2)}) collective-permute-start(bf16[4,32,256]{2,1,0:T(8,128)(2,1)S(1)} %get-tuple-element.49), channel_id=1, source_target_pairs={{0,6},{1,7},{2,4},{3,5},{4,2},{5,3},{6,0},{7,1},{8,14},{9,15},{10,... | collective-permute-start | bytes 196616 | tf_op jit(solution)/shard_map/ppermute | solution.py:502
  32.6 7.1 %collective-permute-start.14 = (bf16[4,32,256]{2,1,0:T(8,128)(2,1)S(1)}, bf16[4,32,256]{2,1,0:T(8,128)(2,1)S(1)}, u32[]{:S(2)}, u32[]{:S(2)}) collective-permute-start(bf16[4,32,256]{2,1,0:T(8,128)(2,1)S(1)} %get-tuple-element.50), channel_id=1, source_target_pairs={{0,7},{1,6},{2,5},{3,4},{4,3},{5,2},{6,1},{7,0},{8,15},{9,14},{10,... | collective-permute-start | bytes 196616 | tf_op jit(solution)/shard_map/ppermute | solution.py:502
  43.6 6.5 %collective-permute-start.18 = (bf16[144,256]{1,0:T(8,128)(2,1)S(1)}, bf16[144,256]{1,0:T(8,128)(2,1)S(1)}, u32[]{:S(2)}, u32[]{:S(2)}) collective-permute-start(bf16[144,256]{1,0:T(8,128)(2,1)S(1)} %get-tuple-element.60), channel_id=1, source_target_pairs={{0,4},{1,5},{2,6},{3,7},{4,0},{5,1},{6,2},{7,3},{8,12},{9,13},{10,... | collective-permute-start | bytes 221192 | tf_op jit(solution)/shard_map/ppermute | solution.py:502
  46.4 7.7 %collective-permute-start.19 = (bf16[144,256]{1,0:T(8,128)(2,1)S(1)}, bf16[144,256]{1,0:T(8,128)(2,1)S(1)}, u32[]{:S(2)}, u32[]{:S(2)}) collective-permute-start(bf16[144,256]{1,0:T(8,128)(2,1)S(1)} %get-tuple-element.61), channel_id=1, source_target_pairs={{0,5},{1,4},{2,7},{3,6},{4,1},{5,0},{6,3},{7,2},{8,13},{9,12},{10,... | collective-permute-start | bytes 221192 | tf_op jit(solution)/shard_map/ppermute | solution.py:502
  46.5 17.4 %collective-permute-start.15 = (bf16[272,256]{1,0:T(8,128)(2,1)S(1)}, bf16[272,256]{1,0:T(8,128)(2,1)S(1)}, u32[]{:S(2)}, u32[]{:S(2)}) collective-permute-start(bf16[272,256]{1,0:T(8,128)(2,1)S(1)} %get-tuple-element.57), channel_id=1, source_target_pairs={{0,1},{1,0},{2,3},{3,2},{4,5},{5,4},{6,7},{7,6},{8,9},{9,8},{10,11... | collective-permute-start | bytes 417800 | tf_op jit(solution)/shard_map/ppermute | solution.py:502
  48.0 16.6 %collective-permute-start.16 = (bf16[272,256]{1,0:T(8,128)(2,1)S(1)}, bf16[272,256]{1,0:T(8,128)(2,1)S(1)}, u32[]{:S(2)}, u32[]{:S(2)}) collective-permute-start(bf16[272,256]{1,0:T(8,128)(2,1)S(1)} %get-tuple-element.58), channel_id=1, source_target_pairs={{0,2},{1,3},{2,0},{3,1},{4,6},{5,7},{6,4},{7,5},{8,10},{9,11},{10,... | collective-permute-start | bytes 417800 | tf_op jit(solution)/shard_map/ppermute | solution.py:502
  49.4 17.6 %collective-permute-start.17 = (bf16[272,256]{1,0:T(8,128)(2,1)S(1)}, bf16[272,256]{1,0:T(8,128)(2,1)S(1)}, u32[]{:S(2)}, u32[]{:S(2)}) collective-permute-start(bf16[272,256]{1,0:T(8,128)(2,1)S(1)} %get-tuple-element.59), channel_id=1, source_target_pairs={{0,3},{1,2},{2,1},{3,0},{4,7},{5,6},{6,5},{7,4},{8,11},{9,10},{10,... | collective-permute-start | bytes 417800 | tf_op jit(solution)/shard_map/ppermute | solution.py:502
  50.1 9.2 %collective-permute-start.20 = (bf16[144,256]{1,0:T(8,128)(2,1)S(1)}, bf16[144,256]{1,0:T(8,128)(2,1)S(1)}, u32[]{:S(2)}, u32[]{:S(2)}) collective-permute-start(bf16[144,256]{1,0:T(8,128)(2,1)S(1)} %get-tuple-element.62), channel_id=1, source_target_pairs={{0,6},{1,7},{2,4},{3,5},{4,2},{5,3},{6,0},{7,1},{8,14},{9,15},{10,... | collective-permute-start | bytes 221192 | tf_op jit(solution)/shard_map/ppermute | solution.py:502
  54.1 7.6 %collective-permute-start.21 = (bf16[144,256]{1,0:T(8,128)(2,1)S(1)}, bf16[144,256]{1,0:T(8,128)(2,1)S(1)}, u32[]{:S(2)}, u32[]{:S(2)}) collective-permute-start(bf16[144,256]{1,0:T(8,128)(2,1)S(1)} %get-tuple-element.63), channel_id=1, source_target_pairs={{0,7},{1,6},{2,5},{3,4},{4,3},{5,2},{6,1},{7,0},{8,15},{9,14},{10,... | collective-permute-start | bytes 221192 | tf_op jit(solution)/shard_map/ppermute | solution.py:502
  59.3 7.8 %collective-permute-start.10 = (bf16[128,256]{1,0:T(8,128)(2,1)S(1)}, bf16[128,256]{1,0:T(8,128)(2,1)S(1)}, u32[]{:S(2)}, u32[]{:S(2)}) collective-permute-start(bf16[128,256]{1,0:T(8,128)(2,1)S(1)} %get-tuple-element.46), channel_id=1, source_target_pairs={{0,7},{1,6},{2,5},{3,4},{4,3},{5,2},{6,1},{7,0},{8,15},{9,14},{10,... | collective-permute-start | bytes 196616 | tf_op jit(solution)/shard_map/ppermute | solution.py:502
  61.7 6.9 %collective-permute-start.7 = (bf16[128,256]{1,0:T(8,128)(2,1)S(1)}, bf16[128,256]{1,0:T(8,128)(2,1)S(1)}, u32[]{:S(2)}, u32[]{:S(2)}) collective-permute-start(bf16[128,256]{1,0:T(8,128)(2,1)S(1)} %get-tuple-element.43), channel_id=1, source_target_pairs={{0,4},{1,5},{2,6},{3,7},{4,0},{5,1},{6,2},{7,3},{8,12},{9,13},{10,... | collective-permute-start | bytes 196616 | tf_op jit(solution)/shard_map/ppermute | solution.py:502
  64.0 6.3 %collective-permute-start.8 = (bf16[128,256]{1,0:T(8,128)(2,1)S(1)}, bf16[128,256]{1,0:T(8,128)(2,1)S(1)}, u32[]{:S(2)}, u32[]{:S(2)}) collective-permute-start(bf16[128,256]{1,0:T(8,128)(2,1)S(1)} %get-tuple-element.44), channel_id=1, source_target_pairs={{0,5},{1,4},{2,7},{3,6},{4,1},{5,0},{6,3},{7,2},{8,13},{9,12},{10,... | collective-permute-start | bytes 196616 | tf_op jit(solution)/shard_map/ppermute | solution.py:502
  64.5 6.1 %collective-permute-start.9 = (bf16[128,256]{1,0:T(8,128)(2,1)S(1)}, bf16[128,256]{1,0:T(8,128)(2,1)S(1)}, u32[]{:S(2)}, u32[]{:S(2)}) collective-permute-start(bf16[128,256]{1,0:T(8,128)(2,1)S(1)} %get-tuple-element.45), channel_id=1, source_target_pairs={{0,6},{1,7},{2,4},{3,5},{4,2},{5,3},{6,0},{7,1},{8,14},{9,15},{10,... | collective-permute-start | bytes 196616 | tf_op jit(solution)/shard_map/ppermute | solution.py:502
  67.0 5.0 %collective-permute-start.22 = (f32[8,128]{1,0:T(8,128)S(1)}, f32[8,128]{1,0:T(8,128)S(1)}, u32[]{:S(2)}, u32[]{:S(2)}) collective-permute-start(f32[8,128]{1,0:T(8,128)S(1)} %shard_map.109.mine), channel_id=1, source_target_pairs={{0,8},{8,0},{16,24},{24,16},{1,9},{9,1},{17,25},{25,17},{2,10},{10... | collective-permute-start | bytes 12296 | tf_op jit(solution)/shard_map/ppermute | solution.py:530
  67.1 4.9 %collective-permute-start.23 = (f32[8,128]{1,0:T(8,128)S(1)}, f32[8,128]{1,0:T(8,128)S(1)}, u32[]{:S(2)}, u32[]{:S(2)}) collective-permute-start(f32[8,128]{1,0:T(8,128)S(1)} %shard_map.109.mine), channel_id=1, source_target_pairs={{0,16},{8,24},{16,0},{24,8},{1,17},{9,25},{17,1},{25,9},{2,18},{10... | collective-permute-start | bytes 12296 | tf_op jit(solution)/shard_map/ppermute | solution.py:530
  (6 other events, 118.1 us)

commit v4 on v3

--- a/solution.py
+++ b/solution.py
@@ -21,7 +21,7 @@
 HALVES = 2
 NORM_EPS = 1e-06
 NEG = -1e30
-TAIL = 16
+TAIL = 8
 VMEM_LIMIT = 24 << 20
 
 
@@ -387,10 +387,11 @@
     res = pl.pallas_call(
         functools.partial(attend_kernel, n, half),
         out_shape=[jax.ShapeDtypeStruct((size, C2), bf16) for size in sizes]
-        + [jax.ShapeDtypeStruct((8, C2), f32)],
+        + [jax.ShapeDtypeStruct((8, C2), f32)] * (1 - half),
         in_specs=[pl.BlockSpec(memory_space=pltpu.SMEM)] + [vmem] * (n + 6 + len(kept)),
-        out_specs=[vmem] * (n + 1),
-        scratch_shapes=[
+        out_specs=[vmem] * (n + 1 - half),
+        scratch_shapes=[pltpu.VMEM((8, C2), f32)] * half
+        + [
             pltpu.VMEM((groups, total + 2, 8, C2), f32),
             pltpu.VMEM((everything, C2), f32),
             pltpu.VMEM((everything, C2), bf16),
@@ -411,7 +412,7 @@
             transcendentals=everything * HEADS * rows,
         ),
     )(meta, *blocks, *weights, before, *kept)
-    return res[:n], res[n]
+    return res[:n], res[-1]
 
 
 def gather_kernel(n, *rest):

time: 73 us -> 72.2 us (0.989)
  starting transfers between devices: 39.7 us -> 38.8 us
    ppermute x22, starting transfers between devices: 37.8 us -> 36.9 us  [send(): return lax.ppermute(block, 'frame', [(i, i ^ k) for i in range(n)])]
  transfers between devices with their start and end apart: 25 -> 25, of which waited for: 9 -> 8; matrix products, arithmetic and copies ran while one was open for 0% -> 0% of each run, Pallas kernels for 9% -> 10%
where the time goes in v4:
time: 72.2 us; the launch traced here: 72 us
  starting transfers between devices  38.8 us (54%)
  Pallas kernels  17.2 us (24%)
  waiting for transfers between devices  14.4 us (20%)
  between operations  1.57 us (2%)
    ppermute x22, starting transfers between devices, send(): return lax.ppermute(block, 'frame', [(i, i ^ k) for i in range(n)])  36.9 us
    ppermute x22, waiting for transfers between devices, send(): return lax.ppermute(block, 'frame', [(i, i ^ k) for i in range(n)])  14.4 us
    pallas_call x2, Pallas kernels, attend(): pl.pallas_call(functools.partial(attend_kernel, n, half), out_shape=[jax....  6.59 us
    pallas_call x1, Pallas kernels, conv_far(): pl.pallas_call(functools.partial(conv_kernel, n), out_shape=[jax.ShapeDty...  6.3 us
    pallas_call x1, Pallas kernels, conv_near(): pl.pallas_call(functools.partial(near_kernel, n), out_shape=[jax.ShapeDty...  2.29 us
    ppermute x3, starting transfers between devices, shards(): lax.ppermute(mine, 'scene', [(i, i ^ step) for i in range(scenes)])  1.91 us
  transfers between devices with their start and end apart: 25, of which 8 were waited for; matrix products, arithmetic and copies ran while one was open for 0% of the time, Pallas kernels for 10%

profile of v4, /device:TPU:0, one launch (start us, length us, event | category | flops | bytes accessed | tf_op | source)
XLA Modules:
  0.0 72.0 jit_solution(1903752539865398468)
XLA Ops:
  1.3 6.3 %shard_map.104 = (bf16[4,32,256]{2,1,0:T(8,128)(2,1)S(1)}, bf16[4,32,256]{2,1,0:T(8,128)(2,1)S(1)}, bf16[4,32,256]{2,1,0:T(8,128)(2,1)S(1)}, bf16[4,32,256]{2,1,...) custom-call(s32[1]{0:T(128)S(6)} %copy.11.meta, ...), custom_call_target="tpu_custom_call" | custom-call | flops 2717908992 | bytes 4000000 | tf_op jit(solution)/shard_map/pallas_call | solution.py:188
  7.6 4.1 %collective-permute-start.3 = (bf16[4,32,256]{2,1,0:T(8,128)(2,1)S(1)}, bf16[4,32,256]{2,1,0:T(8,128)(2,1)S(1)}, u32[]{:S(2)}, u32[]{:S(2)}) collective-permute-start(bf16[4,32,256]{2,1,0:T(8,128)(2,1)S(1)} %get-tuple-element.39), channel_id=1, source_target_pairs={{0,4},{1,5},{2,6},{3,7},{4,0},{5,1},{6,2},{7,3},{8,12},{9,13},{10,... | collective-permute-start | bytes 196616 | tf_op jit(solution)/shard_map/ppermute | solution.py:503
  13.0 2.3 %shard_map.105 = (bf16[4,64,256]{2,1,0:T(8,128)(2,1)S(1)}, bf16[4,64,256]{2,1,0:T(8,128)(2,1)S(1)}, bf16[4,64,256]{2,1,0:T(8,128)(2,1)S(1)}, bf16[4,64,256]{2,1,0:T(8,128)(2,1)S(1)}) custom-call(s32[1]{0:T(128)S(6)} %copy.11.meta, bf16[4,640,1152]{2,1,0:T(8,128)(2,1)S(1)} %get-tuple-element.33.cols2, bf16[3,1152,256]{2,1,0:T(8,128)(2,1)S(1)} %get-tuple-element.34.w2s), custom_call_target="tpu_custom_call" | custom-call | flops 1811939328 | bytes 4000000 | tf_op jit(solution)/shard_map/pallas_call | solution.py:223
  15.6 1.8 %collective-permute-start.1 = (bf16[4,64,256]{2,1,0:T(8,128)(2,1)S(1)}, bf16[4,64,256]{2,1,0:T(8,128)(2,1)S(1)}, u32[]{:S(2)}, u32[]{:S(2)}) collective-permute-start(bf16[4,64,256]{2,1,0:T(8,128)(2,1)S(1)} %get-tuple-element.37), channel_id=1, source_target_pairs={{0,2},{1,3},{2,0},{3,1},{4,6},{5,7},{6,4},{7,5},{8,10},{9,11},{10,... | collective-permute-start | bytes 393224 | tf_op jit(solution)/shard_map/ppermute | solution.py:503
  17.5 1.4 %collective-permute-start.2 = (bf16[4,64,256]{2,1,0:T(8,128)(2,1)S(1)}, bf16[4,64,256]{2,1,0:T(8,128)(2,1)S(1)}, u32[]{:S(2)}, u32[]{:S(2)}) collective-permute-start(bf16[4,64,256]{2,1,0:T(8,128)(2,1)S(1)} %get-tuple-element.38), channel_id=1, source_target_pairs={{0,3},{1,2},{2,1},{3,0},{4,7},{5,6},{6,5},{7,4},{8,11},{9,10},{10,... | collective-permute-start | bytes 393224 | tf_op jit(solution)/shard_map/ppermute | solution.py:503
  18.9 3.6 %collective-permute-start.5 = (bf16[4,32,256]{2,1,0:T(8,128)(2,1)S(1)}, bf16[4,32,256]{2,1,0:T(8,128)(2,1)S(1)}, u32[]{:S(2)}, u32[]{:S(2)}) collective-permute-start(bf16[4,32,256]{2,1,0:T(8,128)(2,1)S(1)} %get-tuple-element.41), channel_id=1, source_target_pairs={{0,6},{1,7},{2,4},{3,5},{4,2},{5,3},{6,0},{7,1},{8,14},{9,15},{10,... | collective-permute-start | bytes 196616 | tf_op jit(solution)/shard_map/ppermute | solution.py:503
  22.6 5.7 %collective-permute-done.5.rest_6_ = bf16[4,32,256]{2,1,0:T(8,128)(2,1)S(1)} collective-permute-done((bf16[4,32,256]{2,1,0:T(8,128)(2,1)S(1)}, bf16[4,32,256]{2,1,0:T(8,128)(2,1)S(1)}, u32[]{:S(2)}, u32[]{:S(2)}) %collective-permute-start.5) | collective-permute-done | bytes 65568 | tf_op jit(solution)/shard_map/ppermute | solution.py:503
  28.3 1.4 %collective-permute-done.6.rest_7_ = bf16[4,32,256]{2,1,0:T(8,128)(2,1)S(1)} collective-permute-done((bf16[4,32,256]{2,1,0:T(8,128)(2,1)S(1)}, bf16[4,32,256]{2,1,0:T(8,128)(2,1)S(1)}, u32[]{:S(2)}, u32[]{:S(2)}) %collective-permute-start.6) | collective-permute-done | bytes 65568 | tf_op jit(solution)/shard_map/ppermute | solution.py:503
  29.7 2.0 %collective-permute-start.12 = (bf16[4,32,256]{2,1,0:T(8,128)(2,1)S(1)}, bf16[4,32,256]{2,1,0:T(8,128)(2,1)S(1)}, u32[]{:S(2)}, u32[]{:S(2)}) collective-permute-start(bf16[4,32,256]{2,1,0:T(8,128)(2,1)S(1)} %get-tuple-element.48), channel_id=1, source_target_pairs={{0,5},{1,4},{2,7},{3,6},{4,1},{5,0},{6,3},{7,2},{8,13},{9,12},{10,... | collective-permute-start | bytes 196616 | tf_op jit(solution)/shard_map/ppermute | solution.py:503
  32.6 3.3 %collective-permute-start.14 = (bf16[4,32,256]{2,1,0:T(8,128)(2,1)S(1)}, bf16[4,32,256]{2,1,0:T(8,128)(2,1)S(1)}, u32[]{:S(2)}, u32[]{:S(2)}) collective-permute-start(bf16[4,32,256]{2,1,0:T(8,128)(2,1)S(1)} %get-tuple-element.50), channel_id=1, source_target_pairs={{0,7},{1,6},{2,5},{3,4},{4,3},{5,2},{6,1},{7,0},{8,15},{9,14},{10,... | collective-permute-start | bytes 196616 | tf_op jit(solution)/shard_map/ppermute | solution.py:503
  36.0 3.2 %shard_map.106 = (bf16[128,256]{1,0:T(8,128)(2,1)S(1)}, bf16[128,256]{1,0:T(8,128)(2,1)S(1)}, bf16[128,256]{1,0:T(8,128)(2,1)S(1)}, bf16[128,256]{1,0:T(8,128)(2...) custom-call(s32[1]{0:T(128)S(6)} %copy.11.meta, ...), custom_call_target="tpu_custom_call" | custom-call | flops 1744830464 | bytes 4000000 | tf_op jit(solution)/shard_map/pallas_call | solution.py:387
  39.6 3.4 %shard_map.107 = (bf16[264,256]{1,0:T(8,128)(2,1)S(1)}, bf16[264,256]{1,0:T(8,128)(2,1)S(1)}, bf16[264,256]{1,0:T(8,128)(2,1)S(1)}, bf16[264,256]{1,0:T(8,128)(2...) custom-call(s32[1]{0:T(128)S(6)} %copy.11.meta, ...), custom_call_target="tpu_custom_call" | custom-call | flops 1744830464 | bytes 4000000 | tf_op jit(solution)/shard_map/pallas_call | solution.py:387
  43.1 2.9 %collective-permute-start.18 = (bf16[136,256]{1,0:T(8,128)(2,1)S(1)}, bf16[136,256]{1,0:T(8,128)(2,1)S(1)}, u32[]{:S(2)}, u32[]{:S(2)}) collective-permute-start(bf16[136,256]{1,0:T(8,128)(2,1)S(1)} %get-tuple-element.60), channel_id=1, source_target_pairs={{0,4},{1,5},{2,6},{3,7},{4,0},{5,1},{6,2},{7,3},{8,12},{9,13},{10,... | collective-permute-start | bytes 208904 | tf_op jit(solution)/shard_map/ppermute | solution.py:503
  46.1 1.4 %collective-permute-start.15 = (bf16[264,256]{1,0:T(8,128)(2,1)S(1)}, bf16[264,256]{1,0:T(8,128)(2,1)S(1)}, u32[]{:S(2)}, u32[]{:S(2)}) collective-permute-start(bf16[264,256]{1,0:T(8,128)(2,1)S(1)} %get-tuple-element.57), channel_id=1, source_target_pairs={{0,1},{1,0},{2,3},{3,2},{4,5},{5,4},{6,7},{7,6},{8,9},{9,8},{10,11... | collective-permute-start | bytes 405512 | tf_op jit(solution)/shard_map/ppermute | solution.py:503
  47.5 1.4 %collective-permute-start.16 = (bf16[264,256]{1,0:T(8,128)(2,1)S(1)}, bf16[264,256]{1,0:T(8,128)(2,1)S(1)}, u32[]{:S(2)}, u32[]{:S(2)}) collective-permute-start(bf16[264,256]{1,0:T(8,128)(2,1)S(1)} %get-tuple-element.58), channel_id=1, source_target_pairs={{0,2},{1,3},{2,0},{3,1},{4,6},{5,7},{6,4},{7,5},{8,10},{9,11},{10,... | collective-permute-start | bytes 405512 | tf_op jit(solution)/shard_map/ppermute | solution.py:503
  49.6 3.3 %collective-permute-start.20 = (bf16[136,256]{1,0:T(8,128)(2,1)S(1)}, bf16[136,256]{1,0:T(8,128)(2,1)S(1)}, u32[]{:S(2)}, u32[]{:S(2)}) collective-permute-start(bf16[136,256]{1,0:T(8,128)(2,1)S(1)} %get-tuple-element.62), channel_id=1, source_target_pairs={{0,6},{1,7},{2,4},{3,5},{4,2},{5,3},{6,0},{7,1},{8,14},{9,15},{10,... | collective-permute-start | bytes 208904 | tf_op jit(solution)/shard_map/ppermute | solution.py:503
  53.7 1.4 %collective-permute-start.21 = (bf16[136,256]{1,0:T(8,128)(2,1)S(1)}, bf16[136,256]{1,0:T(8,128)(2,1)S(1)}, u32[]{:S(2)}, u32[]{:S(2)}) collective-permute-start(bf16[136,256]{1,0:T(8,128)(2,1)S(1)} %get-tuple-element.63), channel_id=1, source_target_pairs={{0,7},{1,6},{2,5},{3,4},{4,3},{5,2},{6,1},{7,0},{8,15},{9,14},{10,... | collective-permute-start | bytes 208904 | tf_op jit(solution)/shard_map/ppermute | solution.py:503
  55.1 3.4 %collective-permute-done.20.rest_10_.rest_6_ = bf16[136,256]{1,0:T(8,128)(2,1)S(1)} collective-permute-done((bf16[136,256]{1,0:T(8,128)(2,1)S(1)}, bf16[136,256]{1,0:T(8,128)(2,1)S(1)}, u32[]{:S(2)}, u32[]{:S(2)}) %collective-permute-start.20) | collective-permute-done | bytes 69664 | tf_op jit(solution)/shard_map/ppermute | solution.py:503
  58.5 2.1 %collective-permute-start.10 = (bf16[128,256]{1,0:T(8,128)(2,1)S(1)}, bf16[128,256]{1,0:T(8,128)(2,1)S(1)}, u32[]{:S(2)}, u32[]{:S(2)}) collective-permute-start(bf16[128,256]{1,0:T(8,128)(2,1)S(1)} %get-tuple-element.46), channel_id=1, source_target_pairs={{0,7},{1,6},{2,5},{3,4},{4,3},{5,2},{6,1},{7,0},{8,15},{9,14},{10,... | collective-permute-start | bytes 196616 | tf_op jit(solution)/shard_map/ppermute | solution.py:503
  61.5 1.6 %collective-permute-start.7 = (bf16[128,256]{1,0:T(8,128)(2,1)S(1)}, bf16[128,256]{1,0:T(8,128)(2,1)S(1)}, u32[]{:S(2)}, u32[]{:S(2)}) collective-permute-start(bf16[128,256]{1,0:T(8,128)(2,1)S(1)} %get-tuple-element.43), channel_id=1, source_target_pairs={{0,4},{1,5},{2,6},{3,7},{4,0},{5,1},{6,2},{7,3},{8,12},{9,13},{10,... | collective-permute-start | bytes 196616 | tf_op jit(solution)/shard_map/ppermute | solution.py:503
  63.7 2.5 %collective-permute-start.9 = (bf16[128,256]{1,0:T(8,128)(2,1)S(1)}, bf16[128,256]{1,0:T(8,128)(2,1)S(1)}, u32[]{:S(2)}, u32[]{:S(2)}) collective-permute-start(bf16[128,256]{1,0:T(8,128)(2,1)S(1)} %get-tuple-element.45), channel_id=1, source_target_pairs={{0,6},{1,7},{2,4},{3,5},{4,2},{5,3},{6,0},{7,1},{8,14},{9,15},{10,... | collective-permute-start | bytes 196616 | tf_op jit(solution)/shard_map/ppermute | solution.py:503
  66.3 1.6 %collective-permute-start.23 = (f32[8,128]{1,0:T(8,128)S(1)}, f32[8,128]{1,0:T(8,128)S(1)}, u32[]{:S(2)}, u32[]{:S(2)}) collective-permute-start(f32[8,128]{1,0:T(8,128)S(1)} %shard_map.109.mine), channel_id=1, source_target_pairs={{0,16},{8,24},{16,0},{24,8},{1,17},{9,25},{17,1},{25,9},{2,18},{10... | collective-permute-start | bytes 12296 | tf_op jit(solution)/shard_map/ppermute | solution.py:531
  68.2 1.6 %collective-permute-done.8.rest_1_ = bf16[128,256]{1,0:T(8,128)(2,1)S(1)} collective-permute-done((bf16[128,256]{1,0:T(8,128)(2,1)S(1)}, bf16[128,256]{1,0:T(8,128)(2,1)S(1)}, u32[]{:S(2)}, u32[]{:S(2)}) %collective-permute-start.8) | collective-permute-done | bytes 65568 | tf_op jit(solution)/shard_map/ppermute | solution.py:503
  69.8 1.4 %shard_map.108 = bf16[4,256,512]{2,1,0:T(8,128)(2,1)} custom-call(bf16[128,256]{1,0:T(8,128)(2,1)S(1)} %collective-permute-done.7.rest_0_, bf16[128,256]{1,0:T(8,128)(2,1)S(1)} %collective-permute-done.8.rest_1_, bf16[128,256]{1,0:T(8,128)(2,1)S(1)} %collective-permute-done.9.rest_2_, bf16[128,256]{1,0:T(8,128)(2,1)S(1)} %collective-permute-done.10.rest_3_, ...), custom_call_target="tpu_custom_call" | custom-call | bytes 4000000 | tf_op jit(solution)/shard_map/pallas_call | solution.py:441
  (44 shorter events, 7.4 us)
Async XLA Ops:
  7.6 11.3 %collective-permute-start.3 = (bf16[4,32,256]{2,1,0:T(8,128)(2,1)S(1)}, bf16[4,32,256]{2,1,0:T(8,128)(2,1)S(1)}, u32[]{:S(2)}, u32[]{:S(2)}) collective-permute-start(bf16[4,32,256]{2,1,0:T(8,128)(2,1)S(1)} %get-tuple-element.39), channel_id=1, source_target_pairs={{0,4},{1,5},{2,6},{3,7},{4,0},{5,1},{6,2},{7,3},{8,12},{9,13},{10,... | collective-permute-start | bytes 196616 | tf_op jit(solution)/shard_map/ppermute | solution.py:503
  11.7 10.7 %collective-permute-start.4 = (bf16[4,32,256]{2,1,0:T(8,128)(2,1)S(1)}, bf16[4,32,256]{2,1,0:T(8,128)(2,1)S(1)}, u32[]{:S(2)}, u32[]{:S(2)}) collective-permute-start(bf16[4,32,256]{2,1,0:T(8,128)(2,1)S(1)} %get-tuple-element.40), channel_id=1, source_target_pairs={{0,5},{1,4},{2,7},{3,6},{4,1},{5,0},{6,3},{7,2},{8,13},{9,12},{10,... | collective-permute-start | bytes 196616 | tf_op jit(solution)/shard_map/ppermute | solution.py:503
  15.3 16.4 %collective-permute-start = (bf16[4,64,256]{2,1,0:T(8,128)(2,1)S(1)}, bf16[4,64,256]{2,1,0:T(8,128)(2,1)S(1)}, u32[]{:S(2)}, u32[]{:S(2)}) collective-permute-start(bf16[4,64,256]{2,1,0:T(8,128)(2,1)S(1)} %get-tuple-element.36), channel_id=1, source_target_pairs={{0,1},{1,0},{2,3},{3,2},{4,5},{5,4},{6,7},{7,6},{8,9},{9,8},{10,11... | collective-permute-start | bytes 393224 | tf_op jit(solution)/shard_map/ppermute | solution.py:503
  15.6 16.9 %collective-permute-start.1 = (bf16[4,64,256]{2,1,0:T(8,128)(2,1)S(1)}, bf16[4,64,256]{2,1,0:T(8,128)(2,1)S(1)}, u32[]{:S(2)}, u32[]{:S(2)}) collective-permute-start(bf16[4,64,256]{2,1,0:T(8,128)(2,1)S(1)} %get-tuple-element.37), channel_id=1, source_target_pairs={{0,2},{1,3},{2,0},{3,1},{4,6},{5,7},{6,4},{7,5},{8,10},{9,11},{10,... | collective-permute-start | bytes 393224 | tf_op jit(solution)/shard_map/ppermute | solution.py:503
  17.5 18.4 %collective-permute-start.2 = (bf16[4,64,256]{2,1,0:T(8,128)(2,1)S(1)}, bf16[4,64,256]{2,1,0:T(8,128)(2,1)S(1)}, u32[]{:S(2)}, u32[]{:S(2)}) collective-permute-start(bf16[4,64,256]{2,1,0:T(8,128)(2,1)S(1)} %get-tuple-element.38), channel_id=1, source_target_pairs={{0,3},{1,2},{2,1},{3,0},{4,7},{5,6},{6,5},{7,4},{8,11},{9,10},{10,... | collective-permute-start | bytes 393224 | tf_op jit(solution)/shard_map/ppermute | solution.py:503
  18.9 9.4 %collective-permute-start.5 = (bf16[4,32,256]{2,1,0:T(8,128)(2,1)S(1)}, bf16[4,32,256]{2,1,0:T(8,128)(2,1)S(1)}, u32[]{:S(2)}, u32[]{:S(2)}) collective-permute-start(bf16[4,32,256]{2,1,0:T(8,128)(2,1)S(1)} %get-tuple-element.41), channel_id=1, source_target_pairs={{0,6},{1,7},{2,4},{3,5},{4,2},{5,3},{6,0},{7,1},{8,14},{9,15},{10,... | collective-permute-start | bytes 196616 | tf_op jit(solution)/shard_map/ppermute | solution.py:503
  22.5 7.2 %collective-permute-start.6 = (bf16[4,32,256]{2,1,0:T(8,128)(2,1)S(1)}, bf16[4,32,256]{2,1,0:T(8,128)(2,1)S(1)}, u32[]{:S(2)}, u32[]{:S(2)}) collective-permute-start(bf16[4,32,256]{2,1,0:T(8,128)(2,1)S(1)} %get-tuple-element.42), channel_id=1, source_target_pairs={{0,7},{1,6},{2,5},{3,4},{4,3},{5,2},{6,1},{7,0},{8,15},{9,14},{10,... | collective-permute-start | bytes 196616 | tf_op jit(solution)/shard_map/ppermute | solution.py:503
  28.3 10.9 %collective-permute-start.11 = (bf16[4,32,256]{2,1,0:T(8,128)(2,1)S(1)}, bf16[4,32,256]{2,1,0:T(8,128)(2,1)S(1)}, u32[]{:S(2)}, u32[]{:S(2)}) collective-permute-start(bf16[4,32,256]{2,1,0:T(8,128)(2,1)S(1)} %get-tuple-element.47), channel_id=1, source_target_pairs={{0,4},{1,5},{2,6},{3,7},{4,0},{5,1},{6,2},{7,3},{8,12},{9,13},{10,... | collective-permute-start | bytes 196616 | tf_op jit(solution)/shard_map/ppermute | solution.py:503
  29.7 9.5 %collective-permute-start.12 = (bf16[4,32,256]{2,1,0:T(8,128)(2,1)S(1)}, bf16[4,32,256]{2,1,0:T(8,128)(2,1)S(1)}, u32[]{:S(2)}, u32[]{:S(2)}) collective-permute-start(bf16[4,32,256]{2,1,0:T(8,128)(2,1)S(1)} %get-tuple-element.48), channel_id=1, source_target_pairs={{0,5},{1,4},{2,7},{3,6},{4,1},{5,0},{6,3},{7,2},{8,13},{9,12},{10,... | collective-permute-start | bytes 196616 | tf_op jit(solution)/shard_map/ppermute | solution.py:503
  31.7 7.5 %collective-permute-start.13 = (bf16[4,32,256]{2,1,0:T(8,128)(2,1)S(1)}, bf16[4,32,256]{2,1,0:T(8,128)(2,1)S(1)}, u32[]{:S(2)}, u32[]{:S(2)}) collective-permute-start(bf16[4,32,256]{2,1,0:T(8,128)(2,1)S(1)} %get-tuple-element.49), channel_id=1, source_target_pairs={{0,6},{1,7},{2,4},{3,5},{4,2},{5,3},{6,0},{7,1},{8,14},{9,15},{10,... | collective-permute-start | bytes 196616 | tf_op jit(solution)/shard_map/ppermute | solution.py:503
  32.6 7.1 %collective-permute-start.14 = (bf16[4,32,256]{2,1,0:T(8,128)(2,1)S(1)}, bf16[4,32,256]{2,1,0:T(8,128)(2,1)S(1)}, u32[]{:S(2)}, u32[]{:S(2)}) collective-permute-start(bf16[4,32,256]{2,1,0:T(8,128)(2,1)S(1)} %get-tuple-element.50), channel_id=1, source_target_pairs={{0,7},{1,6},{2,5},{3,4},{4,3},{5,2},{6,1},{7,0},{8,15},{9,14},{10,... | collective-permute-start | bytes 196616 | tf_op jit(solution)/shard_map/ppermute | solution.py:503
  43.1 6.5 %collective-permute-start.18 = (bf16[136,256]{1,0:T(8,128)(2,1)S(1)}, bf16[136,256]{1,0:T(8,128)(2,1)S(1)}, u32[]{:S(2)}, u32[]{:S(2)}) collective-permute-start(bf16[136,256]{1,0:T(8,128)(2,1)S(1)} %get-tuple-element.60), channel_id=1, source_target_pairs={{0,4},{1,5},{2,6},{3,7},{4,0},{5,1},{6,2},{7,3},{8,12},{9,13},{10,... | collective-permute-start | bytes 208904 | tf_op jit(solution)/shard_map/ppermute | solution.py:503
  45.9 7.7 %collective-permute-start.19 = (bf16[136,256]{1,0:T(8,128)(2,1)S(1)}, bf16[136,256]{1,0:T(8,128)(2,1)S(1)}, u32[]{:S(2)}, u32[]{:S(2)}) collective-permute-start(bf16[136,256]{1,0:T(8,128)(2,1)S(1)} %get-tuple-element.61), channel_id=1, source_target_pairs={{0,5},{1,4},{2,7},{3,6},{4,1},{5,0},{6,3},{7,2},{8,13},{9,12},{10,... | collective-permute-start | bytes 208904 | tf_op jit(solution)/shard_map/ppermute | solution.py:503
  46.1 17.0 %collective-permute-start.15 = (bf16[264,256]{1,0:T(8,128)(2,1)S(1)}, bf16[264,256]{1,0:T(8,128)(2,1)S(1)}, u32[]{:S(2)}, u32[]{:S(2)}) collective-permute-start(bf16[264,256]{1,0:T(8,128)(2,1)S(1)} %get-tuple-element.57), channel_id=1, source_target_pairs={{0,1},{1,0},{2,3},{3,2},{4,5},{5,4},{6,7},{7,6},{8,9},{9,8},{10,11... | collective-permute-start | bytes 405512 | tf_op jit(solution)/shard_map/ppermute | solution.py:503
  47.5 16.2 %collective-permute-start.16 = (bf16[264,256]{1,0:T(8,128)(2,1)S(1)}, bf16[264,256]{1,0:T(8,128)(2,1)S(1)}, u32[]{:S(2)}, u32[]{:S(2)}) collective-permute-start(bf16[264,256]{1,0:T(8,128)(2,1)S(1)} %get-tuple-element.58), channel_id=1, source_target_pairs={{0,2},{1,3},{2,0},{3,1},{4,6},{5,7},{6,4},{7,5},{8,10},{9,11},{10,... | collective-permute-start | bytes 405512 | tf_op jit(solution)/shard_map/ppermute | solution.py:503
  48.9 17.3 %collective-permute-start.17 = (bf16[264,256]{1,0:T(8,128)(2,1)S(1)}, bf16[264,256]{1,0:T(8,128)(2,1)S(1)}, u32[]{:S(2)}, u32[]{:S(2)}) collective-permute-start(bf16[264,256]{1,0:T(8,128)(2,1)S(1)} %get-tuple-element.59), channel_id=1, source_target_pairs={{0,3},{1,2},{2,1},{3,0},{4,7},{5,6},{6,5},{7,4},{8,11},{9,10},{10,... | collective-permute-start | bytes 405512 | tf_op jit(solution)/shard_map/ppermute | solution.py:503
  49.6 8.9 %collective-permute-start.20 = (bf16[136,256]{1,0:T(8,128)(2,1)S(1)}, bf16[136,256]{1,0:T(8,128)(2,1)S(1)}, u32[]{:S(2)}, u32[]{:S(2)}) collective-permute-start(bf16[136,256]{1,0:T(8,128)(2,1)S(1)} %get-tuple-element.62), channel_id=1, source_target_pairs={{0,6},{1,7},{2,4},{3,5},{4,2},{5,3},{6,0},{7,1},{8,14},{9,15},{10,... | collective-permute-start | bytes 208904 | tf_op jit(solution)/shard_map/ppermute | solution.py:503
  53.7 7.9 %collective-permute-start.21 = (bf16[136,256]{1,0:T(8,128)(2,1)S(1)}, bf16[136,256]{1,0:T(8,128)(2,1)S(1)}, u32[]{:S(2)}, u32[]{:S(2)}) collective-permute-start(bf16[136,256]{1,0:T(8,128)(2,1)S(1)} %get-tuple-element.63), channel_id=1, source_target_pairs={{0,7},{1,6},{2,5},{3,4},{4,3},{5,2},{6,1},{7,0},{8,15},{9,14},{10,... | collective-permute-start | bytes 208904 | tf_op jit(solution)/shard_map/ppermute | solution.py:503
  58.5 7.8 %collective-permute-start.10 = (bf16[128,256]{1,0:T(8,128)(2,1)S(1)}, bf16[128,256]{1,0:T(8,128)(2,1)S(1)}, u32[]{:S(2)}, u32[]{:S(2)}) collective-permute-start(bf16[128,256]{1,0:T(8,128)(2,1)S(1)} %get-tuple-element.46), channel_id=1, source_target_pairs={{0,7},{1,6},{2,5},{3,4},{4,3},{5,2},{6,1},{7,0},{8,15},{9,14},{10,... | collective-permute-start | bytes 196616 | tf_op jit(solution)/shard_map/ppermute | solution.py:503
  61.5 6.4 %collective-permute-start.7 = (bf16[128,256]{1,0:T(8,128)(2,1)S(1)}, bf16[128,256]{1,0:T(8,128)(2,1)S(1)}, u32[]{:S(2)}, u32[]{:S(2)}) collective-permute-start(bf16[128,256]{1,0:T(8,128)(2,1)S(1)} %get-tuple-element.43), channel_id=1, source_target_pairs={{0,4},{1,5},{2,6},{3,7},{4,0},{5,1},{6,2},{7,3},{8,12},{9,13},{10,... | collective-permute-start | bytes 196616 | tf_op jit(solution)/shard_map/ppermute | solution.py:503
  63.1 6.6 %collective-permute-start.8 = (bf16[128,256]{1,0:T(8,128)(2,1)S(1)}, bf16[128,256]{1,0:T(8,128)(2,1)S(1)}, u32[]{:S(2)}, u32[]{:S(2)}) collective-permute-start(bf16[128,256]{1,0:T(8,128)(2,1)S(1)} %get-tuple-element.44), channel_id=1, source_target_pairs={{0,5},{1,4},{2,7},{3,6},{4,1},{5,0},{6,3},{7,2},{8,13},{9,12},{10,... | collective-permute-start | bytes 196616 | tf_op jit(solution)/shard_map/ppermute | solution.py:503
  63.7 6.2 %collective-permute-start.9 = (bf16[128,256]{1,0:T(8,128)(2,1)S(1)}, bf16[128,256]{1,0:T(8,128)(2,1)S(1)}, u32[]{:S(2)}, u32[]{:S(2)}) collective-permute-start(bf16[128,256]{1,0:T(8,128)(2,1)S(1)} %get-tuple-element.45), channel_id=1, source_target_pairs={{0,6},{1,7},{2,4},{3,5},{4,2},{5,3},{6,0},{7,1},{8,14},{9,15},{10,... | collective-permute-start | bytes 196616 | tf_op jit(solution)/shard_map/ppermute | solution.py:503
  66.2 5.0 %collective-permute-start.22 = (f32[8,128]{1,0:T(8,128)S(1)}, f32[8,128]{1,0:T(8,128)S(1)}, u32[]{:S(2)}, u32[]{:S(2)}) collective-permute-start(f32[8,128]{1,0:T(8,128)S(1)} %shard_map.109.mine), channel_id=1, source_target_pairs={{0,8},{8,0},{16,24},{24,16},{1,9},{9,1},{17,25},{25,17},{2,10},{10... | collective-permute-start | bytes 12296 | tf_op jit(solution)/shard_map/ppermute | solution.py:531
  66.3 4.9 %collective-permute-start.23 = (f32[8,128]{1,0:T(8,128)S(1)}, f32[8,128]{1,0:T(8,128)S(1)}, u32[]{:S(2)}, u32[]{:S(2)}) collective-permute-start(f32[8,128]{1,0:T(8,128)S(1)} %shard_map.109.mine), channel_id=1, source_target_pairs={{0,16},{8,24},{16,0},{24,8},{1,17},{9,25},{17,1},{25,9},{2,18},{10... | collective-permute-start | bytes 12296 | tf_op jit(solution)/shard_map/ppermute | solution.py:531
  (6 other events, 118.1 us)
